TPU v7x, 256 devices: a whole 4x4x8 slice. The times are simulated.
256 devices in a mesh: gz: 8 (over y, core), xy: 32 (over z, x).
Axes of the slice: x: 4, y: 4, z: 8, core: 2. Of those that a mesh axis runs over, the one named last changes fastest.
Arguments:
- right_side: float32 [12, 16, 64, 512], P(None, 'gz', 'xy'), may hold values from -24 to 24
- jac_diag: bfloat16 [12, 12, 16, 64, 512], P(None, None, 'gz', 'xy'), may hold values from -1.25 to 7.05
- jac_off: bfloat16 [6, 12, 12, 16, 64, 512], P(None, None, None, 'gz', 'xy'), may hold values from -0.59765625 to 0.59765625
- block_inv: bfloat16 [12, 12, 16, 64, 512], P(None, None, 'gz', 'xy'), may hold values from -0.125 to 0.405
- press_weight: bfloat16 [12, 16, 64, 512], P(None, 'gz', 'xy'), may hold values from 0.099609375 to 1
- press_diag: bfloat16 [16, 64, 512], P('gz', 'xy'), may hold values from 6.5 to 9
- press_off: bfloat16 [6, 16, 64, 512], P(None, 'gz', 'xy'), may hold values from -1 to -0.19921875
- well_index: float32 [16, 64, 512], P('gz', 'xy'), may hold values from 0.5 to 5
- well_columns: int32 [64], replicated, may hold values from 0 to 32767
- agg_map: int32 [16, 64, 512], P('gz', 'xy'), may hold values from 0 to 7
- level1_op: bfloat16 [8, 8, 16, 64, 4], P(None, None, 'gz', 'xy'), may hold values from -1.65 to 5.05
- coarsest_inv: bfloat16 [16, 64, 16, 64], P('gz', 'xy'), may hold values from -0.13479223 to 0.31156893
Outputs:
- solution: float32 [12, 16, 64, 512], P(None, 'gz', 'xy')
- residual: float32 [12, 16, 64, 512], P(None, 'gz', 'xy')
- hessenberg: float32 [3, 2], replicated
Inputs may be any that keep to these rules, and one draw needn't show every extreme that they name: `well_columns`: flat areal index x * 512 + y of each vertical well, which is perforated in every layer; a column may hold several wells. `agg_map`: an aggregate may be empty.
All inputs are finite; a program needn't handle non-finite values.
Results may differ from a plain program's by a relative error of at most 0.0018.
Values may be sent and summed in bfloat16 or wider, within the bound.
No kernel may reach another device: no remote copies, remote signals or barrier semaphores. Data moves between devices by JAX's collectives and lax.ppermute only.
A program may use at most 64 MiB of HBM per device.

v0:
```python
import jax
import jax.numpy as jnp
from jax import lax
from jax.sharding import Mesh
from jax.sharding import PartitionSpec as P

ITERS = 2
GZ = ("gz_0", "gz_1")
XY = ("xy_0", "xy_1")


EPSILON = 1e-06


def with_halo(shard, sides, width):
    edges = {}
    for axis, dim in sides:
        size, length = (lax.axis_size(axis), shard.shape[dim])
        up = [(i, (i + 1) % size) for i in range(size - 1)]
        last = lax.slice_in_dim(shard, length - width, length, axis=dim)
        initial = lax.slice_in_dim(shard, 0, width, axis=dim)
        edges[dim] = (
            lax.ppermute(last, axis, up),
            lax.ppermute(initial, axis, [(b, a) for a, b in up]),
        )
    done = []
    for _, dim in sides:
        low, high = edges[dim]
        around = [(width, width) if d in done else (0, 0) for d in range(shard.ndim)]
        shard = jnp.concatenate([jnp.pad(low, around), shard, jnp.pad(high, around)], axis=dim)
        done.append(dim)
    return shard


def copy_for_each(shard, axis):
    size = lax.axis_size(axis)
    return lax.all_to_all(
        jnp.broadcast_to(shard[None], (size, *shard.shape)), axis, 0, 0, tiled=True
    )


def over_copies(shard, axis):
    return copy_for_each(shard, axis).sum(axis=0)


def over_axes(shard, axes):
    far, near = axes
    nearer = over_copies(shard, near)
    return over_copies(nearer, far)


def together(arrays, axis):
    ends = [0]
    for a in arrays:
        ends.append(ends[-1] + a.size)
    running = over_axes(jnp.concatenate([a.ravel() for a in arrays]), axis)
    return tuple((running[b:e].reshape(a.shape) for a, b, e in zip(arrays, ends, ends[1:])))


def joined_along(pieces, dim):
    shape = list(pieces.shape[1:])
    shape[dim] *= pieces.shape[0]
    return jnp.moveaxis(pieces, 0, dim).reshape(shape)


def gather_axes(shard, axes, dim):
    far, near = axes
    initial = copy_for_each(shard, far)
    pieces = jnp.swapaxes(copy_for_each(initial, near), 0, 1)
    return joined_along(pieces.reshape(-1, *shard.shape), dim)


def neighbours(padded):
    return jnp.stack(
        [
            padded[..., :-2, 1:-1, 1:-1],
            padded[..., 2:, 1:-1, 1:-1],
            padded[..., 1:-1, :-2, 1:-1],
            padded[..., 1:-1, 2:, 1:-1],
            padded[..., 1:-1, 1:-1, :-2],
            padded[..., 1:-1, 1:-1, 2:],
        ]
    )


def pad_along_y(field):
    widths = [(0, 0)] * (field.ndim - 1) + [(1, 1)]
    return jnp.pad(field, widths)


def fine_near(field):
    padded = with_halo(field, ((GZ, 1), (XY, 2)), 1)
    return neighbours(pad_along_y(padded))


def pressure_near(field):
    padded = with_halo(field, ((GZ, 0), (XY, 1)), 1)
    return neighbours(pad_along_y(padded))


def least_squares(hessen, beta):
    upper = [list(line) for line in hessen]
    target = [beta] + [jnp.zeros((), jnp.float32) for line in range(ITERS)]
    rotations = []
    for column in range(ITERS):
        for row, (cosine, sine) in enumerate(rotations):
            first, second = (upper[row][column], upper[row + 1][column])
            upper[row][column] = cosine * first + sine * second
            upper[row + 1][column] = cosine * second - sine * first
        first, second = (upper[column][column], upper[column + 1][column])
        radius = jnp.sqrt(first * first + second * second)
        cosine, sine = (first / radius, second / radius)
        upper[column][column] = radius
        leading = target[column]
        target[column] = cosine * leading
        target[column + 1] = -sine * leading
        rotations.append((cosine, sine))
    weights = [None] * ITERS
    for column in reversed(range(ITERS)):
        total = target[column]
        for later in range(column + 1, ITERS):
            total = total - upper[column][later] * weights[later]
        weights[column] = total / upper[column][column]
    return weights


def on_device(
    right_side,
    jac_diag,
    jac_off,
    block_inv,
    press_weight,
    press_diag,
    press_off,
    well_index,
    well_columns,
    agg_map,
    level1_op,
    coarsest_inv,
):
    depth, width, length = (right_side.shape[1], right_side.shape[2], right_side.shape[3])
    aggregates = level1_op.shape[0]
    blocks = level1_op.shape[4]
    block_len = length // blocks
    layer_devices = lax.axis_size(GZ)
    areal_devices = lax.axis_size(XY)
    columns = (
        lax.axis_index(XY) * width + jnp.arange(width, dtype=jnp.int32)[:, None]
    ) * length + jnp.arange(length, dtype=jnp.int32)[None, :]
    well_mask = (well_columns[:, None] == columns.reshape(1, -1)).astype(jnp.float32)
    wells_here = jnp.sum(well_mask, axis=0).reshape(width, length)
    local_weight = jnp.dot(
        well_mask, jnp.sum(well_index, axis=0).reshape(-1), precision=lax.Precision.HIGHEST
    )
    local_norm = jnp.sum(right_side * right_side)
    norm_squared, well_weight = together(
        (local_norm, local_weight), ("gz_0", ("gz_1", "xy_0", "xy_1"))
    )

    def well_term(pressure):
        local = jnp.dot(
            well_mask,
            jnp.sum(well_index * pressure, axis=0).reshape(-1),
            precision=lax.Precision.HIGHEST,
        )
        totals = over_axes(local, ("gz_0", ("gz_1", "xy_0", "xy_1")))
        spread = jnp.dot(totals / well_weight, well_mask, precision=lax.Precision.HIGHEST).reshape(
            width, length
        )
        return well_index * (wells_here * pressure - spread)

    def apply_column(pressure):
        near = pressure_near(pressure)
        result = jac_diag[:, 0].astype(jnp.float32) * pressure[None]
        result = result + jnp.sum(jac_off[:, :, 0].astype(jnp.float32) * near[:, None], axis=0)
        return result.at[0].add(well_term(pressure))

    diag_pressure = press_diag.astype(jnp.float32)

    def apply_pressure(field):
        near = pressure_near(field)
        return diag_pressure * field + jnp.sum(press_off.astype(jnp.float32) * near, axis=0)

    one_hot = (
        agg_map[None] == jnp.arange(aggregates, dtype=jnp.int32)[:, None, None, None]
    ).astype(jnp.float32)
    coarse_op = level1_op.astype(jnp.float32)
    coarse_diag = jnp.stack([coarse_op[index, index] for index in range(aggregates)])
    beta = jnp.sqrt(norm_squared + EPSILON)
    basis = [right_side / beta]
    directions = []
    images = []
    hessen = [[jnp.zeros((), jnp.float32) for column in range(ITERS)] for row in range(ITERS + 1)]
    for step in range(ITERS):
        precondition_vector = basis[step]
        pressure_rhs = jnp.sum(press_weight.astype(jnp.float32) * precondition_vector, axis=0)
        first_guess = pressure_rhs / diag_pressure
        fine_rest = pressure_rhs - apply_pressure(first_guess)
        coarse_rhs = jnp.sum(
            (one_hot * fine_rest[None]).reshape(aggregates, depth, width, blocks, block_len),
            axis=-1,
        )
        coarse_guess = coarse_rhs / coarse_diag
        coarse_rest = coarse_rhs - jnp.sum(coarse_op * coarse_guess[None], axis=1)
        coarsest_rhs = jnp.sum(coarse_rest, axis=(0, 3)).astype(jnp.bfloat16)
        gathered = gather_axes(coarsest_rhs.reshape(-1), (("gz_0", "gz_1", "xy_0"), "xy_1"), 0)
        ordered = (
            gathered.reshape(layer_devices, areal_devices, depth, width)
            .transpose(0, 2, 1, 3)
            .reshape(-1)
        )
        coarsest = jnp.dot(
            coarsest_inv.reshape(depth * width, -1), ordered, preferred_element_type=jnp.float32
        ).reshape(depth, width)
        coarse_value = coarse_guess + coarsest[None, :, :, None]
        smooth_guess = first_guess + jnp.sum(
            one_hot * jnp.repeat(coarse_value, block_len, axis=-1), axis=0
        )
        precondition_pressure = (
            smooth_guess + (pressure_rhs - apply_pressure(smooth_guess)) / diag_pressure
        )
        remainder = precondition_vector - apply_column(precondition_pressure)
        correction = jnp.sum(block_inv.astype(jnp.float32) * remainder[None], axis=1)
        direction = correction.at[0].add(precondition_pressure)
        apply_near = fine_near(direction)
        centre = jnp.sum(jac_diag.astype(jnp.float32) * direction[None], axis=1)
        coupled = jnp.sum(jac_off.astype(jnp.float32) * apply_near[:, None], axis=(0, 2))
        apply_result = centre + coupled
        image = apply_result.at[0].add(well_term(direction[0]))
        directions.append(direction)
        images.append(image)
        products = jnp.stack([jnp.sum(image * vector) for vector in basis])
        coeffs, image_norm = together(
            (products, jnp.sum(image * image)), ("gz_0", ("gz_1", "xy_0", "xy_1"))
        )
        rest = image
        squares = jnp.zeros((), jnp.float32)
        for row in range(step + 1):
            rest = rest - coeffs[row] * basis[row]
            squares = squares + coeffs[row] * coeffs[row]
        height = jnp.sqrt(image_norm - squares + EPSILON)
        for row in range(step + 1):
            hessen[row][step] = coeffs[row]
        hessen[step + 1][step] = height
        if step + 1 < ITERS:
            basis.append(rest / height)
    weights = least_squares(hessen, beta)
    solution = weights[0] * directions[0]
    step = 1
    solution = solution + weights[step] * directions[step]
    applied = weights[0] * images[0]
    step = 1
    applied = applied + weights[step] * images[step]
    residual = right_side - applied
    hessenberg = jnp.stack([jnp.stack(line) for line in hessen])
    return (solution, residual, hessenberg)


def solution(mesh):
    split = Mesh(mesh.devices.reshape(4, 2, 8, 4), ("gz_0", "gz_1", "xy_0", "xy_1"))
    return jax.shard_map(
        on_device,
        mesh=split,
        in_specs=(
            P(None, GZ, XY, None),
            P(None, None, GZ, XY, None),
            P(None, None, None, GZ, XY, None),
            P(None, None, GZ, XY, None),
            P(None, GZ, XY, None),
            P(GZ, XY, None),
            P(None, GZ, XY, None),
            P(GZ, XY, None),
            P(),
            P(GZ, XY, None),
            P(None, None, GZ, XY, None),
            P(GZ, XY, None, None),
        ),
        out_specs=(P(None, GZ, XY, None), P(None, GZ, XY, None), P()),
        check_vma=False,
    )
```

profile of v0, /device:TPU:1, one launch (start us, length us, event | category | flops | bytes accessed | tf_op | source)
XLA Modules:
  0.0 448.7 jit_solution(2635581023989541877)
XLA Ops:
  5.4 13.1 %all-to-all-start = ((f32[64,1,65]{2,1,0:T(1,128)}), f32[64,1,65]{2,1,0:T(1,128)S(1)}, u32[]{:S(2)}, u32[]{:S(2)}) async-start(f32[64,1,65]{2,1,0:T(1,128)} %broadcast_in_dim.44), calls=%async_computation | async-start | bytes 65536 | tf_op jit(solution)/shard_map/all_to_all | solution.py:37
  19.3 8.3 %all-to-all-done = f32[64,1,65]{2,1,0:T(1,128)S(1)} async-done(((f32[64,1,65]{2,1,0:T(1,128)}), f32[64,1,65]{2,1,0:T(1,128)S(1)}, u32[]{:S(2)}, u32[]{:S(2)}) %all-to-all-start) | async-done | bytes 16672 | tf_op jit(solution)/shard_map/all_to_all | solution.py:37
  28.2 4.2 all-to-all-start.1
  33.3 3.1 all-to-all-done.1
  38.3 4.0 collective-permute-start
  47.8 3.0 collective-permute-done.3
  51.8 17.8 %all_to_all.106 = bf16[64,1,4]{2,1,0:T(2,128)(2,1)S(1)} all-to-all(bf16[64,1,4]{2,1,0:T(2,128)(2,1)S(1)} %broadcast_in_dim.46), channel_id=1, replica_groups=mesh['gz_0'=4,'gz_1'=2,'xy_0'=8,'xy_1'=4] {'gz_0','gz_1','xy_0'}, dimensions={0} | all-to-all | bytes 1024 | tf_op jit(solution)/shard_map/all_to_all | solution.py:37
  70.4 4.5 all-to-all-start.3
  75.1 3.8 all-to-all-done.3
  80.1 4.5 collective-permute-start.4
  90.1 3.0 collective-permute-done.7
  93.5 5.1 %collective-permute-start.8 = (f32[1,2,512]{2,1,0:T(2,128)S(1)}, f32[1,2,512]{2,1,0:T(2,128)S(1)}, u32[]{:S(2)}, u32[]{:S(2)}) collective-permute-start(f32[1,2,512]{2,1,0:T(2,128)S(1)} %get-tuple-element.137), channel_id=1, source_target_pairs={{0,32},{32,64},{64,96},{96,128},{128,160},{160,192},{192,224},{1,3... | collective-permute-start | bytes 12296 | tf_op jit(solution)/shard_map/ppermute | solution.py:23
  104.9 10.9 %all-to-all-start.4 = ((f32[64,1,64]{2,1,0:T(1,128)}), f32[64,1,64]{2,1,0:T(1,128)S(1)}, u32[]{:S(2)}, u32[]{:S(2)}) async-start(f32[64,1,64]{2,1,0:T(1,128)} %broadcast_in_dim.50), calls=%async_computation.4 | async-start | bytes 65536 | tf_op jit(solution)/shard_map/all_to_all | solution.py:37
  117.6 7.3 %all-to-all-done.4 = f32[64,1,64]{2,1,0:T(1,128)S(1)} async-done(((f32[64,1,64]{2,1,0:T(1,128)}), f32[64,1,64]{2,1,0:T(1,128)S(1)}, u32[]{:S(2)}, u32[]{:S(2)}) %all-to-all-start.4) | async-done | bytes 16416 | tf_op jit(solution)/shard_map/all_to_all | solution.py:37
  125.5 3.7 all-to-all-start.5
  130.1 3.2 all-to-all-done.5
  136.1 6.2 %all-to-all-start.6 = ((f32[64,1,64]{2,1,0:T(1,128)}), f32[64,1,64]{2,1,0:T(1,128)S(1)}, u32[]{:S(2)}, u32[]{:S(2)}) async-start(f32[64,1,64]{2,1,0:T(1,128)} %broadcast_in_dim.52), calls=%async_computation.6 | async-start | bytes 65536 | tf_op jit(solution)/shard_map/all_to_all | solution.py:37
  142.9 8.4 %all-to-all-done.6 = f32[64,1,64]{2,1,0:T(1,128)S(1)} async-done(((f32[64,1,64]{2,1,0:T(1,128)}), f32[64,1,64]{2,1,0:T(1,128)S(1)}, u32[]{:S(2)}, u32[]{:S(2)}) %all-to-all-start.6) | async-done | bytes 16416 | tf_op jit(solution)/shard_map/all_to_all | solution.py:37
  151.9 3.8 all-to-all-start.7
  155.7 2.5 fusion.2
  158.3 4.0 collective-permute-start.12
  164.2 2.8 collective-permute-start.14
  180.2 3.7 fusion
  187.0 16.5 %all_to_all.107 = f32[64,1,2]{2,1,0:T(1,128)} all-to-all(f32[64,1,2]{2,1,0:T(1,128)S(1)} %broadcast_in_dim.54), channel_id=1, replica_groups=mesh['gz_0'=4,'gz_1'=2,'xy_0'=8,'xy_1'=4] {'gz_1','xy_0','xy_1'}, dimensions={0} | all-to-all | bytes 1024 | tf_op jit(solution)/shard_map/all_to_all | solution.py:37
  204.4 9.0 %all_to_all.108 = f32[4,1,2]{2,1,0:T(1,128)S(1)} all-to-all(f32[4,1,2]{2,1,0:T(1,128)S(1)} %broadcast_in_dim.55), channel_id=1, replica_groups=mesh['gz_0'=4,'gz_1'=2,'xy_0'=8,'xy_1'=4] {'gz_0'}, dimensions={0} | all-to-all | bytes 64 | tf_op jit(solution)/shard_map/all_to_all | solution.py:37
  216.0 2.4 fusion.42
  219.1 3.8 collective-permute-start.16
  228.6 3.0 collective-permute-done.19
  244.2 18.0 %all_to_all.109 = bf16[64,1,4]{2,1,0:T(2,128)(2,1)} all-to-all(bf16[64,1,4]{2,1,0:T(2,128)(2,1)S(1)} %broadcast_in_dim.56), channel_id=1, replica_groups=mesh['gz_0'=4,'gz_1'=2,'xy_0'=8,'xy_1'=4] {'gz_0','gz_1','xy_0'}, dimensions={0} | all-to-all | bytes 1024 | tf_op jit(solution)/shard_map/all_to_all | solution.py:37
  266.2 8.4 %all_to_all.110 = bf16[4,2,128]{2,1,0:T(2,128)(2,1)} all-to-all(bf16[4,2,128]{2,1,0:T(2,128)(2,1)} %reshape.603), channel_id=1, replica_groups=mesh['gz_0'=4,'gz_1'=2,'xy_0'=8,'xy_1'=4] {'xy_1'}, dimensions={0} | all-to-all | bytes 4096 | tf_op jit(solution)/shard_map/all_to_all | solution.py:37
  288.5 4.8 %collective-permute-start.20 = (f32[1,2,512]{2,1,0:T(2,128)S(1)}, f32[1,2,512]{2,1,0:T(2,128)S(1)}, u32[]{:S(2)}, u32[]{:S(2)}) collective-permute-start(f32[1,2,512]{2,1,0:T(2,128)S(1)} %get-tuple-element.129), channel_id=1, source_target_pairs={{0,32},{32,64},{64,96},{96,128},{128,160},{160,192},{192,224},{1,3... | collective-permute-start | bytes 12296 | tf_op jit(solution)/shard_map/ppermute | solution.py:23
  298.5 3.0 collective-permute-done.23
  304.5 5.1 %collective-permute-start.24 = (f32[1,2,512]{2,1,0:T(2,128)}, f32[1,2,512]{2,1,0:T(2,128)}, u32[]{:S(2)}, u32[]{:S(2)}) collective-permute-start(f32[1,2,512]{2,1,0:T(2,128)} %get-tuple-element.125), channel_id=1, source_target_pairs={{0,32},{32,64},{64,96},{96,128},{128,160},{160,192},{192,224},{1,3... | collective-permute-start | bytes 12296 | tf_op jit(solution)/shard_map/ppermute | solution.py:23
  311.5 2.8 collective-permute-start.26
  317.2 11.0 %all-to-all-start.12 = ((f32[64,1,64]{2,1,0:T(1,128)}), f32[64,1,64]{2,1,0:T(1,128)}, u32[]{:S(2)}, u32[]{:S(2)}) async-start(f32[64,1,64]{2,1,0:T(1,128)} %broadcast_in_dim.60), calls=%async_computation.12 | async-start | bytes 65536 | tf_op jit(solution)/shard_map/all_to_all | solution.py:37
  332.9 4.4 all-to-all-done.12
  339.8 3.8 all-to-all-start.13
  345.2 2.6 all-to-all-done.13
  358.2 7.0 %all-to-all-start.14 = ((f32[64,1,64]{2,1,0:T(1,128)}), f32[64,1,64]{2,1,0:T(1,128)}, u32[]{:S(2)}, u32[]{:S(2)}) async-start(f32[64,1,64]{2,1,0:T(1,128)} %broadcast_in_dim.62), calls=%async_computation.14 | async-start | bytes 65536 | tf_op jit(solution)/shard_map/all_to_all | solution.py:37
  366.7 7.5 %all-to-all-done.14 = f32[64,1,64]{2,1,0:T(1,128)} async-done(((f32[64,1,64]{2,1,0:T(1,128)}), f32[64,1,64]{2,1,0:T(1,128)}, u32[]{:S(2)}, u32[]{:S(2)}) %all-to-all-start.14) | async-done | bytes 16416 | tf_op jit(solution)/shard_map/all_to_all | solution.py:37
  376.8 3.8 all-to-all-start.15
  380.6 2.4 fusion.3
  383.0 4.1 collective-permute-start.28
  389.0 2.6 collective-permute-start.30
  403.8 3.7 fusion.1
  411.6 7.7 %all-to-all-start.16 = ((f32[64,1,3]{2,1,0:T(1,128)}), f32[64,1,3]{2,1,0:T(1,128)S(1)}, u32[]{:S(2)}, u32[]{:S(2)}) async-start(f32[64,1,3]{2,1,0:T(1,128)} %broadcast_in_dim.64), calls=%async_computation.16 | async-start | bytes 65536 | tf_op jit(solution)/shard_map/all_to_all | solution.py:37
  420.1 8.3 %all-to-all-done.16 = f32[64,1,3]{2,1,0:T(1,128)S(1)} async-done(((f32[64,1,3]{2,1,0:T(1,128)}), f32[64,1,3]{2,1,0:T(1,128)S(1)}, u32[]{:S(2)}, u32[]{:S(2)}) %all-to-all-start.16) | async-done | bytes 800 | tf_op jit(solution)/shard_map/all_to_all | solution.py:37
  428.6 9.0 %all_to_all.111 = f32[4,1,3]{2,1,0:T(1,128)S(1)} all-to-all(f32[4,1,3]{2,1,0:T(1,128)S(1)} %broadcast_in_dim.65), channel_id=1, replica_groups=mesh['gz_0'=4,'gz_1'=2,'xy_0'=8,'xy_1'=4] {'gz_0'}, dimensions={0} | all-to-all | bytes 96 | tf_op jit(solution)/shard_map/all_to_all | solution.py:37
  (354 shorter events, 152.2 us)
Async XLA Ops:
  1.5 133.6 %copy-start.29 = (s32[1,4,2,128]{3,1,2,0:T(4,128)}, s32[1,4,2,128]{3,1,2,0:T(4,128)S(1)}, u32[]{:S(2)}) copy-start(s32[1,4,2,128]{3,1,2,0:T(4,128)S(1)} %copy.127) | copy-start | bytes 12292
  5.4 22.1 %all-to-all-start = ((f32[64,1,65]{2,1,0:T(1,128)}), f32[64,1,65]{2,1,0:T(1,128)S(1)}, u32[]{:S(2)}, u32[]{:S(2)}) async-start(f32[64,1,65]{2,1,0:T(1,128)} %broadcast_in_dim.44), calls=%async_computation | async-start | bytes 65536 | tf_op jit(solution)/shard_map/all_to_all | solution.py:37
  28.2 8.2 %all-to-all-start.1 = ((f32[4,1,65]{2,1,0:T(1,128)}), f32[4,1,65]{2,1,0:T(1,128)S(1)}, u32[]{:S(2)}, u32[]{:S(2)}) async-start(f32[4,1,65]{2,1,0:T(1,128)} %broadcast_in_dim.45), calls=%async_computation.1 | async-start | bytes 4096 | tf_op jit(solution)/shard_map/all_to_all | solution.py:37
  33.2 82.7 %copy-start.17 = (s32[2,2,4,128]{3,2,1,0:T(4,128)}, s32[2,2,4,128]{3,2,1,0:T(4,128)S(1)}, u32[]{:S(2)}) copy-start(s32[2,2,4,128]{3,2,1,0:T(4,128)S(1)} %eq.35) | copy-start | bytes 24580
  36.4 96.9 %copy-start.34 = (f32[65]{0:T(128)}, f32[65]{0:T(128)S(1)}, u32[]{:S(2)}) copy-start(f32[65]{0:T(128)S(1)} %reduce_sum.439) | copy-start | bytes 784
  37.5 96.1 %copy-start.4 = (f32[12,2,2,512]{3,2,1,0:T(2,128)}, f32[12,2,2,512]{3,2,1,0:T(2,128)S(1)}, u32[]{:S(2)}) copy-start(f32[12,2,2,512]{3,2,1,0:T(2,128)S(1)} %get-tuple-element.105) | copy-start | bytes 294916
  38.3 9.5 %collective-permute-start = (f32[1,2,512]{2,1,0:T(2,128)S(1)}, f32[1,2,512]{2,1,0:T(2,128)S(1)}, u32[]{:S(2)}, u32[]{:S(2)}) collective-permute-start(f32[1,2,512]{2,1,0:T(2,128)S(1)} %get-tuple-element.145), channel_id=1, source_target_pairs={{0,32},{32,64},{64,96},{96,128},{128,160},{160,192},{192,224},{1,3... | collective-permute-start | bytes 12296 | tf_op jit(solution)/shard_map/ppermute | solution.py:23
  42.3 8.5 %collective-permute-start.1 = (f32[1,2,512]{2,1,0:T(2,128)S(1)}, f32[1,2,512]{2,1,0:T(2,128)S(1)}, u32[]{:S(2)}, u32[]{:S(2)}) collective-permute-start(f32[1,2,512]{2,1,0:T(2,128)S(1)} %get-tuple-element.144), channel_id=1, source_target_pairs={{32,0},{64,32},{96,64},{128,96},{160,128},{192,160},{224,192},{33,... | collective-permute-start | bytes 12296 | tf_op jit(solution)/shard_map/ppermute | solution.py:24
  44.3 3.5 collective-permute-start.2
  46.5 4.4 collective-permute-start.3
  70.4 8.5 %all-to-all-start.3 = ((bf16[4,2,128]{2,1,0:T(2,128)(2,1)}), bf16[4,2,128]{2,1,0:T(2,128)(2,1)S(1)}, u32[]{:S(2)}, u32[]{:S(2)}) async-start(bf16[4,2,128]{2,1,0:T(2,128)(2,1)} %reshape.601), calls=%async_computation.3 | async-start | bytes 4096 | tf_op jit(solution)/shard_map/all_to_all | solution.py:37
  80.1 9.9 %collective-permute-start.4 = (f32[1,2,512]{2,1,0:T(2,128)S(1)}, f32[1,2,512]{2,1,0:T(2,128)S(1)}, u32[]{:S(2)}, u32[]{:S(2)}) collective-permute-start(f32[1,2,512]{2,1,0:T(2,128)S(1)} %get-tuple-element.141), channel_id=1, source_target_pairs={{0,32},{32,64},{64,96},{96,128},{128,160},{160,192},{192,224},{1,3... | collective-permute-start | bytes 12296 | tf_op jit(solution)/shard_map/ppermute | solution.py:23
  84.6 8.5 %collective-permute-start.5 = (f32[1,2,512]{2,1,0:T(2,128)S(1)}, f32[1,2,512]{2,1,0:T(2,128)S(1)}, u32[]{:S(2)}, u32[]{:S(2)}) collective-permute-start(f32[1,2,512]{2,1,0:T(2,128)S(1)} %get-tuple-element.140), channel_id=1, source_target_pairs={{32,0},{64,32},{96,64},{128,96},{160,128},{192,160},{224,192},{33,... | collective-permute-start | bytes 12296 | tf_op jit(solution)/shard_map/ppermute | solution.py:24
  86.5 3.5 collective-permute-start.6
  88.7 4.4 collective-permute-start.7
  93.5 22.4 %collective-permute-start.8 = (f32[1,2,512]{2,1,0:T(2,128)S(1)}, f32[1,2,512]{2,1,0:T(2,128)S(1)}, u32[]{:S(2)}, u32[]{:S(2)}) collective-permute-start(f32[1,2,512]{2,1,0:T(2,128)S(1)} %get-tuple-element.137), channel_id=1, source_target_pairs={{0,32},{32,64},{64,96},{96,128},{128,160},{160,192},{192,224},{1,3... | collective-permute-start | bytes 12296 | tf_op jit(solution)/shard_map/ppermute | solution.py:23
  98.6 17.4 %collective-permute-start.9 = (f32[1,2,512]{2,1,0:T(2,128)S(1)}, f32[1,2,512]{2,1,0:T(2,128)S(1)}, u32[]{:S(2)}, u32[]{:S(2)}) collective-permute-start(f32[1,2,512]{2,1,0:T(2,128)S(1)} %get-tuple-element.136), channel_id=1, source_target_pairs={{32,0},{64,32},{96,64},{128,96},{160,128},{192,160},{224,192},{33,... | collective-permute-start | bytes 12296 | tf_op jit(solution)/shard_map/ppermute | solution.py:24
  100.5 15.4 %collective-permute-start.10 = (f32[2,1,512]{2,1,0:T(1,128)S(1)}, f32[2,1,512]{2,1,0:T(1,128)S(1)}, u32[]{:S(2)}, u32[]{:S(2)}) collective-permute-start(f32[2,1,512]{2,1,0:T(1,128)S(1)} %get-tuple-element.135), channel_id=1, source_target_pairs={{0,1},{1,2},{2,3},{3,4},{4,5},{5,6},{6,7},{7,8},{8,9},{9,10},{10,1... | collective-permute-start | bytes 12296 | tf_op jit(solution)/shard_map/ppermute | solution.py:23
  102.7 13.2 %collective-permute-start.11 = (f32[2,1,512]{2,1,0:T(1,128)S(1)}, f32[2,1,512]{2,1,0:T(1,128)S(1)}, u32[]{:S(2)}, u32[]{:S(2)}) collective-permute-start(f32[2,1,512]{2,1,0:T(1,128)S(1)} %get-tuple-element.134), channel_id=1, source_target_pairs={{1,0},{2,1},{3,2},{4,3},{5,4},{6,5},{7,6},{8,7},{9,8},{10,9},{11,1... | collective-permute-start | bytes 12296 | tf_op jit(solution)/shard_map/ppermute | solution.py:24
  104.9 20.0 %all-to-all-start.4 = ((f32[64,1,64]{2,1,0:T(1,128)}), f32[64,1,64]{2,1,0:T(1,128)S(1)}, u32[]{:S(2)}, u32[]{:S(2)}) async-start(f32[64,1,64]{2,1,0:T(1,128)} %broadcast_in_dim.50), calls=%async_computation.4 | async-start | bytes 65536 | tf_op jit(solution)/shard_map/all_to_all | solution.py:37
  125.5 7.8 %all-to-all-start.5 = ((f32[4,1,64]{2,1,0:T(1,128)}), f32[4,1,64]{2,1,0:T(1,128)S(1)}, u32[]{:S(2)}, u32[]{:S(2)}) async-start(f32[4,1,64]{2,1,0:T(1,128)} %broadcast_in_dim.51), calls=%async_computation.5 | async-start | bytes 4096 | tf_op jit(solution)/shard_map/all_to_all | solution.py:37
  136.1 15.3 %all-to-all-start.6 = ((f32[64,1,64]{2,1,0:T(1,128)}), f32[64,1,64]{2,1,0:T(1,128)S(1)}, u32[]{:S(2)}, u32[]{:S(2)}) async-start(f32[64,1,64]{2,1,0:T(1,128)} %broadcast_in_dim.52), calls=%async_computation.6 | async-start | bytes 65536 | tf_op jit(solution)/shard_map/all_to_all | solution.py:37
  151.9 16.6 %all-to-all-start.7 = ((f32[4,1,64]{2,1,0:T(1,128)}), f32[4,1,64]{2,1,0:T(1,128)}, u32[]{:S(2)}, u32[]{:S(2)}) async-start(f32[4,1,64]{2,1,0:T(1,128)} %broadcast_in_dim.53), calls=%async_computation.7 | async-start | bytes 4096 | tf_op jit(solution)/shard_map/all_to_all | solution.py:37
  158.3 14.2 %collective-permute-start.12 = (f32[12,1,2,512]{3,2,1,0:T(2,128)}, f32[12,1,2,512]{3,2,1,0:T(2,128)}, u32[]{:S(2)}, u32[]{:S(2)}) collective-permute-start(f32[12,1,2,512]{3,2,1,0:T(2,128)} %get-tuple-element.113), channel_id=1, source_target_pairs={{0,32},{32,64},{64,96},{96,128},{128,160},{160,192},{192,224},{1,3... | collective-permute-start | bytes 147464 | tf_op jit(solution)/shard_map/ppermute | solution.py:23
  162.3 12.8 %collective-permute-start.13 = (f32[12,1,2,512]{3,2,1,0:T(2,128)}, f32[12,1,2,512]{3,2,1,0:T(2,128)}, u32[]{:S(2)}, u32[]{:S(2)}) collective-permute-start(f32[12,1,2,512]{3,2,1,0:T(2,128)} %get-tuple-element.112), channel_id=1, source_target_pairs={{32,0},{64,32},{96,64},{128,96},{160,128},{192,160},{224,192},{33,... | collective-permute-start | bytes 147464 | tf_op jit(solution)/shard_map/ppermute | solution.py:24
  164.2 9.2 %collective-permute-start.14 = (f32[12,2,1,512]{3,2,1,0:T(1,128)}, f32[12,2,1,512]{3,2,1,0:T(1,128)}, u32[]{:S(2)}, u32[]{:S(2)}) collective-permute-start(f32[12,2,1,512]{3,2,1,0:T(1,128)} %get-tuple-element.111), channel_id=1, source_target_pairs={{0,1},{1,2},{2,3},{3,4},{4,5},{5,6},{6,7},{7,8},{8,9},{9,10},{10,1... | collective-permute-start | bytes 147464 | tf_op jit(solution)/shard_map/ppermute | solution.py:23
  167.0 7.2 %collective-permute-start.15 = (f32[12,2,1,512]{3,2,1,0:T(1,128)}, f32[12,2,1,512]{3,2,1,0:T(1,128)}, u32[]{:S(2)}, u32[]{:S(2)}) collective-permute-start(f32[12,2,1,512]{3,2,1,0:T(1,128)} %get-tuple-element.110), channel_id=1, source_target_pairs={{1,0},{2,1},{3,2},{4,3},{5,4},{6,5},{7,6},{8,7},{9,8},{10,9},{11,1... | collective-permute-start | bytes 147464 | tf_op jit(solution)/shard_map/ppermute | solution.py:24
  219.1 9.4 %collective-permute-start.16 = (f32[1,2,512]{2,1,0:T(2,128)S(1)}, f32[1,2,512]{2,1,0:T(2,128)S(1)}, u32[]{:S(2)}, u32[]{:S(2)}) collective-permute-start(f32[1,2,512]{2,1,0:T(2,128)S(1)} %get-tuple-element.133), channel_id=1, source_target_pairs={{0,32},{32,64},{64,96},{96,128},{128,160},{160,192},{192,224},{1,3... | collective-permute-start | bytes 12296 | tf_op jit(solution)/shard_map/ppermute | solution.py:23
  223.0 8.6 %collective-permute-start.17 = (f32[1,2,512]{2,1,0:T(2,128)S(1)}, f32[1,2,512]{2,1,0:T(2,128)S(1)}, u32[]{:S(2)}, u32[]{:S(2)}) collective-permute-start(f32[1,2,512]{2,1,0:T(2,128)S(1)} %get-tuple-element.132), channel_id=1, source_target_pairs={{32,0},{64,32},{96,64},{128,96},{160,128},{192,160},{224,192},{33,... | collective-permute-start | bytes 12296 | tf_op jit(solution)/shard_map/ppermute | solution.py:24
  224.9 3.7 collective-permute-start.18
  227.2 4.4 collective-permute-start.19
  288.5 10.0 %collective-permute-start.20 = (f32[1,2,512]{2,1,0:T(2,128)S(1)}, f32[1,2,512]{2,1,0:T(2,128)S(1)}, u32[]{:S(2)}, u32[]{:S(2)}) collective-permute-start(f32[1,2,512]{2,1,0:T(2,128)S(1)} %get-tuple-element.129), channel_id=1, source_target_pairs={{0,32},{32,64},{64,96},{96,128},{128,160},{160,192},{192,224},{1,3... | collective-permute-start | bytes 12296 | tf_op jit(solution)/shard_map/ppermute | solution.py:23
  293.3 8.2 %collective-permute-start.21 = (f32[1,2,512]{2,1,0:T(2,128)S(1)}, f32[1,2,512]{2,1,0:T(2,128)S(1)}, u32[]{:S(2)}, u32[]{:S(2)}) collective-permute-start(f32[1,2,512]{2,1,0:T(2,128)S(1)} %get-tuple-element.128), channel_id=1, source_target_pairs={{32,0},{64,32},{96,64},{128,96},{160,128},{192,160},{224,192},{33,... | collective-permute-start | bytes 12296 | tf_op jit(solution)/shard_map/ppermute | solution.py:24
  295.2 3.2 collective-permute-start.22
  297.1 4.4 collective-permute-start.23
  304.5 23.6 %collective-permute-start.24 = (f32[1,2,512]{2,1,0:T(2,128)}, f32[1,2,512]{2,1,0:T(2,128)}, u32[]{:S(2)}, u32[]{:S(2)}) collective-permute-start(f32[1,2,512]{2,1,0:T(2,128)} %get-tuple-element.125), channel_id=1, source_target_pairs={{0,32},{32,64},{64,96},{96,128},{128,160},{160,192},{192,224},{1,3... | collective-permute-start | bytes 12296 | tf_op jit(solution)/shard_map/ppermute | solution.py:23
  309.6 20.6 %collective-permute-start.25 = (f32[1,2,512]{2,1,0:T(2,128)}, f32[1,2,512]{2,1,0:T(2,128)}, u32[]{:S(2)}, u32[]{:S(2)}) collective-permute-start(f32[1,2,512]{2,1,0:T(2,128)} %get-tuple-element.124), channel_id=1, source_target_pairs={{32,0},{64,32},{96,64},{128,96},{160,128},{192,160},{224,192},{33,... | collective-permute-start | bytes 12296 | tf_op jit(solution)/shard_map/ppermute | solution.py:24
  311.5 17.3 %collective-permute-start.26 = (f32[2,1,512]{2,1,0:T(1,128)}, f32[2,1,512]{2,1,0:T(1,128)}, u32[]{:S(2)}, u32[]{:S(2)}) collective-permute-start(f32[2,1,512]{2,1,0:T(1,128)} %get-tuple-element.123), channel_id=1, source_target_pairs={{0,1},{1,2},{2,3},{3,4},{4,5},{5,6},{6,7},{7,8},{8,9},{9,10},{10,1... | collective-permute-start | bytes 12296 | tf_op jit(solution)/shard_map/ppermute | solution.py:23
  314.3 15.2 %collective-permute-start.27 = (f32[2,1,512]{2,1,0:T(1,128)}, f32[2,1,512]{2,1,0:T(1,128)}, u32[]{:S(2)}, u32[]{:S(2)}) collective-permute-start(f32[2,1,512]{2,1,0:T(1,128)} %get-tuple-element.122), channel_id=1, source_target_pairs={{1,0},{2,1},{3,2},{4,3},{5,4},{6,5},{7,6},{8,7},{9,8},{10,9},{11,1... | collective-permute-start | bytes 12296 | tf_op jit(solution)/shard_map/ppermute | solution.py:24
  317.2 20.1 %all-to-all-start.12 = ((f32[64,1,64]{2,1,0:T(1,128)}), f32[64,1,64]{2,1,0:T(1,128)}, u32[]{:S(2)}, u32[]{:S(2)}) async-start(f32[64,1,64]{2,1,0:T(1,128)} %broadcast_in_dim.60), calls=%async_computation.12 | async-start | bytes 65536 | tf_op jit(solution)/shard_map/all_to_all | solution.py:37
  339.8 8.0 %all-to-all-start.13 = ((f32[4,1,64]{2,1,0:T(1,128)}), f32[4,1,64]{2,1,0:T(1,128)}, u32[]{:S(2)}, u32[]{:S(2)}) async-start(f32[4,1,64]{2,1,0:T(1,128)} %broadcast_in_dim.61), calls=%async_computation.13 | async-start | bytes 4096 | tf_op jit(solution)/shard_map/all_to_all | solution.py:37
  358.2 16.0 %all-to-all-start.14 = ((f32[64,1,64]{2,1,0:T(1,128)}), f32[64,1,64]{2,1,0:T(1,128)}, u32[]{:S(2)}, u32[]{:S(2)}) async-start(f32[64,1,64]{2,1,0:T(1,128)} %broadcast_in_dim.62), calls=%async_computation.14 | async-start | bytes 65536 | tf_op jit(solution)/shard_map/all_to_all | solution.py:37
  376.8 16.1 %all-to-all-start.15 = ((f32[4,1,64]{2,1,0:T(1,128)}), f32[4,1,64]{2,1,0:T(1,128)}, u32[]{:S(2)}, u32[]{:S(2)}) async-start(f32[4,1,64]{2,1,0:T(1,128)} %broadcast_in_dim.63), calls=%async_computation.15 | async-start | bytes 4096 | tf_op jit(solution)/shard_map/all_to_all | solution.py:37
  383.0 14.0 %collective-permute-start.28 = (f32[12,1,2,512]{3,2,1,0:T(2,128)}, f32[12,1,2,512]{3,2,1,0:T(2,128)}, u32[]{:S(2)}, u32[]{:S(2)}) collective-permute-start(f32[12,1,2,512]{3,2,1,0:T(2,128)} %get-tuple-element.109), channel_id=1, source_target_pairs={{0,32},{32,64},{64,96},{96,128},{128,160},{160,192},{192,224},{1,3... | collective-permute-start | bytes 147464 | tf_op jit(solution)/shard_map/ppermute | solution.py:23
  387.1 12.6 %collective-permute-start.29 = (f32[12,1,2,512]{3,2,1,0:T(2,128)}, f32[12,1,2,512]{3,2,1,0:T(2,128)}, u32[]{:S(2)}, u32[]{:S(2)}) collective-permute-start(f32[12,1,2,512]{3,2,1,0:T(2,128)} %get-tuple-element.108), channel_id=1, source_target_pairs={{32,0},{64,32},{96,64},{128,96},{160,128},{192,160},{224,192},{33,... | collective-permute-start | bytes 147464 | tf_op jit(solution)/shard_map/ppermute | solution.py:24
  389.0 8.9 %collective-permute-start.30 = (f32[12,2,1,512]{3,2,1,0:T(1,128)}, f32[12,2,1,512]{3,2,1,0:T(1,128)}, u32[]{:S(2)}, u32[]{:S(2)}) collective-permute-start(f32[12,2,1,512]{3,2,1,0:T(1,128)} %get-tuple-element.107), channel_id=1, source_target_pairs={{0,1},{1,2},{2,3},{3,4},{4,5},{5,6},{6,7},{7,8},{8,9},{9,10},{10,1... | collective-permute-start | bytes 147464 | tf_op jit(solution)/shard_map/ppermute | solution.py:23
  391.6 7.1 %collective-permute-start.31 = (f32[12,2,1,512]{3,2,1,0:T(1,128)}, f32[12,2,1,512]{3,2,1,0:T(1,128)}, u32[]{:S(2)}, u32[]{:S(2)}) collective-permute-start(f32[12,2,1,512]{3,2,1,0:T(1,128)} %get-tuple-element.106), channel_id=1, source_target_pairs={{1,0},{2,1},{3,2},{4,3},{5,4},{6,5},{7,6},{8,7},{9,8},{10,9},{11,1... | collective-permute-start | bytes 147464 | tf_op jit(solution)/shard_map/ppermute | solution.py:24
  411.6 16.9 %all-to-all-start.16 = ((f32[64,1,3]{2,1,0:T(1,128)}), f32[64,1,3]{2,1,0:T(1,128)S(1)}, u32[]{:S(2)}, u32[]{:S(2)}) async-start(f32[64,1,3]{2,1,0:T(1,128)} %broadcast_in_dim.64), calls=%async_computation.16 | async-start | bytes 65536 | tf_op jit(solution)/shard_map/all_to_all | solution.py:37
  (31 other events, 704.7 us)
where the time goes:
time: 454 us; the launch traced here: 449 us
  starting transfers between devices  160 us (35%)
  blocking collectives  78.8 us (17%)
  other arithmetic  73.5 us (16%)
  waiting for transfers between devices  69.1 us (15%)
  local copies, waits for them, and re-layouts  48.3 us (11%)
  between operations  10.9 us (2%)
  matrix products  8.43 us (2%)
    all_to_all x12, starting transfers between devices, copy_for_each(): lax.all_to_all(jnp.broadcast_to(shard[None], (size, *shard.shape)), axis,...  79.6 us
    all_to_all x6, blocking collectives, copy_for_each(): lax.all_to_all(jnp.broadcast_to(shard[None], (size, *shard.shape)), axis,...  78.8 us
    all_to_all x12, waiting for transfers between devices, copy_for_each(): lax.all_to_all(jnp.broadcast_to(shard[None], (size, *shard.shape)), axis,...  57 us
    ppermute x16, starting transfers between devices, with_halo(): lax.ppermute(last, axis, up)  54.3 us
    ppermute x16, starting transfers between devices, with_halo(): lax.ppermute(initial, axis, [(b, a) for a, b in up])  25.8 us
    ppermute x16, waiting for transfers between devices, with_halo(): lax.ppermute(initial, axis, [(b, a) for a, b in up])  12 us
  transfers between devices with their start and end apart: 44, of which 14 were waited for; matrix products, arithmetic and copies ran while one was open for 7% of the time, Pallas kernels for 0%

commit v1 on v0

v1 whole, which is shorter than its diff:
```python
import jax
import jax.numpy as jnp
from jax import lax
from jax.experimental import pallas as pl
from jax.experimental.pallas import tpu as pltpu
from jax.sharding import PartitionSpec as P

EPSILON = 1e-06
NC = 12
AGG = 8
F32 = jnp.float32
ROWS, LANES = 8, 128
VMEM = pl.BlockSpec(memory_space=pltpu.VMEM)
SMEM = pl.BlockSpec(memory_space=pltpu.SMEM)


def dense(a):
    s = a.shape[:-2]
    n = len(s)
    a = jnp.swapaxes(a.reshape(s + (2, 4, LANES)), n, n + 1)
    return a.reshape(s + (ROWS, LANES))


def undense(a):
    s = a.shape[:-2]
    n = len(s)
    a = jnp.swapaxes(a.reshape(s + (4, 2, LANES)), n, n + 1)
    return a.reshape(s + (2, 4 * LANES))


def grids():
    return (
        lax.broadcasted_iota(jnp.int32, (ROWS, LANES), 0),
        lax.broadcasted_iota(jnp.int32, (ROWS, LANES), 1),
    )


def even_rows():
    return (grids()[0] & 1) == 0


def turn(a, shift, axis):
    return pltpu.roll(a, shift % a.shape[axis], axis)


def pack_low(f):
    return jnp.where(even_rows(), f[0], turn(f[1], 1, 0))


def pack_high(f):
    return jnp.where(even_rows(), turn(f[0], -1, 0), f[1])


def along_y(f):
    row, lane = grids()
    t = turn(f, 1, 1)
    before = jnp.where(lane == 0, jnp.where(row < 2, 0.0, turn(t, 2, 0)), t)
    t = turn(f, -1, 1)
    after = jnp.where(lane == LANES - 1, jnp.where(row >= ROWS - 2, 0.0, turn(t, -2, 0)), t)
    return before, after


def near(f, zlo, zhi, xlo, xhi):
    even = even_rows()
    y0, y1 = along_y(f[0]), along_y(f[1])
    xm = (
        jnp.where(even, xlo, turn(f[0], 1, 0)),
        jnp.where(even, turn(xlo, -1, 0), turn(f[1], 1, 0)),
    )
    xp = (
        jnp.where(even, turn(f[0], -1, 0), turn(xhi, 1, 0)),
        jnp.where(even, turn(f[1], -1, 0), xhi),
    )
    return ((zlo, f[0]), (f[1], zhi), xm, xp, (y0[0], y1[0]), (y0[1], y1[1]))


def position():
    return lax.axis_index("gz"), lax.axis_index("xy")


def edges(sizes, halos):
    g, s = position()
    ok = (g > 0, g < sizes[0] - 1, s > 0, s < sizes[1] - 1)
    return [jnp.where(o, h, 0.0) for o, h in zip(ok, halos)]


def total(a):
    return jnp.sum(jnp.sum(a, axis=0, keepdims=True), axis=1, keepdims=True)


def scalar_stencil(f, halos, pd, po):
    nb = near(f, *halos)
    out = []
    for z in range(2):
        t = pd[z].astype(F32) * f[z]
        for k in range(6):
            t = t + po[k, z].astype(F32) * nb[k][z]
        out.append(t)
    return out


def call(body, outs, ins, args, **kw):
    return pl.pallas_call(
        body,
        out_shape=[jax.ShapeDtypeStruct(o, F32) for o in outs],
        in_specs=ins,
        out_specs=[VMEM] * len(outs),
        **kw,
    )(*args)


def rings(msgs):
    out = []
    for m, (axis, step) in zip(msgs, (("gz", 1), ("gz", -1), ("xy", 1), ("xy", -1))):
        if m is None:
            continue
        n = lax.axis_size(axis)
        out.append(lax.ppermute(m, axis, [(i, (i + step) % n) for i in range(n)]))
    return out


def spread(buf, axis):
    return lax.all_to_all(buf, axis, 0, 0, tiled=True)


def guess_of(v, pw, pd, rhs_ref, fg_ref):
    fg = []
    for z in range(2):
        t = pw[0, z].astype(F32) * v[0][z]
        for i in range(1, NC):
            t = t + pw[i, z].astype(F32) * v[i][z]
        rhs_ref[z] = t
        fg.append(t / pd[z].astype(F32))
        fg_ref[z] = fg[z]
    return fg


def first_kernel(
    cols, r, pw, pd, wi, inv, rhs_ref, fg_ref, up_z, down_z, up_x, down_x, wc_ref, ws_ref
):
    v = [[r[i, z] for z in range(2)] for i in range(NC)]
    fg = guess_of(v, pw, pd, rhs_ref, fg_ref)
    low, high = pack_low(fg), pack_high(fg)
    rows = [[inv[z, x].astype(F32) for x in range(2)] for z in range(2)]
    for ref, field, pair in (
        (up_z, fg[1], rows[1]),
        (down_z, fg[0], rows[0]),
        (up_x, high, (rows[0][1], rows[1][1])),
        (down_x, low, (rows[0][0], rows[1][0])),
    ):
        ref[0] = field
        for n in range(2):
            for h in range(2):
                ref[1 + 2 * n + h] = jnp.zeros((ROWS, LANES), F32)
                ref[1 + 2 * n + h, :, 0:64] = pair[n][8 * h : 8 * h + 8]
    row, lane = grids()
    _, s = position()
    here = (2 * s + (row & 1)) * 512 + (row >> 1) * LANES + lane
    count = jnp.zeros((ROWS, LANES), F32)
    for w in range(cols.shape[0]):
        count = count + jnp.where(here == cols[w], 1.0, 0.0)
    for z in range(2):
        wc_ref[z] = wi[z] * count
    ws_ref[...] = wi[0] + wi[1]


def coarse_kernel(sizes, extra_is_dots, fg, rhs, zlo, zhi, xlo, xhi, pd, po, ag, lv, extra, part_ref,
                  up_z, down_z, up_x, down_x, buf):
    halos = edges(sizes, [h[0] for h in (zlo, zhi, xlo, xhi)])
    f = [fg[0], fg[1]]
    applied = scalar_stencil(f, halos, pd, po)
    row16 = lax.broadcasted_iota(jnp.int32, (16, LANES), 0)
    lane16 = lax.broadcasted_iota(jnp.int32, (16, LANES), 1)
    even = (lax.broadcasted_iota(jnp.int32, (ROWS, 1), 0) & 1) == 0
    g, s = position()
    tile = jnp.zeros((16, LANES), F32)
    part = []
    for z in range(2):
        rest = rhs[z] - applied[z]
        level = lv[z]
        guess = f[z]
        sums = jnp.zeros((ROWS, 1), F32)
        for a in range(AGG):
            mine = ag[z] == a
            c = jnp.sum(jnp.where(mine, rest, 0.0), axis=1, keepdims=True)
            value = c / level[:, a : a + 1]
            guess = guess + jnp.where(mine, value, 0.0)
            sums = sums + (c - level[:, AGG + a : AGG + a + 1] * value)
        part.append(guess)
        part_ref[z] = guess
        for x in range(2):
            t = jnp.sum(jnp.where(even if x == 0 else ~even, sums, 0.0), axis=0, keepdims=True)
            tile = tile + jnp.where((row16 == 2 * g + z) & (lane16 == 2 * s + x), t, 0.0)
    up_z[...] = part[1]
    down_z[...] = part[0]
    up_x[...] = pack_high(part)
    down_x[...] = pack_low(part)
    top = tile[0:8] + extra[...] if extra_is_dots else tile[0:8]
    for m in range(buf.shape[0]):
        buf[m, 0] = top
        buf[m, 1] = tile[8:16]
        if not extra_is_dots:
            buf[m, 2] = extra[...]


def relay_kernel(n, got, *outs):
    size, parts = got.shape[0], got.shape[1]
    sums = []
    for q in range(parts):
        t = got[0, q]
        for m in range(1, size):
            t = t + got[m, q]
        sums.append(t)
    for m in range(outs[0].shape[0]):
        for q in range(n):
            outs[0][m, q] = sums[q]
    if len(outs) > 1:
        outs[1][...] = sums[n]


def pressure_kernel(sizes, got, inv, nz, pz, nx, px, part, hzlo, hzhi, hxlo, hxhi, rhs, pd, po, wi,
                    p_ref, buf, up_x, down_x, tops_ref):
    even = even_rows()
    t = [got[0, q] for q in range(2)]
    for m in range(1, got.shape[0]):
        t = [t[q] + got[m, q] for q in range(2)]
    tops_ref[...] = t[0]
    a, b = t[0][:, 0:64], t[1][:, 0:64]

    def beside(ref):
        return [total(ref[1 + 2 * n, :, 0:64] * a + ref[2 + 2 * n, :, 0:64] * b) for n in range(2)]

    own = []
    for z in range(2):
        pair = []
        for x in range(2):
            w = inv[z, x].astype(F32)
            pair.append(total(w[0:8] * a + w[8:16] * b))
        own.append(jnp.where(even, pair[0], pair[1]))
    halos = []
    for ref, h in ((nz, hzlo), (pz, hzhi), (nx, hxlo), (px, hxhi)):
        c = beside(ref)
        halos.append(h[...] + jnp.where(even, c[0], c[1]))
    halos = edges(sizes, halos)
    f = [part[z] + own[z] for z in range(2)]
    applied = scalar_stencil(f, halos, pd, po)
    p = []
    for z in range(2):
        p.append(f[z] + (rhs[z] - applied[z]) / pd[z].astype(F32))
        p_ref[z] = p[z]
    up_x[...] = pack_high(p)
    down_x[...] = pack_low(p)
    column = wi[0] * p[0] + wi[1] * p[1]
    for m in range(buf.shape[0]):
        buf[m, 0] = p[0]
        buf[m, 1] = p[1]
        buf[m, 2] = column


def columns_of(got, q):
    t = got[0, q]
    for m in range(1, got.shape[0]):
        t = t + got[m, q]
    return t


def steps_of(tops):
    rr, rw, ww = (total(tops[0:1, 64 + m : 65 + m]) for m in range(3))
    beta = jnp.sqrt(rr + EPSILON)
    h00 = rw / (beta * beta)
    rest = jnp.maximum(ww / (beta * beta) - h00 * h00, 0.0)
    return beta, h00, jnp.sqrt(rest + EPSILON)


def direction_kernel(sizes, later, v, p, got, hxlo, hxhi, jd, jo, bi, wc, wsum, wi, tops, d0,
                     d_ref, up_z, down_z, up_x, down_x, buf):
    g, _ = position()
    f = [p[0], p[1]]
    halos = edges(
        sizes,
        [got[jnp.maximum(g - 1, 0), 1], got[jnp.minimum(g + 1, sizes[0] - 1), 0], hxlo[...], hxhi[...]],
    )
    nb = near(f, *halos)
    level = columns_of(got, 2) / wsum[...]
    rem = []
    for i in range(NC):
        pair = []
        for z in range(2):
            t = jd[i, z].astype(F32) * f[z]
            for k in range(6):
                t = t + jo[k, i, z].astype(F32) * nb[k][z]
            if i == 0:
                t = t + wc[z] * (f[z] - level)
            pair.append(v[i, z] - t)
        rem.append(pair)
    if later:
        beta, h00, h10 = steps_of(tops)
        scale = 1.0 / (beta * h10)
    for i in range(NC):
        pair = []
        for z in range(2):
            ts = [None, None]
            for j in range(NC):
                u = bi[i, j, z].astype(F32) * rem[j][z]
                ts[j % 2] = u if ts[j % 2] is None else ts[j % 2] + u
            t = ts[0] + ts[1]
            if i == 0:
                t = t + f[z]
            if later:
                t = (t - h00 * d0[i, z]) * scale
            d_ref[i, z] = t
            pair.append(t)
        up_z[i] = pair[1]
        down_z[i] = pair[0]
        up_x[i] = pack_high(pair)
        down_x[i] = pack_low(pair)
        if i == 0:
            column = wi[0] * pair[0] + wi[1] * pair[1]
            for m in range(buf.shape[0]):
                buf[m, 0] = column


def image_kernel(sizes, later, d, zlo, zhi, xlo, xhi, got, jd, jo, wc, wsum, r, w0, tops, pw, pd,
                 w_ref, dots_ref, *more):
    *outs, nb = more
    level = columns_of(got, 0) / wsum[...]
    for j in range(NC):
        f = [d[j, 0], d[j, 1]]
        n = near(f, *edges(sizes, [h[j] for h in (zlo, zhi, xlo, xhi)]))
        for z in range(2):
            nb[0, j, z] = f[z]
            for k in range(6):
                nb[k + 1, j, z] = n[k][z]

    def row(i, carry):
        for z in range(2):
            ts = [None] * 4
            for k in range(7):
                for j in range(NC):
                    c = (jd[i, j, z] if k == 0 else jo[k - 1, i, j, z]).astype(F32)
                    u = c * nb[k, j, z]
                    q = j % 4
                    ts[q] = u if ts[q] is None else ts[q] + u
            w_ref[i, z] = (ts[0] + ts[1]) + (ts[2] + ts[3])
        return carry

    lax.fori_loop(0, NC, row, 0)
    for z in range(2):
        w_ref[0, z] = w_ref[0, z] + wc[z] * (d[0, z] - level)
    if later:
        beta, h00, h10 = steps_of(tops)
        scale = 1.0 / (beta * h10)
    sums = [jnp.zeros((ROWS, LANES), F32) for _ in range(3)]
    for i in range(NC):
        for z in range(2):
            w = w_ref[i, z]
            if later:
                first = w * (r[i, z] * (1.0 / beta))
                second = w * ((w0[i, z] - h00 * r[i, z]) * scale)
            else:
                first = r[i, z] * r[i, z]
                second = w * r[i, z]
            sums = [sums[0] + first, sums[1] + second, sums[2] + w * w]
    row_at, lane = grids()
    t = jnp.zeros((ROWS, LANES), F32)
    for m in range(3):
        t = t + jnp.where((row_at == 0) & (lane == 64 + m), total(sums[m]), 0.0)
    if later:
        for m in range(dots_ref.shape[0]):
            dots_ref[m, 0] = t
    else:
        dots_ref[...] = t
        rhs_ref, fg_ref, up_z, down_z, up_x, down_x = outs
        v = [[w_ref[i, z] for z in range(2)] for i in range(NC)]
        fg = guess_of(v, pw, pd, rhs_ref, fg_ref)
        up_z[0] = fg[1]
        down_z[0] = fg[0]
        up_x[0] = pack_high(fg)
        down_x[0] = pack_low(fg)


def last_kernel(got, tops, r, d0, w0, d1, w1, sol_ref, res_ref, hess_ref):
    t = got[0, 0]
    for m in range(1, got.shape[0]):
        t = t + got[m, 0]
    h01, h11, norm = (total(t[0:1, 64 + m : 65 + m]) for m in range(3))
    beta, h00, h10 = steps_of(tops)
    h21 = jnp.sqrt(jnp.maximum(norm - h01 * h01 - h11 * h11, 0.0) + EPSILON)
    radius = jnp.sqrt(h00 * h00 + h10 * h10)
    c0, s0 = h00 / radius, h10 / radius
    u00, u01, u11 = radius, c0 * h01 + s0 * h11, c0 * h11 - s0 * h01
    t0, t1 = c0 * beta, -s0 * beta
    radius = jnp.sqrt(u11 * u11 + h21 * h21)
    t1 = (u11 / radius) * t1
    y1 = t1 / radius
    y0 = (t0 - u01 * y1) / u00
    y0 = y0 / beta
    for i in range(NC):
        for z in range(2):
            sol_ref[i, z] = y0 * d0[i, z] + y1 * d1[i, z]
            res_ref[i, z] = r[i, z] - (y0 * w0[i, z] + y1 * w1[i, z])
    at = lax.broadcasted_iota(jnp.int32, (3, 2), 0)
    col = lax.broadcasted_iota(jnp.int32, (3, 2), 1)
    h = jnp.zeros((3, 2), F32)
    for i, j, value in ((0, 0, h00), (1, 0, h10), (0, 1, h01), (1, 1, h11), (2, 1, h21)):
        h = h + jnp.where((at == i) & (col == j), value, 0.0)
    hess_ref[...] = h


def on_device(
    right_side, jac_diag, jac_off, block_inv, press_weight, press_diag, press_off, well_index,
    well_columns, agg_map, level1_op, coarsest_inv,
):
    sizes = (lax.axis_size("gz"), lax.axis_size("xy"))
    r, jd, jo, bi = dense(right_side), dense(jac_diag), dense(jac_off), dense(block_inv)
    pw, pd, po = dense(press_weight), dense(press_diag), dense(press_off)
    wi, ag = dense(well_index), dense(agg_map)
    op = level1_op.astype(F32)
    lv = jnp.concatenate([jnp.stack([op[a, a] for a in range(AGG)]), jnp.sum(op, axis=0)])
    lv = lv.transpose(1, 3, 2, 0).reshape(2, ROWS, 2 * AGG)
    vec, field, plane, msg = (NC, 2, ROWS, LANES), (2, ROWS, LANES), (ROWS, LANES), (5, ROWS, LANES)
    side = (NC, ROWS, LANES)
    gz, xy = sizes
    jd0, jo0 = jd[:, 0], jo[:, :, 0]

    def bind(body, *static):
        def kernel(*refs):
            return body(*static, *refs)

        return kernel

    rhs, fg, *msgs, wc, ws = call(
        first_kernel, [field, field, msg, msg, msg, msg, field, plane], [SMEM] + [VMEM] * 5,
        (well_columns, r, pw, pd, wi, coarsest_inv),
    )
    v, extra, rows, wsum = r, ws, None, None
    kept = []
    for step in range(2):
        later = step == 1
        halo = rings(msgs)
        rows = halo if rows is None else rows
        parts = 2 if later else 3
        part, *msgs, buf = call(
            bind(coarse_kernel, sizes, later), [field] + [plane] * 4 + [(gz, parts, ROWS, LANES)],
            [VMEM] * 11, (fg, rhs, *halo, pd, po, ag, lv, extra),
        )
        halo = rings(msgs)
        got = spread(buf, "gz")
        outs = [(xy, 2, ROWS, LANES)] + ([] if later else [plane])
        buf, *found = call(bind(relay_kernel, 2), outs, [VMEM], (got,))
        wsum = found[0] if found else wsum
        got = spread(buf, "xy")
        p, buf, *msgs, tops = call(
            bind(pressure_kernel, sizes), [field, (gz, 3, ROWS, LANES), plane, plane, plane],
            [VMEM] * 15, (got, coarsest_inv, *rows, part, *halo, rhs, pd, po, wi),
        )
        xlo, xhi = rings([None, None, *msgs])
        got = spread(buf, "gz")
        d0 = kept[0][0] if later else r
        d, *msgs, buf = call(
            bind(direction_kernel, sizes, later), [vec, side, side, side, side, (gz, 1, ROWS, LANES)],
            [VMEM] * 13,
            (v, p, got, xlo, xhi, jd0, jo0, bi, wc, wsum, wi, tops, d0),
        )
        halo = rings(msgs)
        got = spread(buf, "gz")
        outs = [vec, (gz, 1, ROWS, LANES)] if later else [vec, plane, field, field] + [(1, *plane)] * 4
        w0 = kept[0][1] if later else r
        w, dots, *more = call(
            bind(image_kernel, sizes, later), outs, [VMEM] * 15,
            (d, *halo, got, jd, jo, wc, wsum, r, w0, tops, pw, pd),
            scratch_shapes=[pltpu.VMEM((7, NC, 2, ROWS, LANES), F32)],
        )
        kept.append((d, w))
        if not later:
            rhs, fg, *msgs = more
            v, extra = w, dots
    got = spread(dots, "gz")
    (buf,) = call(bind(relay_kernel, 1), [(xy, 1, ROWS, LANES)], [VMEM], (got,))
    got = spread(buf, "xy")
    solution, residual, hessenberg = call(
        last_kernel, [vec, vec, (3, 2)], [VMEM] * 7, (got, tops, r, *kept[0], *kept[1])
    )
    return undense(solution), undense(residual), hessenberg


def solution(mesh):
    return jax.shard_map(
        on_device,
        mesh=mesh,
        in_specs=(
            P(None, "gz", "xy", None),
            P(None, None, "gz", "xy", None),
            P(None, None, None, "gz", "xy", None),
            P(None, None, "gz", "xy", None),
            P(None, "gz", "xy", None),
            P("gz", "xy", None),
            P(None, "gz", "xy", None),
            P("gz", "xy", None),
            P(),
            P("gz", "xy", None),
            P(None, None, "gz", "xy", None),
            P("gz", "xy", None, None),
        ),
        out_specs=(P(None, "gz", "xy", None), P(None, "gz", "xy", None), P()),
        check_vma=False,
    )
```

time: 454 us -> 203 us (0.45)
  starting transfers between devices: 160 us -> 80.4 us
  other arithmetic: 73.5 us -> 1.56 us
  waiting for transfers between devices: 69.1 us -> 10.8 us
  local copies, waits for them, and re-layouts: 48.3 us -> 10.3 us
  Pallas kernels: 0 us -> 29.4 us
  blocking collectives: 78.8 us -> 68.1 us
  between operations: 10.9 us -> 0.96 us
  matrix products: 8.43 us -> 0 us
    all_to_all x12 -> x4, starting transfers between devices: 79.6 us -> 26.8 us  [spread(): return lax.all_to_all(buf, axis, 0, 0, tiled=True)]
    all_to_all x12 -> x4, waiting for transfers between devices: 57 us -> 6.51 us  [spread(): return lax.all_to_all(buf, axis, 0, 0, tiled=True)]
    reduce_sum x45 -> x1, other arithmetic: 39.6 us -> 0.8 us  [on_device(): jnp.sum(op, axis=0)]
    pallas_call x0 -> x13, Pallas kernels: none -> 29.4 us  [call(): pl.pallas_call(body, out_shape=[jax.ShapeDtypeStruct(o, F32) for o in out...]
    ppermute x32 -> x28, starting transfers between devices: 80.2 us -> 53.6 us  [rings(): out.append(lax.ppermute(m, axis, [(i, (i + step) % n) for i in range(n)]))]
    all_to_all x6, blocking collectives: 78.8 us -> 68.1 us  [spread(): return lax.all_to_all(buf, axis, 0, 0, tiled=True)]
    concatenate x11 -> x0, other arithmetic: 9.23 us -> none  [the longest x8 5.13 us: with_halo(): jnp.concatenate([jnp.pad(low, around), shard, jnp.pad(high, around)], axi...]
    broadcast_in_dim x16 -> x0, local copies, waits for them, and re-layouts: 8.98 us -> none  [copy_for_each(): jnp.broadcast_to(shard[None], (size, *shard.shape))]
  transfers between devices with their start and end apart: 44 -> 32, of which waited for: 14 -> 5; matrix products, arithmetic and copies ran while one was open for 7% -> 3% of each run, Pallas kernels for 0% -> 0%
where the time goes in v1:
time: 203 us; the launch traced here: 201 us
  starting transfers between devices  80.4 us (40%)
  blocking collectives  68.1 us (34%)
  Pallas kernels  29.4 us (14%)
  waiting for transfers between devices  10.8 us (5%)
  local copies, waits for them, and re-layouts  10.3 us (5%)
    all_to_all x6, blocking collectives, spread(): return lax.all_to_all(buf, axis, 0, 0, tiled=True)  68.1 us
    ppermute x28, starting transfers between devices, rings(): out.append(lax.ppermute(m, axis, [(i, (i + step) % n) for i in range(n)]))  53.6 us
    pallas_call x13, Pallas kernels, call(): pl.pallas_call(body, out_shape=[jax.ShapeDtypeStruct(o, F32) for o in out...  29.4 us
    all_to_all x4, starting transfers between devices, spread(): return lax.all_to_all(buf, axis, 0, 0, tiled=True)  26.8 us
    all_to_all x4, waiting for transfers between devices, spread(): return lax.all_to_all(buf, axis, 0, 0, tiled=True)  6.51 us
    unnamed x65, local copies, waits for them, and re-layouts  6.38 us
    ppermute x28, waiting for transfers between devices, rings(): out.append(lax.ppermute(m, axis, [(i, (i + step) % n) for i in range(n)]))  4.26 us
  transfers between devices with their start and end apart: 32, of which 5 were waited for; matrix products, arithmetic and copies ran while one was open for 3% of the time, Pallas kernels for 0%

profile of v1, /device:TPU:1, one launch (start us, length us, event | category | flops | bytes accessed | tf_op | source)
XLA Modules:
  0.0 201.5 jit_solution(12643717025041359064)
XLA Ops:
  0.6 1.6 shard_map.139
  2.3 2.7 %collective-permute-start = (f32[5,8,128]{2,1,0:T(8,128)}, f32[5,8,128]{2,1,0:T(8,128)S(1)}, u32[]{:S(2)}, u32[]{:S(2)}) collective-permute-start(f32[5,8,128]{2,1,0:T(8,128)} %get-tuple-element.62), channel_id=1, source_target_pairs={{0,32},{32,64},{64,96},{96,128},{128,160},{160,192},{192,224},{224... | collective-permute-start | bytes 61448 | tf_op jit(solution)/shard_map/ppermute | solution.py:118
  6.2 6.6 %collective-permute-start.3 = (f32[5,8,128]{2,1,0:T(8,128)}, f32[5,8,128]{2,1,0:T(8,128)S(1)}, u32[]{:S(2)}, u32[]{:S(2)}) collective-permute-start(f32[5,8,128]{2,1,0:T(8,128)} %get-tuple-element.65), channel_id=1, source_target_pairs={{0,31},{1,0},{2,1},{3,2},{4,3},{5,4},{6,5},{7,6},{8,7},{9,8},{10,9... | collective-permute-start | bytes 61448 | tf_op jit(solution)/shard_map/ppermute | solution.py:118
  13.6 0.8 convert_reduce_fusion
  15.8 2.0 shard_map.140
  17.7 11.0 %all_to_all.50.refs_0_ = f32[8,3,8,128]{3,2,1,0:T(8,128)} all-to-all(f32[8,3,8,128]{3,2,1,0:T(8,128)} %get-tuple-element.67), channel_id=1, replica_groups=mesh['gz'=8,'xy'=32] {'gz'}, dimensions={0} | all-to-all | bytes 196608 | tf_op jit(solution)/shard_map/all_to_all | solution.py:123
  28.7 1.6 shard_map.141
  30.3 8.1 %all-to-all-start.1 = ((f32[32,2,8,128]{3,2,1,0:T(8,128)}), f32[32,2,8,128]{3,2,1,0:T(8,128)S(1)}, u32[]{:S(2)}, u32[]{:S(2)}) async-start(f32[32,2,8,128]{3,2,1,0:T(8,128)} %get-tuple-element.68), calls=%async_computation.1 | async-start | bytes 524288 | tf_op jit(solution)/shard_map/all_to_all | solution.py:123
  38.4 1.3 collective-permute-start.4
  39.7 1.5 collective-permute-start.6
  41.2 3.4 %collective-permute-start.7 = (f32[8,128]{1,0:T(8,128)}, f32[8,128]{1,0:T(8,128)S(1)}, u32[]{:S(2)}, u32[]{:S(2)}) collective-permute-start(f32[8,128]{1,0:T(8,128)} %get-tuple-element.73), channel_id=1, source_target_pairs={{0,31},{1,0},{2,1},{3,2},{4,3},{5,4},{6,5},{7,6},{8,7},{9,8},{10,9... | collective-permute-start | bytes 12296 | tf_op jit(solution)/shard_map/ppermute | solution.py:118
  44.6 1.7 slice_bitcast_fusion.refs_6_
  46.4 3.2 %all-to-all-done.1.refs_0_ = f32[32,2,8,128]{3,2,1,0:T(8,128)S(1)} async-done(((f32[32,2,8,128]{3,2,1,0:T(8,128)}), f32[32,2,8,128]{3,2,1,0:T(8,128)S(1)}, u32[]{:S(2)}, u32[]{:S(2)}) %all-to-all-start.1) | async-done | bytes 262176 | tf_op jit(solution)/shard_map/all_to_all | solution.py:123
  50.4 1.9 shard_map.142
  52.3 5.7 %all-to-all-start.2 = ((f32[8,3,8,128]{3,2,1,0:T(8,128)}), f32[8,3,8,128]{3,2,1,0:T(8,128)S(1)}, u32[]{:S(2)}, u32[]{:S(2)}) async-start(f32[8,3,8,128]{3,2,1,0:T(8,128)} %get-tuple-element.75), calls=%async_computation.2 | async-start | bytes 196608 | tf_op jit(solution)/shard_map/all_to_all | solution.py:123
  58.0 4.8 %collective-permute-start.9 = (f32[8,128]{1,0:T(8,128)}, f32[8,128]{1,0:T(8,128)S(1)}, u32[]{:S(2)}, u32[]{:S(2)}) collective-permute-start(f32[8,128]{1,0:T(8,128)} %get-tuple-element.77), channel_id=1, source_target_pairs={{0,31},{1,0},{2,1},{3,2},{4,3},{5,4},{6,5},{7,6},{8,7},{9,8},{10,9... | collective-permute-start | bytes 12296 | tf_op jit(solution)/shard_map/ppermute | solution.py:118
  62.8 1.4 slice_bitcast_fusion.1.refs_5_
  64.9 2.2 %shard_map.143 = (f32[12,2,8,128]{3,2,1,0:T(8,128)}, f32[12,8,128]{2,1,0:T(8,128)}, f32[12,8,128]{2,1,0:T(8,128)}, f32[12,8,128]{2,1,0:T(8,128)}, f32[12,8,128]{2,1,0:T(8,128)}, /*index=5*/f32[8,1,8,128]{3,2,1,0:T(8,128)}) custom-call(f32[12,2,8,128]{3,2,1,0:T(8,128)} %bitcast.81, f32[2,8,128]{2,1,0:T(8,128)} %get-tuple-element.74.refs_1_, ...), custom_call_target="tpu_custom_call" | custom-call | tf_op jit(solution)/shard_map/pallas_call | solution.py:103
  67.1 2.5 %collective-permute-start.10 = (f32[12,8,128]{2,1,0:T(8,128)}, f32[12,8,128]{2,1,0:T(8,128)S(1)}, u32[]{:S(2)}, u32[]{:S(2)}) collective-permute-start(f32[12,8,128]{2,1,0:T(8,128)} %get-tuple-element.82), channel_id=1, source_target_pairs={{0,32},{32,64},{64,96},{96,128},{128,160},{160,192},{192,224},{224... | collective-permute-start | bytes 147464 | tf_op jit(solution)/shard_map/ppermute | solution.py:118
  69.7 5.1 %collective-permute-start.13 = (f32[12,8,128]{2,1,0:T(8,128)}, f32[12,8,128]{2,1,0:T(8,128)S(1)}, u32[]{:S(2)}, u32[]{:S(2)}) collective-permute-start(f32[12,8,128]{2,1,0:T(8,128)} %get-tuple-element.85), channel_id=1, source_target_pairs={{0,31},{1,0},{2,1},{3,2},{4,3},{5,4},{6,5},{7,6},{8,7},{9,8},{10,9... | collective-permute-start | bytes 147464 | tf_op jit(solution)/shard_map/ppermute | solution.py:118
  74.7 10.4 %all_to_all.51.refs_5_ = f32[8,1,8,128]{3,2,1,0:T(8,128)} all-to-all(f32[8,1,8,128]{3,2,1,0:T(8,128)} %get-tuple-element.86), channel_id=1, replica_groups=mesh['gz'=8,'xy'=32] {'gz'}, dimensions={0} | all-to-all | bytes 65536 | tf_op jit(solution)/shard_map/all_to_all | solution.py:123
  85.8 4.0 %shard_map.144 = (f32[12,2,8,128]{3,2,1,0:T(8,128)}, f32[8,128]{1,0:T(8,128)}, f32[2,8,128]{2,1,0:T(8,128)}, f32[2,8,128]{2,1,0:T(8,128)}, f32[1,8,128]{2,1,0:T(...) custom-call(f32[12,2,8,128]{3,2,1,0:T(8,128)} %get-tuple-element.81.refs_0_.refs_12_.d0, ...), custom_call_target="tpu_custom_call" | custom-call | tf_op jit(solution)/shard_map/pallas_call | solution.py:103
  89.9 0.9 collective-permute-start.14
  90.8 4.8 %collective-permute-start.17 = (f32[1,8,128]{2,1,0:T(8,128)}, f32[1,8,128]{2,1,0:T(8,128)S(1)}, u32[]{:S(2)}, u32[]{:S(2)}) collective-permute-start(f32[1,8,128]{2,1,0:T(8,128)} %get-tuple-element.93), channel_id=1, source_target_pairs={{0,31},{1,0},{2,1},{3,2},{4,3},{5,4},{6,5},{7,6},{8,7},{9,8},{10,9... | collective-permute-start | bytes 12296 | tf_op jit(solution)/shard_map/ppermute | solution.py:118
  95.6 1.2 collective-permute-done.16.refs_4_
  97.4 1.8 shard_map.145
  99.2 12.7 %all_to_all.52.refs_0_ = f32[8,2,8,128]{3,2,1,0:T(8,128)} all-to-all(f32[8,2,8,128]{3,2,1,0:T(8,128)} %get-tuple-element.95), channel_id=1, replica_groups=mesh['gz'=8,'xy'=32] {'gz'}, dimensions={0} | all-to-all | bytes 131072 | tf_op jit(solution)/shard_map/all_to_all | solution.py:123
  111.9 1.6 shard_map.146
  113.5 7.4 %all-to-all-start.5 = ((f32[32,2,8,128]{3,2,1,0:T(8,128)}), f32[32,2,8,128]{3,2,1,0:T(8,128)S(1)}, u32[]{:S(2)}, u32[]{:S(2)}) async-start(f32[32,2,8,128]{3,2,1,0:T(8,128)} %shard_map.146), calls=%async_computation.5 | async-start | bytes 524288 | tf_op jit(solution)/shard_map/all_to_all | solution.py:123
  120.9 1.2 collective-permute-start.18
  122.1 1.5 collective-permute-start.20
  123.6 3.4 %collective-permute-start.21 = (f32[8,128]{1,0:T(8,128)}, f32[8,128]{1,0:T(8,128)S(1)}, u32[]{:S(2)}, u32[]{:S(2)}) collective-permute-start(f32[8,128]{1,0:T(8,128)} %get-tuple-element.100), channel_id=1, source_target_pairs={{0,31},{1,0},{2,1},{3,2},{4,3},{5,4},{6,5},{7,6},{8,7},{9,8},{10,9... | collective-permute-start | bytes 12296 | tf_op jit(solution)/shard_map/ppermute | solution.py:118
  127.1 1.8 collective-permute-done.20.refs_9_
  128.9 3.3 %all-to-all-done.5.refs_0_ = f32[32,2,8,128]{3,2,1,0:T(8,128)S(1)} async-done(((f32[32,2,8,128]{3,2,1,0:T(8,128)}), f32[32,2,8,128]{3,2,1,0:T(8,128)S(1)}, u32[]{:S(2)}, u32[]{:S(2)}) %all-to-all-start.5) | async-done | bytes 262176 | tf_op jit(solution)/shard_map/all_to_all | solution.py:123
  132.9 1.9 shard_map.147
  134.8 5.7 %all-to-all-start.6 = ((f32[8,3,8,128]{3,2,1,0:T(8,128)}), f32[8,3,8,128]{3,2,1,0:T(8,128)S(1)}, u32[]{:S(2)}, u32[]{:S(2)}) async-start(f32[8,3,8,128]{3,2,1,0:T(8,128)} %get-tuple-element.102), calls=%async_computation.6 | async-start | bytes 196608 | tf_op jit(solution)/shard_map/all_to_all | solution.py:123
  140.5 4.8 %collective-permute-start.23 = (f32[8,128]{1,0:T(8,128)}, f32[8,128]{1,0:T(8,128)S(1)}, u32[]{:S(2)}, u32[]{:S(2)}) collective-permute-start(f32[8,128]{1,0:T(8,128)} %get-tuple-element.104), channel_id=1, source_target_pairs={{0,31},{1,0},{2,1},{3,2},{4,3},{5,4},{6,5},{7,6},{8,7},{9,8},{10,9... | collective-permute-start | bytes 12296 | tf_op jit(solution)/shard_map/ppermute | solution.py:118
  145.3 1.2 collective-permute-done.22.refs_3_
  147.1 2.4 %shard_map.148 = (f32[12,2,8,128]{3,2,1,0:T(8,128)}, f32[12,8,128]{2,1,0:T(8,128)}, f32[12,8,128]{2,1,0:T(8,128)}, f32[12,8,128]{2,1,0:T(8,128)}, f32[12,8,128]{2,1,0:T(8,128)}, /*index=5*/f32[8,1,8,128]{3,2,1,0:T(8,128)}) custom-call(f32[12,2,8,128]{3,2,1,0:T(8,128)} %get-tuple-element.87.refs_0_.refs_11_.w0, f32[2,8,128]{2,1,0:T(8,128)} %get-tuple-element.101.refs_1_, ...), custom_call_target="tpu_custom_call" | custom-call | tf_op jit(solution)/shard_map/pallas_call | solution.py:103
  149.6 2.8 %collective-permute-start.24 = (f32[12,8,128]{2,1,0:T(8,128)}, f32[12,8,128]{2,1,0:T(8,128)S(1)}, u32[]{:S(2)}, u32[]{:S(2)}) collective-permute-start(f32[12,8,128]{2,1,0:T(8,128)} %get-tuple-element.107), channel_id=1, source_target_pairs={{0,32},{32,64},{64,96},{96,128},{128,160},{160,192},{192,224},{224... | collective-permute-start | bytes 147464 | tf_op jit(solution)/shard_map/ppermute | solution.py:118
  152.4 5.1 %collective-permute-start.27 = (f32[12,8,128]{2,1,0:T(8,128)}, f32[12,8,128]{2,1,0:T(8,128)S(1)}, u32[]{:S(2)}, u32[]{:S(2)}) collective-permute-start(f32[12,8,128]{2,1,0:T(8,128)} %get-tuple-element.110), channel_id=1, source_target_pairs={{0,31},{1,0},{2,1},{3,2},{4,3},{5,4},{6,5},{7,6},{8,7},{9,8},{10,9... | collective-permute-start | bytes 147464 | tf_op jit(solution)/shard_map/ppermute | solution.py:118
  157.4 10.4 %all_to_all.53.refs_5_ = f32[8,1,8,128]{3,2,1,0:T(8,128)} all-to-all(f32[8,1,8,128]{3,2,1,0:T(8,128)} %get-tuple-element.111), channel_id=1, replica_groups=mesh['gz'=8,'xy'=32] {'gz'}, dimensions={0} | all-to-all | bytes 65536 | tf_op jit(solution)/shard_map/all_to_all | solution.py:123
  168.5 4.4 %shard_map.149 = (f32[12,2,8,128]{3,2,1,0:T(8,128)}, f32[8,1,8,128]{3,2,1,0:T(8,128)}) custom-call(f32[12,2,8,128]{3,2,1,0:T(8,128)} %get-tuple-element.106.refs_0_.d1, f32[12,8,128]{2,1,0:T(8,128)} %copy-done.10, f32[12,8,128]{2,1,0:T(8,128)} %copy-done.12, f32[12,8,128]{2,1,0:T(8,128)} %copy-done.14, f32[12,8,128]{2,1,0:T(8,128)} %copy-done.15, ...), custom_call_target="tpu_custom_call" | custom-call | tf_op jit(solution)/shard_map/pallas_call | solution.py:103
  172.9 9.4 %all_to_all.54.refs_0_ = f32[8,1,8,128]{3,2,1,0:T(8,128)} all-to-all(f32[8,1,8,128]{3,2,1,0:T(8,128)} %get-tuple-element.112), channel_id=1, replica_groups=mesh['gz'=8,'xy'=32] {'gz'}, dimensions={0} | all-to-all | bytes 65536 | tf_op jit(solution)/shard_map/all_to_all | solution.py:123
  182.3 1.4 shard_map.150
  183.7 14.1 %all_to_all.55.got = f32[32,1,8,128]{3,2,1,0:T(8,128)} all-to-all(f32[32,1,8,128]{3,2,1,0:T(8,128)} %shard_map.150), channel_id=1, replica_groups=mesh['gz'=8,'xy'=32] {'xy'}, dimensions={0} | all-to-all | bytes 262144 | tf_op jit(solution)/shard_map/all_to_all | solution.py:123
  197.8 2.4 %shard_map.151 = (f32[12,2,8,128]{3,2,1,0:T(8,128)}, f32[12,2,8,128]{3,2,1,0:T(8,128)}, f32[3,2]{1,0:T(4,128)}) custom-call(f32[32,1,8,128]{3,2,1,0:T(8,128)} %all_to_all.55.got, f32[8,128]{1,0:T(8,128)} %get-tuple-element.105.refs_11_.refs_12_.tops, f32[12,2,8,128]{3,2,1,0:T(8,128)} %bitcast.86, f32[12,2,8,128]{3,2,1,0:T(8,128)} %get-tuple-element.81.refs_0_.refs_12_.d0, ...), custom_call_target="tpu_custom_call" | custom-call | tf_op jit(solution)/shard_map/pallas_call | solution.py:103
  200.2 1.3 copy.75
  (107 shorter events, 8.0 us)
Async XLA Ops:
  2.3 12.8 %collective-permute-start = (f32[5,8,128]{2,1,0:T(8,128)}, f32[5,8,128]{2,1,0:T(8,128)S(1)}, u32[]{:S(2)}, u32[]{:S(2)}) collective-permute-start(f32[5,8,128]{2,1,0:T(8,128)} %get-tuple-element.62), channel_id=1, source_target_pairs={{0,32},{32,64},{64,96},{96,128},{128,160},{160,192},{192,224},{224... | collective-permute-start | bytes 61448 | tf_op jit(solution)/shard_map/ppermute | solution.py:118
  4.9 10.2 %collective-permute-start.1 = (f32[5,8,128]{2,1,0:T(8,128)}, f32[5,8,128]{2,1,0:T(8,128)S(1)}, u32[]{:S(2)}, u32[]{:S(2)}) collective-permute-start(f32[5,8,128]{2,1,0:T(8,128)} %get-tuple-element.63), channel_id=1, source_target_pairs={{0,224},{32,0},{64,32},{96,64},{128,96},{160,128},{192,160},{224,1... | collective-permute-start | bytes 61448 | tf_op jit(solution)/shard_map/ppermute | solution.py:118
  5.5 9.6 %collective-permute-start.2 = (f32[5,8,128]{2,1,0:T(8,128)}, f32[5,8,128]{2,1,0:T(8,128)S(1)}, u32[]{:S(2)}, u32[]{:S(2)}) collective-permute-start(f32[5,8,128]{2,1,0:T(8,128)} %get-tuple-element.64), channel_id=1, source_target_pairs={{0,1},{1,2},{2,3},{3,4},{4,5},{5,6},{6,7},{7,8},{8,9},{9,10},{10,1... | collective-permute-start | bytes 61448 | tf_op jit(solution)/shard_map/ppermute | solution.py:118
  6.2 9.0 %collective-permute-start.3 = (f32[5,8,128]{2,1,0:T(8,128)}, f32[5,8,128]{2,1,0:T(8,128)S(1)}, u32[]{:S(2)}, u32[]{:S(2)}) collective-permute-start(f32[5,8,128]{2,1,0:T(8,128)} %get-tuple-element.65), channel_id=1, source_target_pairs={{0,31},{1,0},{2,1},{3,2},{4,3},{5,4},{6,5},{7,6},{8,7},{9,8},{10,9... | collective-permute-start | bytes 61448 | tf_op jit(solution)/shard_map/ppermute | solution.py:118
  30.3 19.3 %all-to-all-start.1 = ((f32[32,2,8,128]{3,2,1,0:T(8,128)}), f32[32,2,8,128]{3,2,1,0:T(8,128)S(1)}, u32[]{:S(2)}, u32[]{:S(2)}) async-start(f32[32,2,8,128]{3,2,1,0:T(8,128)} %get-tuple-element.68), calls=%async_computation.1 | async-start | bytes 524288 | tf_op jit(solution)/shard_map/all_to_all | solution.py:123
  38.4 7.9 %collective-permute-start.4 = (f32[8,128]{1,0:T(8,128)}, f32[8,128]{1,0:T(8,128)S(1)}, u32[]{:S(2)}, u32[]{:S(2)}) collective-permute-start(f32[8,128]{1,0:T(8,128)} %get-tuple-element.70), channel_id=1, source_target_pairs={{0,32},{32,64},{64,96},{96,128},{128,160},{160,192},{192,224},{224... | collective-permute-start | bytes 12296 | tf_op jit(solution)/shard_map/ppermute | solution.py:118
  39.7 6.7 %collective-permute-start.5 = (f32[8,128]{1,0:T(8,128)}, f32[8,128]{1,0:T(8,128)S(1)}, u32[]{:S(2)}, u32[]{:S(2)}) collective-permute-start(f32[8,128]{1,0:T(8,128)} %get-tuple-element.71), channel_id=1, source_target_pairs={{0,224},{32,0},{64,32},{96,64},{128,96},{160,128},{192,160},{224,1... | collective-permute-start | bytes 12296 | tf_op jit(solution)/shard_map/ppermute | solution.py:118
  39.7 6.7 %collective-permute-start.6 = (f32[8,128]{1,0:T(8,128)}, f32[8,128]{1,0:T(8,128)S(1)}, u32[]{:S(2)}, u32[]{:S(2)}) collective-permute-start(f32[8,128]{1,0:T(8,128)} %get-tuple-element.72), channel_id=1, source_target_pairs={{0,1},{1,2},{2,3},{3,4},{4,5},{5,6},{6,7},{7,8},{8,9},{9,10},{10,1... | collective-permute-start | bytes 12296 | tf_op jit(solution)/shard_map/ppermute | solution.py:118
  41.2 5.2 %collective-permute-start.7 = (f32[8,128]{1,0:T(8,128)}, f32[8,128]{1,0:T(8,128)S(1)}, u32[]{:S(2)}, u32[]{:S(2)}) collective-permute-start(f32[8,128]{1,0:T(8,128)} %get-tuple-element.73), channel_id=1, source_target_pairs={{0,31},{1,0},{2,1},{3,2},{4,3},{5,4},{6,5},{7,6},{8,7},{9,8},{10,9... | collective-permute-start | bytes 12296 | tf_op jit(solution)/shard_map/ppermute | solution.py:118
  46.4 3.3 %copy-start.17 = (f32[8,128]{1,0:T(8,128)}, f32[8,128]{1,0:T(8,128)S(1)}, u32[]{:S(2)}) copy-start(f32[8,128]{1,0:T(8,128)S(1)} %collective-permute-done.4.refs_7_) | copy-start | bytes 12292
  46.4 3.3 %copy-start.19 = (f32[8,128]{1,0:T(8,128)}, f32[8,128]{1,0:T(8,128)S(1)}, u32[]{:S(2)}) copy-start(f32[8,128]{1,0:T(8,128)S(1)} %collective-permute-done.5.refs_8_) | copy-start | bytes 12292
  46.4 3.2 %copy-start.21 = (f32[8,128]{1,0:T(8,128)}, f32[8,128]{1,0:T(8,128)S(1)}, u32[]{:S(2)}) copy-start(f32[8,128]{1,0:T(8,128)S(1)} %collective-permute-done.6.refs_9_) | copy-start | bytes 12292
  46.4 3.2 %copy-start.23 = (f32[8,128]{1,0:T(8,128)}, f32[8,128]{1,0:T(8,128)S(1)}, u32[]{:S(2)}) copy-start(f32[8,128]{1,0:T(8,128)S(1)} %collective-permute-done.7.refs_10_) | copy-start | bytes 12292
  49.7 0.7 copy-start.1
  52.3 11.9 %all-to-all-start.2 = ((f32[8,3,8,128]{3,2,1,0:T(8,128)}), f32[8,3,8,128]{3,2,1,0:T(8,128)S(1)}, u32[]{:S(2)}, u32[]{:S(2)}) async-start(f32[8,3,8,128]{3,2,1,0:T(8,128)} %get-tuple-element.75), calls=%async_computation.2 | async-start | bytes 196608 | tf_op jit(solution)/shard_map/all_to_all | solution.py:123
  58.0 6.2 %collective-permute-start.8 = (f32[8,128]{1,0:T(8,128)}, f32[8,128]{1,0:T(8,128)S(1)}, u32[]{:S(2)}, u32[]{:S(2)}) collective-permute-start(f32[8,128]{1,0:T(8,128)} %get-tuple-element.76), channel_id=1, source_target_pairs={{0,1},{1,2},{2,3},{3,4},{4,5},{5,6},{6,7},{7,8},{8,9},{9,10},{10,1... | collective-permute-start | bytes 12296 | tf_op jit(solution)/shard_map/ppermute | solution.py:118
  58.0 6.2 %collective-permute-start.9 = (f32[8,128]{1,0:T(8,128)}, f32[8,128]{1,0:T(8,128)S(1)}, u32[]{:S(2)}, u32[]{:S(2)}) collective-permute-start(f32[8,128]{1,0:T(8,128)} %get-tuple-element.77), channel_id=1, source_target_pairs={{0,31},{1,0},{2,1},{3,2},{4,3},{5,4},{6,5},{7,6},{8,7},{9,8},{10,9... | collective-permute-start | bytes 12296 | tf_op jit(solution)/shard_map/ppermute | solution.py:118
  64.3 0.6 copy-start.2
  67.1 18.0 %collective-permute-start.10 = (f32[12,8,128]{2,1,0:T(8,128)}, f32[12,8,128]{2,1,0:T(8,128)S(1)}, u32[]{:S(2)}, u32[]{:S(2)}) collective-permute-start(f32[12,8,128]{2,1,0:T(8,128)} %get-tuple-element.82), channel_id=1, source_target_pairs={{0,32},{32,64},{64,96},{96,128},{128,160},{160,192},{192,224},{224... | collective-permute-start | bytes 147464 | tf_op jit(solution)/shard_map/ppermute | solution.py:118
  69.7 15.5 %collective-permute-start.11 = (f32[12,8,128]{2,1,0:T(8,128)}, f32[12,8,128]{2,1,0:T(8,128)S(1)}, u32[]{:S(2)}, u32[]{:S(2)}) collective-permute-start(f32[12,8,128]{2,1,0:T(8,128)} %get-tuple-element.83), channel_id=1, source_target_pairs={{0,224},{32,0},{64,32},{96,64},{128,96},{160,128},{192,160},{224,1... | collective-permute-start | bytes 147464 | tf_op jit(solution)/shard_map/ppermute | solution.py:118
  69.7 15.5 %collective-permute-start.12 = (f32[12,8,128]{2,1,0:T(8,128)}, f32[12,8,128]{2,1,0:T(8,128)S(1)}, u32[]{:S(2)}, u32[]{:S(2)}) collective-permute-start(f32[12,8,128]{2,1,0:T(8,128)} %get-tuple-element.84), channel_id=1, source_target_pairs={{0,1},{1,2},{2,3},{3,4},{4,5},{5,6},{6,7},{7,8},{8,9},{9,10},{10,1... | collective-permute-start | bytes 147464 | tf_op jit(solution)/shard_map/ppermute | solution.py:118
  69.7 15.5 %collective-permute-start.13 = (f32[12,8,128]{2,1,0:T(8,128)}, f32[12,8,128]{2,1,0:T(8,128)S(1)}, u32[]{:S(2)}, u32[]{:S(2)}) collective-permute-start(f32[12,8,128]{2,1,0:T(8,128)} %get-tuple-element.85), channel_id=1, source_target_pairs={{0,31},{1,0},{2,1},{3,2},{4,3},{5,4},{6,5},{7,6},{8,7},{9,8},{10,9... | collective-permute-start | bytes 147464 | tf_op jit(solution)/shard_map/ppermute | solution.py:118
  89.9 5.7 %collective-permute-start.14 = (f32[1,8,128]{2,1,0:T(8,128)}, f32[1,8,128]{2,1,0:T(8,128)S(1)}, u32[]{:S(2)}, u32[]{:S(2)}) collective-permute-start(f32[1,8,128]{2,1,0:T(8,128)} %get-tuple-element.90), channel_id=1, source_target_pairs={{0,32},{32,64},{64,96},{96,128},{128,160},{160,192},{192,224},{224... | collective-permute-start | bytes 12296 | tf_op jit(solution)/shard_map/ppermute | solution.py:118
  90.8 4.8 %collective-permute-start.15 = (f32[1,8,128]{2,1,0:T(8,128)}, f32[1,8,128]{2,1,0:T(8,128)S(1)}, u32[]{:S(2)}, u32[]{:S(2)}) collective-permute-start(f32[1,8,128]{2,1,0:T(8,128)} %get-tuple-element.91), channel_id=1, source_target_pairs={{0,224},{32,0},{64,32},{96,64},{128,96},{160,128},{192,160},{224,1... | collective-permute-start | bytes 12296 | tf_op jit(solution)/shard_map/ppermute | solution.py:118
  90.8 6.0 %collective-permute-start.16 = (f32[1,8,128]{2,1,0:T(8,128)}, f32[1,8,128]{2,1,0:T(8,128)S(1)}, u32[]{:S(2)}, u32[]{:S(2)}) collective-permute-start(f32[1,8,128]{2,1,0:T(8,128)} %get-tuple-element.92), channel_id=1, source_target_pairs={{0,1},{1,2},{2,3},{3,4},{4,5},{5,6},{6,7},{7,8},{8,9},{9,10},{10,1... | collective-permute-start | bytes 12296 | tf_op jit(solution)/shard_map/ppermute | solution.py:118
  90.8 6.0 %collective-permute-start.17 = (f32[1,8,128]{2,1,0:T(8,128)}, f32[1,8,128]{2,1,0:T(8,128)S(1)}, u32[]{:S(2)}, u32[]{:S(2)}) collective-permute-start(f32[1,8,128]{2,1,0:T(8,128)} %get-tuple-element.93), channel_id=1, source_target_pairs={{0,31},{1,0},{2,1},{3,2},{4,3},{5,4},{6,5},{7,6},{8,7},{9,8},{10,9... | collective-permute-start | bytes 12296 | tf_op jit(solution)/shard_map/ppermute | solution.py:118
  95.6 1.2 copy-start.28
  95.6 1.2 copy-start.29
  113.5 18.6 %all-to-all-start.5 = ((f32[32,2,8,128]{3,2,1,0:T(8,128)}), f32[32,2,8,128]{3,2,1,0:T(8,128)S(1)}, u32[]{:S(2)}, u32[]{:S(2)}) async-start(f32[32,2,8,128]{3,2,1,0:T(8,128)} %shard_map.146), calls=%async_computation.5 | async-start | bytes 524288 | tf_op jit(solution)/shard_map/all_to_all | solution.py:123
  120.9 6.2 %collective-permute-start.18 = (f32[8,128]{1,0:T(8,128)}, f32[8,128]{1,0:T(8,128)S(1)}, u32[]{:S(2)}, u32[]{:S(2)}) collective-permute-start(f32[8,128]{1,0:T(8,128)} %get-tuple-element.97), channel_id=1, source_target_pairs={{0,32},{32,64},{64,96},{96,128},{128,160},{160,192},{192,224},{224... | collective-permute-start | bytes 12296 | tf_op jit(solution)/shard_map/ppermute | solution.py:118
  122.1 4.9 %collective-permute-start.19 = (f32[8,128]{1,0:T(8,128)}, f32[8,128]{1,0:T(8,128)S(1)}, u32[]{:S(2)}, u32[]{:S(2)}) collective-permute-start(f32[8,128]{1,0:T(8,128)} %get-tuple-element.98), channel_id=1, source_target_pairs={{0,224},{32,0},{64,32},{96,64},{128,96},{160,128},{192,160},{224,1... | collective-permute-start | bytes 12296 | tf_op jit(solution)/shard_map/ppermute | solution.py:118
  122.1 6.7 %collective-permute-start.20 = (f32[8,128]{1,0:T(8,128)}, f32[8,128]{1,0:T(8,128)S(1)}, u32[]{:S(2)}, u32[]{:S(2)}) collective-permute-start(f32[8,128]{1,0:T(8,128)} %get-tuple-element.99), channel_id=1, source_target_pairs={{0,1},{1,2},{2,3},{3,4},{4,5},{5,6},{6,7},{7,8},{8,9},{9,10},{10,1... | collective-permute-start | bytes 12296 | tf_op jit(solution)/shard_map/ppermute | solution.py:118
  123.6 5.2 %collective-permute-start.21 = (f32[8,128]{1,0:T(8,128)}, f32[8,128]{1,0:T(8,128)S(1)}, u32[]{:S(2)}, u32[]{:S(2)}) collective-permute-start(f32[8,128]{1,0:T(8,128)} %get-tuple-element.100), channel_id=1, source_target_pairs={{0,31},{1,0},{2,1},{3,2},{4,3},{5,4},{6,5},{7,6},{8,7},{9,8},{10,9... | collective-permute-start | bytes 12296 | tf_op jit(solution)/shard_map/ppermute | solution.py:118
  127.1 5.1 %copy-start.16 = (f32[8,128]{1,0:T(8,128)}, f32[8,128]{1,0:T(8,128)S(1)}, u32[]{:S(2)}) copy-start(f32[8,128]{1,0:T(8,128)S(1)} %collective-permute-done.18.refs_7_) | copy-start | bytes 12292
  127.1 5.1 %copy-start.18 = (f32[8,128]{1,0:T(8,128)}, f32[8,128]{1,0:T(8,128)S(1)}, u32[]{:S(2)}) copy-start(f32[8,128]{1,0:T(8,128)S(1)} %collective-permute-done.19.refs_8_) | copy-start | bytes 12292
  128.9 3.3 %copy-start.20 = (f32[8,128]{1,0:T(8,128)}, f32[8,128]{1,0:T(8,128)S(1)}, u32[]{:S(2)}) copy-start(f32[8,128]{1,0:T(8,128)S(1)} %collective-permute-done.20.refs_9_) | copy-start | bytes 12292
  128.9 3.3 %copy-start.22 = (f32[8,128]{1,0:T(8,128)}, f32[8,128]{1,0:T(8,128)S(1)}, u32[]{:S(2)}) copy-start(f32[8,128]{1,0:T(8,128)S(1)} %collective-permute-done.21.refs_10_) | copy-start | bytes 12292
  132.2 0.7 copy-start
  134.8 11.7 %all-to-all-start.6 = ((f32[8,3,8,128]{3,2,1,0:T(8,128)}), f32[8,3,8,128]{3,2,1,0:T(8,128)S(1)}, u32[]{:S(2)}, u32[]{:S(2)}) async-start(f32[8,3,8,128]{3,2,1,0:T(8,128)} %get-tuple-element.102), calls=%async_computation.6 | async-start | bytes 196608 | tf_op jit(solution)/shard_map/all_to_all | solution.py:123
  140.5 6.0 %collective-permute-start.22 = (f32[8,128]{1,0:T(8,128)}, f32[8,128]{1,0:T(8,128)S(1)}, u32[]{:S(2)}, u32[]{:S(2)}) collective-permute-start(f32[8,128]{1,0:T(8,128)} %get-tuple-element.103), channel_id=1, source_target_pairs={{0,1},{1,2},{2,3},{3,4},{4,5},{5,6},{6,7},{7,8},{8,9},{9,10},{10,1... | collective-permute-start | bytes 12296 | tf_op jit(solution)/shard_map/ppermute | solution.py:118
  140.5 6.0 %collective-permute-start.23 = (f32[8,128]{1,0:T(8,128)}, f32[8,128]{1,0:T(8,128)S(1)}, u32[]{:S(2)}, u32[]{:S(2)}) collective-permute-start(f32[8,128]{1,0:T(8,128)} %get-tuple-element.104), channel_id=1, source_target_pairs={{0,31},{1,0},{2,1},{3,2},{4,3},{5,4},{6,5},{7,6},{8,7},{9,8},{10,9... | collective-permute-start | bytes 12296 | tf_op jit(solution)/shard_map/ppermute | solution.py:118
  146.5 0.6 copy-start.3
  149.6 18.3 %collective-permute-start.24 = (f32[12,8,128]{2,1,0:T(8,128)}, f32[12,8,128]{2,1,0:T(8,128)S(1)}, u32[]{:S(2)}, u32[]{:S(2)}) collective-permute-start(f32[12,8,128]{2,1,0:T(8,128)} %get-tuple-element.107), channel_id=1, source_target_pairs={{0,32},{32,64},{64,96},{96,128},{128,160},{160,192},{192,224},{224... | collective-permute-start | bytes 147464 | tf_op jit(solution)/shard_map/ppermute | solution.py:118
  152.3 15.5 %collective-permute-start.25 = (f32[12,8,128]{2,1,0:T(8,128)}, f32[12,8,128]{2,1,0:T(8,128)S(1)}, u32[]{:S(2)}, u32[]{:S(2)}) collective-permute-start(f32[12,8,128]{2,1,0:T(8,128)} %get-tuple-element.108), channel_id=1, source_target_pairs={{0,224},{32,0},{64,32},{96,64},{128,96},{160,128},{192,160},{224,1... | collective-permute-start | bytes 147464 | tf_op jit(solution)/shard_map/ppermute | solution.py:118
  152.3 15.5 %collective-permute-start.26 = (f32[12,8,128]{2,1,0:T(8,128)}, f32[12,8,128]{2,1,0:T(8,128)S(1)}, u32[]{:S(2)}, u32[]{:S(2)}) collective-permute-start(f32[12,8,128]{2,1,0:T(8,128)} %get-tuple-element.109), channel_id=1, source_target_pairs={{0,1},{1,2},{2,3},{3,4},{4,5},{5,6},{6,7},{7,8},{8,9},{9,10},{10,1... | collective-permute-start | bytes 147464 | tf_op jit(solution)/shard_map/ppermute | solution.py:118
  152.4 15.5 %collective-permute-start.27 = (f32[12,8,128]{2,1,0:T(8,128)}, f32[12,8,128]{2,1,0:T(8,128)S(1)}, u32[]{:S(2)}, u32[]{:S(2)}) collective-permute-start(f32[12,8,128]{2,1,0:T(8,128)} %get-tuple-element.110), channel_id=1, source_target_pairs={{0,31},{1,0},{2,1},{3,2},{4,3},{5,4},{6,5},{7,6},{8,7},{9,8},{10,9... | collective-permute-start | bytes 147464 | tf_op jit(solution)/shard_map/ppermute | solution.py:118
  167.8 0.6 copy-start.12
  167.9 0.6 copy-start.15
  (16 other events, 9.7 us)

commit v2 on v1

v2 whole, which is shorter than its diff:
```python
import jax
import jax.numpy as jnp
from jax import lax
from jax.experimental import pallas as pl
from jax.experimental.pallas import tpu as pltpu
from jax.sharding import PartitionSpec as P

EPSILON = 1e-06
NC = 12
AGG = 8
F32 = jnp.float32
ROWS, LANES = 8, 128
VMEM = pl.BlockSpec(memory_space=pltpu.VMEM)
SMEM = pl.BlockSpec(memory_space=pltpu.SMEM)


def dense(a):
    s = a.shape[:-2]
    n = len(s)
    a = jnp.swapaxes(a.reshape(s + (2, 4, LANES)), n, n + 1)
    return a.reshape(s + (ROWS, LANES))


def undense(a):
    s = a.shape[:-2]
    n = len(s)
    a = jnp.swapaxes(a.reshape(s + (4, 2, LANES)), n, n + 1)
    return a.reshape(s + (2, 4 * LANES))


def grids():
    return (
        lax.broadcasted_iota(jnp.int32, (ROWS, LANES), 0),
        lax.broadcasted_iota(jnp.int32, (ROWS, LANES), 1),
    )


def even_rows():
    return (grids()[0] & 1) == 0


def turn(a, shift, axis):
    return pltpu.roll(a, shift % a.shape[axis], axis)


def pack_low(f):
    return jnp.where(even_rows(), f[0], turn(f[1], 1, 0))


def pack_high(f):
    return jnp.where(even_rows(), turn(f[0], -1, 0), f[1])


def along_y(f):
    row, lane = grids()
    t = turn(f, 1, 1)
    before = jnp.where(lane == 0, jnp.where(row < 2, 0.0, turn(t, 2, 0)), t)
    t = turn(f, -1, 1)
    after = jnp.where(lane == LANES - 1, jnp.where(row >= ROWS - 2, 0.0, turn(t, -2, 0)), t)
    return before, after


def near(f, zlo, zhi, xlo, xhi):
    even = even_rows()
    y0, y1 = along_y(f[0]), along_y(f[1])
    xm = (
        jnp.where(even, xlo, turn(f[0], 1, 0)),
        jnp.where(even, turn(xlo, -1, 0), turn(f[1], 1, 0)),
    )
    xp = (
        jnp.where(even, turn(f[0], -1, 0), turn(xhi, 1, 0)),
        jnp.where(even, turn(f[1], -1, 0), xhi),
    )
    return ((zlo, f[0]), (f[1], zhi), xm, xp, (y0[0], y1[0]), (y0[1], y1[1]))


def position():
    return lax.axis_index("gz"), lax.axis_index("xy")


def edges(sizes, halos):
    g, s = position()
    ok = (g > 0, g < sizes[0] - 1, s > 0, s < sizes[1] - 1)
    return [jnp.where(o, h, 0.0) for o, h in zip(ok, halos)]


def total(a):
    return jnp.sum(jnp.sum(a, axis=0, keepdims=True), axis=1, keepdims=True)


def scalar_stencil(f, halos, pd, po):
    nb = near(f, *halos)
    out = []
    for z in range(2):
        t = pd[z].astype(F32) * f[z]
        for k in range(6):
            t = t + po[k, z].astype(F32) * nb[k][z]
        out.append(t)
    return out


def summed(got, q):
    t = got[0, q]
    for m in range(1, got.shape[0]):
        t = t + got[m, q]
    return t


def beside_z(sizes, got, q, below):
    g, _ = position()
    return got[jnp.maximum(g - 1, 0) if below else jnp.minimum(g + 1, sizes[0] - 1), q]


def packed(levels):
    return pack_high([levels[0]] * 2), pack_low([levels[1]] * 2)


def call(body, outs, ins, args, fast=True, **kw):
    return pl.pallas_call(
        body,
        out_shape=[pltpu.VMEM(o, F32) if fast else jax.ShapeDtypeStruct(o, F32) for o in outs],
        in_specs=ins,
        out_specs=[VMEM] * len(outs),
        **kw,
    )(*args)


def near_by(a):
    return pltpu.with_memory_space_constraint(a, pltpu.VMEM)


def rings(msgs):
    out = []
    for m, (axis, step) in zip(msgs, (("gz", 1), ("gz", -1), ("xy", 1), ("xy", -1))):
        if m is None:
            continue
        n = lax.axis_size(axis)
        out.append(near_by(lax.ppermute(m, axis, [(i, (i + step) % n) for i in range(n)])))
    return out


def spread(buf, axis, shape=None):
    got = lax.all_to_all(buf, axis, 0, 0, tiled=True)
    return near_by(got if shape is None else got.reshape(shape))


def guess_of(v, pw, pd, rhs_ref, fg_ref):
    fg = []
    for z in range(2):
        t = pw[0, z].astype(F32) * v[0][z]
        for i in range(1, NC):
            t = t + pw[i, z].astype(F32) * v[i][z]
        rhs_ref[z] = t
        fg.append(t / pd[z].astype(F32))
        fg_ref[z] = fg[z]
    return fg


def order_inverse(inv, inv_ref):
    col = lax.broadcasted_iota(jnp.int32, (64, LANES), 0)
    lane = lax.broadcasted_iota(jnp.int32, (64, LANES), 1)
    wanted = 2 * (lane >> 5) + (lane & 1)
    mine = (col & 15) == ((lane & 31) >> 1)
    for m in range(ROWS):
        pick = jnp.where(col == 8 * m + wanted, 1.0, 0.0).astype(jnp.bfloat16)
        t = jnp.dot(inv[...], pick, preferred_element_type=F32)
        t = jnp.where(mine, t, 0.0)
        for n in range(4):
            inv_ref[n, m : m + 1, :] = jnp.sum(t[16 * n : 16 * n + 16], axis=0, keepdims=True)


def in_one_row(values):
    return jnp.sum(pltpu.roll(values, 0, 1, stride=16, stride_axis=0), axis=0, keepdims=True)


def in_rows(row):
    at, _ = grids()
    t = jnp.broadcast_to(row, (ROWS, LANES))
    for bit in (1, 2, 4):
        t = jnp.where((at & bit) != 0, turn(t, -16 * bit, 1), t)
    return t


def two_rows(ref, first, second):
    at = lax.broadcasted_iota(jnp.int32, ref.shape, 0)
    ref[...] = jnp.where((at & 1) == 0, first, second)


GUESS, INVERSE, AGGREGATE, SHARE, WEIGHT = 0, 1, 3, 4, 5


def first_kernel(
    cols, r, pw, pd, wi, ag, inv, rhs_ref, fg_ref, up_z, down_z, up_x, down_x, wc_ref, inv_ref
):
    v = [[r[i, z] for z in range(2)] for i in range(NC)]
    fg = guess_of(v, pw, pd, rhs_ref, fg_ref)
    order_inverse(inv, inv_ref)
    row, lane = grids()
    _, s = position()
    here = (2 * s + (row & 1)) * 512 + (row >> 1) * LANES + lane
    count = jnp.zeros((ROWS, LANES), F32)
    for w in range(cols.shape[0]):
        count = count + jnp.where(here == cols[w], 1.0, 0.0)
    wc = [wi[z] * count for z in range(2)]
    for z in range(2):
        wc_ref[z] = wc[z]
    share = [pw[0, z].astype(F32) * wc[z] / pd[z].astype(F32) for z in range(2)]
    agg = [ag[z].astype(F32) for z in range(2)]
    weight = wi[0] + wi[1]
    for ref, pick, pair in (
        (up_z, lambda f: f[1], (2, 3)),
        (down_z, lambda f: f[0], (0, 1)),
        (up_x, pack_high, (1, 3)),
        (down_x, pack_low, (0, 2)),
    ):
        ref[GUESS] = pick(fg)
        for n in range(2):
            ref[INVERSE + n] = inv_ref[pair[n]]
        ref[AGGREGATE] = pick(agg)
        ref[SHARE] = pick(share)
        ref[WEIGHT] = weight


def coarse_body(fg, rhs, halos, pd, po, ag, lv, part_ref):
    applied = scalar_stencil(fg, halos, pd, po)
    _, lane = grids()
    even = (lax.broadcasted_iota(jnp.int32, (ROWS, 1), 0) & 1) == 0
    g, s = position()
    place = 32 * (s & 3) + 4 * g
    tile = jnp.zeros((1, LANES), F32)
    at = lax.broadcasted_iota(jnp.int32, (1, LANES), 1)
    values = jnp.zeros((ROWS, LANES), F32)
    for z in range(2):
        rest = rhs[z] - applied[z]
        level = lv[z]
        guess = fg[z]
        sums = jnp.zeros((ROWS, 1), F32)
        for a in range(AGG):
            mine = ag[z] == a
            c = jnp.sum(jnp.where(mine, rest, 0.0), axis=1, keepdims=True)
            value = c / level[:, a : a + 1]
            guess = guess + jnp.where(mine, value, 0.0)
            sums = sums + (c - level[:, AGG + a : AGG + a + 1] * value)
            values = values + jnp.where(lane == AGG * z + a, value, 0.0)
        part_ref[z] = guess
        for x in range(2):
            t = jnp.sum(jnp.where(even if x == 0 else ~even, sums, 0.0), axis=0, keepdims=True)
            tile = tile + jnp.where(at == place + 2 * z + x, t, 0.0)
    return tile, in_one_row(values)


def first_coarse_kernel(sizes, fg, rhs, wi, zlo, zhi, xlo, xhi, pd, po, ag, lv, part_ref, rows_ref, buf):
    halos = edges(sizes, [h[GUESS] for h in (zlo, zhi, xlo, xhi)])
    tile, values = coarse_body([fg[0], fg[1]], rhs, halos, pd, po, ag, lv, part_ref)
    two_rows(rows_ref, tile, values)
    weight = wi[0] + wi[1]
    for m in range(buf.shape[0]):
        buf[m, 0] = rows_ref[0:ROWS]
        buf[m, 1] = weight
        buf[m, 2] = xlo[WEIGHT]
        buf[m, 3] = xhi[WEIGHT]


def second_coarse_kernel(
    sizes, fg, rhs, r, w, wc, pw, wsums, got, xlo, xhi, szlo, szhi, sxlo, sxhi, dots, pd, po, ag, lv,
    part_ref, rhs_ref, halo_ref, level_ref, rows_ref,
):
    level = summed(got, 1) / wsums[0]
    level_ref[...] = level
    sides = packed([summed(got, 2) / wsums[1], summed(got, 3) / wsums[2]])
    halos = [
        beside_z(sizes, got, 0, True) - szlo[SHARE] * level,
        beside_z(sizes, got, 0, False) - szhi[SHARE] * level,
        xlo[...] - sxlo[SHARE] * sides[0],
        xhi[...] - sxhi[SHARE] * sides[1],
    ]
    halos = edges(sizes, halos)
    for n in range(4):
        halo_ref[n] = halos[n]
    rhs_now, fg_now = [], []
    first = second = jnp.zeros((ROWS, LANES), F32)
    for z in range(2):
        fall = wc[z] * level
        t = rhs[z] - pw[0, z].astype(F32) * fall
        rhs_ref[z] = t
        rhs_now.append(t)
        fg_now.append(t / pd[z].astype(F32))
        first = first + r[0, z] * fall
        second = second + (2.0 * w[0, z] - fall) * fall
    tile, values = coarse_body(fg_now, rhs_now, halos, pd, po, ag, lv, part_ref)
    _, s = position()
    lane = lax.broadcasted_iota(jnp.int32, (1, LANES), 1)
    sums = dots[0:1]
    for m, t in ((1, first), (2, second)):
        sums = sums - jnp.where(lane == m, total(t), 0.0)
    two_rows(rows_ref, tile + pltpu.roll(sums, 32 * ((s + 1) & 3), 1), values)


def relay(rows, own, out_ref):
    at = lax.broadcasted_iota(jnp.int32, rows.shape, 0)
    tile = jnp.sum(jnp.where((at & 1) == 0, rows, 0.0), axis=0, keepdims=True)
    two_rows(out_ref, tile, own)


def first_relay_kernel(got, own, out_ref, sums_ref, rows_ref):
    for m in range(got.shape[0]):
        rows_ref[2 * m : 2 * m + 2] = got[m, 0, 0:2]
    relay(rows_ref[...], own[1:2], out_ref)
    for n in range(3):
        sums_ref[n] = summed(got, 1 + n)


def second_relay_kernel(got, own, out_ref):
    relay(got[...], own[1:2], out_ref)


def pressure_kernel(sizes, later, got, got_z, inv, zlo, zhi, xlo, xhi, halo, part, rhs, pd, po, wi,
                    p_ref, buf, up_x, down_x, tops_ref):
    even = even_rows()
    _, s = position()
    g, _ = position()
    _, lane = grids()
    t = tops = jnp.zeros((ROWS, LANES), F32)
    for k in range(4):
        some = got[pl.ds(2 * k, ROWS, stride=8), :]
        t = t + jnp.where((lane >> 5) == k, some, 0.0)
        tops = tops + turn(some, -32 * ((k + 1) % 4), 1)
    tops_ref[...] = tops
    own = []
    for z in range(2):
        pair = [total(inv[2 * z + x] * t) for x in range(2)]
        own.append(jnp.where(even, pair[0], pair[1]))
    low = in_rows(got[pl.ds(2 * jnp.maximum(s - 1, 0) + 1, 1), :])
    high = in_rows(got[pl.ds(2 * jnp.minimum(s + 1, sizes[1] - 1) + 1, 1), :])
    below = in_rows(got_z[pl.ds(2 * jnp.maximum(g - 1, 0) + 1, 1), :])
    above = in_rows(got_z[pl.ds(2 * jnp.minimum(g + 1, sizes[0] - 1) + 1, 1), :])
    low_even, high_odd = turn(low, -1, 0), turn(high, 1, 0)
    halos = []
    for n, ref in enumerate((zlo, zhi, xlo, xhi)):
        c = [total(ref[INVERSE + m] * t) for m in range(2)]
        h = halo[n] if later else ref[GUESS]
        h = h + jnp.where(even, c[0], c[1])
        agg = ref[AGGREGATE]
        for a in range(AGG):
            one, two = slice(a, a + 1), slice(AGG + a, AGG + a + 1)
            value = (
                below[:, two],
                above[:, one],
                jnp.where(even, low_even[:, one], low[:, two]),
                jnp.where(even, high[:, one], high_odd[:, two]),
            )[n]
            h = h + jnp.where(agg == float(a), value, 0.0)
        halos.append(h)
    halos = edges(sizes, halos)
    f = [part[z] + own[z] for z in range(2)]
    applied = scalar_stencil(f, halos, pd, po)
    p = []
    for z in range(2):
        p.append(f[z] + (rhs[z] - applied[z]) / pd[z].astype(F32))
        p_ref[z] = p[z]
    up_x[...] = pack_high(p)
    down_x[...] = pack_low(p)
    column = wi[0] * p[0] + wi[1] * p[1]
    for m in range(buf.shape[0]):
        buf[m, 0] = jnp.where(g < m, p[1], p[0])
        buf[m, 1] = column


def steps_of(tops):
    rr, rw, ww = (total(tops[:, m : m + 1]) for m in range(3))
    beta = jnp.sqrt(rr + EPSILON)
    h00 = rw / (beta * beta)
    rest = jnp.maximum(ww / (beta * beta) - h00 * h00, 0.0)
    return beta, h00, jnp.sqrt(rest + EPSILON)


def direction_kernel(sizes, later, v, p, got, hxlo, hxhi, jd, jo, bi, wc, wsums, wi, *more):
    if later:
        tops, d0, old, *more = more
        beta, h00, h10 = steps_of(tops)
        scale = 1.0 / (beta * h10)
    d_ref, up_z, down_z, up_x, down_x, column_ref = more
    f = [p[0], p[1]]
    halos = [beside_z(sizes, got, 0, True), beside_z(sizes, got, 0, False), hxlo[...], hxhi[...]]
    nb = near(f, *edges(sizes, halos))
    level = summed(got, 1) / wsums[0]
    rem = []
    for i in range(NC):
        pair = []
        for z in range(2):
            t = jd[i, z].astype(F32) * f[z]
            for k in range(6):
                t = t + jo[k, i, z].astype(F32) * nb[k][z]
            if i == 0:
                t = t + wc[z] * (f[z] - level)
                if later:
                    t = t + wc[z] * old[...]
            pair.append(v[i, z] - t)
        rem.append(pair)
    for i in range(NC):
        pair = []
        for z in range(2):
            ts = [None, None]
            for j in range(NC):
                u = bi[i, j, z].astype(F32) * rem[j][z]
                ts[j % 2] = u if ts[j % 2] is None else ts[j % 2] + u
            t = ts[0] + ts[1]
            if i == 0:
                t = t + f[z]
            if later:
                t = (t - h00 * d0[i, z]) * scale
            d_ref[i, z] = t
            pair.append(t)
        up_z[i] = pair[1]
        down_z[i] = pair[0]
        up_x[i] = pack_high(pair)
        down_x[i] = pack_low(pair)
        if i == 0:
            column = wi[0] * pair[0] + wi[1] * pair[1]
            column_ref[...] = column
            if not later:
                up_x[NC] = column
                down_x[NC] = column


def image_kernel(sizes, later, d, zlo, zhi, xlo, xhi, column, jd, jo, wc, r, *more):
    if later:
        w0, tops, old, w_ref, buf, nb = more
    else:
        pw, pd, w_ref, buf, rhs_ref, fg_ref, up_x, down_x, dots_ref, nb = more
    for j in range(NC):
        f = [d[j, 0], d[j, 1]]
        n = near(f, *edges(sizes, [h[j] for h in (zlo, zhi, xlo, xhi)]))
        for z in range(2):
            nb[0, j, z] = f[z]
            for k in range(6):
                nb[k + 1, j, z] = n[k][z]

    def row(i, carry):
        for z in range(2):
            ts = [None] * 4
            for k in range(7):
                for j in range(NC):
                    c = (jd[i, j, z] if k == 0 else jo[k - 1, i, j, z]).astype(F32)
                    u = c * nb[k, j, z]
                    q = j % 4
                    ts[q] = u if ts[q] is None else ts[q] + u
            w_ref[i, z] = (ts[0] + ts[1]) + (ts[2] + ts[3])
        return carry

    lax.fori_loop(0, NC, row, 0)
    for z in range(2):
        w_ref[0, z] = w_ref[0, z] + wc[z] * d[0, z]
    row_at, lane = grids()
    zero = jnp.zeros((ROWS, LANES), F32)
    sums = [zero, zero, zero]
    falls = [zero] * 4
    if later:
        beta, h00, h10 = steps_of(tops)
        scale = 1.0 / (beta * h10)
    for i in range(NC):
        for z in range(2):
            w = w_ref[i, z]
            if later:
                before = w0[i, z] - wc[z] * old[...] if i == 0 else w0[i, z]
                b0 = r[i, z] * (1.0 / beta)
                b1 = (before - h00 * r[i, z]) * scale
                first, second = w * b0, w * b1
                if i == 0:
                    falls = [t + wc[z] * u for t, u in zip(falls, (b0, b1, w, wc[z]))]
            else:
                first, second = r[i, z] * r[i, z], w * r[i, z]
            sums = [sums[0] + first, sums[1] + second, sums[2] + w * w]
    t = zero
    for m in range(3):
        t = t + jnp.where((row_at == 0) & (lane == m), total(sums[m]), 0.0)
    if later:
        for m in range(buf.shape[0]):
            buf[m, 0] = t
            buf[m, 1] = column[...]
            for n in range(4):
                buf[m, 2 + n] = falls[n]
    else:
        dots_ref[...] = t
        v = [[w_ref[i, z] for z in range(2)] for i in range(NC)]
        fg = guess_of(v, pw, pd, rhs_ref, fg_ref)
        up_x[...] = pack_high(fg)
        down_x[...] = pack_low(fg)
        below, above = edges(sizes, [zero, zero, xlo[NC], xhi[NC]])[2:]
        g, _ = position()
        for m in range(buf.shape[0]):
            buf[m, 0] = jnp.where(g < m, fg[1], fg[0])
            buf[m, 1] = column[...]
            buf[m, 2] = below
            buf[m, 3] = above


def close_kernel(got, wsums, buf, level_ref):
    row, lane = grids()
    level = summed(got, 1) / wsums[0]
    level_ref[...] = level
    falls = [summed(got, 2 + n) for n in range(4)]
    t = summed(got, 0)
    for m, fall in enumerate((falls[0], falls[1], 2.0 * falls[2] - falls[3] * level)):
        t = t - jnp.where((row == 0) & (lane == m), total(fall * level), 0.0)
    buf[...] = jnp.broadcast_to(t[0:1], buf.shape)


def last_kernel(got, tops, r, d0, w0, d1, w1, wc, level0, level1, sol_ref, res_ref, hess_ref):
    t = jnp.sum(got[...], axis=0, keepdims=True)
    h01, h11, norm = (t[:, m : m + 1] for m in range(3))
    beta, h00, h10 = steps_of(tops)
    h21 = jnp.sqrt(jnp.maximum(norm - h01 * h01 - h11 * h11, 0.0) + EPSILON)
    radius = jnp.sqrt(h00 * h00 + h10 * h10)
    c0, s0 = h00 / radius, h10 / radius
    u00, u01, u11 = radius, c0 * h01 + s0 * h11, c0 * h11 - s0 * h01
    t0, t1 = c0 * beta, -s0 * beta
    radius = jnp.sqrt(u11 * u11 + h21 * h21)
    t1 = (u11 / radius) * t1
    y1 = t1 / radius
    y0 = (t0 - u01 * y1) / u00
    y0 = y0 / beta
    for i in range(NC):
        for z in range(2):
            sol_ref[i, z] = y0 * d0[i, z] + y1 * d1[i, z]
            t = y0 * w0[i, z] + y1 * w1[i, z]
            if i == 0:
                t = t - wc[z] * (y0 * level0[...] + y1 * level1[...])
            res_ref[i, z] = r[i, z] - t
    col = lax.broadcasted_iota(jnp.int32, (2, 3), 0)
    at = lax.broadcasted_iota(jnp.int32, (2, 3), 1)
    h = jnp.zeros((2, 3), F32)
    for i, j, value in ((0, 0, h00), (1, 0, h10), (0, 1, h01), (1, 1, h11), (2, 1, h21)):
        h = h + jnp.where((at == i) & (col == j), value, 0.0)
    hess_ref[...] = h


def on_device(
    right_side, jac_diag, jac_off, block_inv, press_weight, press_diag, press_off, well_index,
    well_columns, agg_map, level1_op, coarsest_inv,
):
    sizes = (lax.axis_size("gz"), lax.axis_size("xy"))
    r, jd, jo, bi = dense(right_side), dense(jac_diag), dense(jac_off), dense(block_inv)
    pw, pd, po = dense(press_weight), dense(press_diag), dense(press_off)
    wi, ag = dense(well_index), dense(agg_map)
    op = level1_op.astype(F32)
    lv = jnp.concatenate([jnp.stack([op[a, a] for a in range(AGG)]), jnp.sum(op, axis=0)])
    lv = lv.transpose(1, 3, 2, 0).reshape(2, ROWS, 2 * AGG)
    jd0, jo0 = jd[:, 0], jo[:, :, 0]
    vec, field, plane = (NC, 2, ROWS, LANES), (2, ROWS, LANES), (ROWS, LANES)
    gz, xy = sizes

    def bind(body, *static):
        def kernel(*refs):
            return body(*static, *refs)

        return kernel

    given = (r, jd, jo, bi, pw, pd, po, wi, ag, lv, jd0, jo0)

    def run(body, outs, *args, **kw):
        args = [a if any(a is b for b in given) else near_by(a) for a in args]
        return call(body, outs, [VMEM] * len(args), args, **kw)

    def many(size, parts):
        return (size, parts, ROWS, LANES)

    rhs, fg, *msgs, wc, inv = call(
        first_kernel, [field, field] + [(6, ROWS, LANES)] * 4 + [field, (4, ROWS, LANES)],
        [SMEM] + [VMEM] * 6, (well_columns, r, pw, pd, wi, ag, coarsest_inv.reshape(64, 64)),
    )
    fixed = rings(msgs)
    part, rows, buf = run(
        bind(first_coarse_kernel, sizes), [field, (2 * gz, LANES), many(gz, 4)],
        fg, rhs, wi, *fixed, pd, po, ag, lv,
    )
    shapes = [(7, NC, 2, ROWS, LANES)]
    for step in range(2):
        later = step == 1
        if later:
            got_z = spread(rows.reshape(gz, 2, LANES), "gz", (2 * gz, LANES))
            (buf,) = run(second_relay_kernel, [(2 * xy, LANES)], got_z, rows)
        else:
            buf, wsums, got_z = run(
                first_relay_kernel, [(2 * xy, LANES), (3, ROWS, LANES), (2 * gz, LANES)],
                spread(buf, "gz"), rows,
            )
        got = spread(buf.reshape(xy, 2, LANES), "xy", (2 * xy, LANES))
        p, buf, *msgs, tops = run(
            bind(pressure_kernel, sizes, later), [field, many(gz, 2), plane, plane, plane],
            got, got_z, inv, *fixed, halo if later else inv, part, rhs, pd, po, wi,
        )
        xlo, xhi = rings([None, None, *msgs])
        got = spread(buf, "gz")
        side = (NC, ROWS, LANES)
        wide = side if later else (NC + 1, ROWS, LANES)
        more = (tops, d0, level0) if later else ()
        d, *msgs, column = run(
            bind(direction_kernel, sizes, later), [vec, side, side, wide, wide, plane],
            w0 if later else r, p, got, xlo, xhi, jd0, jo0, bi, wc, wsums, wi, *more,
        )
        sides = rings(msgs)
        scratch = [pltpu.VMEM(s, F32) for s in shapes]
        if later:
            d1 = d
            w1, buf = run(
                bind(image_kernel, sizes, later), [vec, many(gz, 6)],
                d, *sides, column, jd, jo, wc, r, w0, tops, level0, scratch_shapes=scratch,
            )
        else:
            d0 = d
            w0, buf, rhs, fg, *msgs, dots = run(
                bind(image_kernel, sizes, later),
                [vec, many(gz, 4), field, field, plane, plane, plane],
                d, *sides, column, jd, jo, wc, r, pw, pd, scratch_shapes=scratch,
            )
            xlo, xhi = rings([None, None, *msgs])
            got = spread(buf, "gz")
            part, rhs, halo, level0, rows = run(
                bind(second_coarse_kernel, sizes),
                [field, field, (4, ROWS, LANES), plane, (2 * gz, LANES)],
                fg, rhs, r, w0, wc, pw, wsums, got, xlo, xhi, *fixed, dots, pd, po, ag, lv,
            )
    got = spread(buf, "gz")
    buf, level1 = run(close_kernel, [(xy, LANES), plane], got, wsums)
    got = spread(buf.reshape(xy, 1, LANES), "xy", (xy, LANES))
    solution, residual, hessenberg = run(
        last_kernel, [vec, vec, (2, 3)], got, tops, r, d0, w0, d1, w1, wc, level0, level1, fast=False
    )
    return undense(solution), undense(residual), hessenberg.T


def solution(mesh):
    return jax.shard_map(
        on_device,
        mesh=mesh,
        in_specs=(
            P(None, "gz", "xy", None),
            P(None, None, "gz", "xy", None),
            P(None, None, None, "gz", "xy", None),
            P(None, None, "gz", "xy", None),
            P(None, "gz", "xy", None),
            P("gz", "xy", None),
            P(None, "gz", "xy", None),
            P("gz", "xy", None),
            P(),
            P("gz", "xy", None),
            P(None, None, "gz", "xy", None),
            P("gz", "xy", None, None),
        ),
        out_specs=(P(None, "gz", "xy", None), P(None, "gz", "xy", None), P()),
        check_vma=False,
    )
```

time: 203 us -> 168 us (0.83)
  starting transfers between devices: 80.4 us -> 63.5 us
  Pallas kernels: 29.4 us -> 21 us
  local copies, waits for them, and re-layouts: 10.3 us -> 3.96 us
  blocking collectives: 68.1 us -> 62.5 us
  waiting for transfers between devices: 10.8 us -> 14 us
    ppermute x28 -> x18, starting transfers between devices: 53.6 us -> 40.5 us  [rings(): lax.ppermute(m, axis, [(i, (i + step) % n) for i in range(n)])]
    pallas_call x13, Pallas kernels: 29.4 us -> 21 us  [call(): pl.pallas_call(body, out_shape=[pltpu.VMEM(o, F32) if fast else jax.Shape...]
    unnamed x65 -> x0, local copies, waits for them, and re-layouts: 6.38 us -> none
    all_to_all x6 -> x5, blocking collectives: 68.1 us -> 62.5 us  [spread(): got = lax.all_to_all(buf, axis, 0, 0, tiled=True)]
    all_to_all x4, starting transfers between devices: 26.8 us -> 22.9 us  [spread(): got = lax.all_to_all(buf, axis, 0, 0, tiled=True)]
    ppermute x28 -> x18, waiting for transfers between devices: 4.26 us -> 7 us  [rings(): lax.ppermute(m, axis, [(i, (i + step) % n) for i in range(n)])]
  transfers between devices with their start and end apart: 32 -> 22, of which waited for: 5 -> 6; matrix products, arithmetic and copies ran while one was open for 3% -> 3% of each run, Pallas kernels for 0% -> 0%
where the time goes in v2:
time: 168 us; the launch traced here: 167 us
  starting transfers between devices  63.5 us (38%)
  blocking collectives  62.5 us (37%)
  Pallas kernels  21 us (12%)
  waiting for transfers between devices  14 us (8%)
  local copies, waits for them, and re-layouts  3.96 us (2%)
    all_to_all x5, blocking collectives, spread(): got = lax.all_to_all(buf, axis, 0, 0, tiled=True)  62.5 us
    ppermute x18, starting transfers between devices, rings(): lax.ppermute(m, axis, [(i, (i + step) % n) for i in range(n)])  40.5 us
    all_to_all x4, starting transfers between devices, spread(): got = lax.all_to_all(buf, axis, 0, 0, tiled=True)  22.9 us
    pallas_call x13, Pallas kernels, call(): pl.pallas_call(body, out_shape=[pltpu.VMEM(o, F32) if fast else jax.Shape...  21 us
    ppermute x18, waiting for transfers between devices, rings(): lax.ppermute(m, axis, [(i, (i + step) % n) for i in range(n)])  7 us
    all_to_all x4, waiting for transfers between devices, spread(): got = lax.all_to_all(buf, axis, 0, 0, tiled=True)  6.99 us
  transfers between devices with their start and end apart: 22, of which 6 were waited for; matrix products, arithmetic and copies ran while one was open for 3% of the time, Pallas kernels for 0%

profile of v2, /device:TPU:1, one launch (start us, length us, event | category | flops | bytes accessed | tf_op | source)
XLA Modules:
  0.0 167.2 jit_solution(753151836651171979)
XLA Ops:
  0.6 1.2 shard_map.139
  1.8 2.7 %collective-permute-start = (f32[6,8,128]{2,1,0:T(8,128)S(1)}, f32[6,8,128]{2,1,0:T(8,128)S(1)}, u32[]{:S(2)}, u32[]{:S(2)}) collective-permute-start(f32[6,8,128]{2,1,0:T(8,128)S(1)} %get-tuple-element.59), channel_id=1, source_target_pairs={{0,32},{32,64},{64,96},{96,128},{128,160},{160,192},{192,224},{224... | collective-permute-start | bytes 73736 | tf_op jit(solution)/shard_map/ppermute | solution.py:138
  4.5 0.6 collective-permute-start.1
  5.1 0.7 collective-permute-start.2
  5.7 6.6 %collective-permute-start.3 = (f32[6,8,128]{2,1,0:T(8,128)S(1)}, f32[6,8,128]{2,1,0:T(8,128)S(1)}, u32[]{:S(2)}, u32[]{:S(2)}) collective-permute-start(f32[6,8,128]{2,1,0:T(8,128)S(1)} %get-tuple-element.62), channel_id=1, source_target_pairs={{0,31},{1,0},{2,1},{3,2},{4,3},{5,4},{6,5},{7,6},{8,7},{9,8},{10,9... | collective-permute-start | bytes 73736 | tf_op jit(solution)/shard_map/ppermute | solution.py:138
  12.3 0.8 convert_element_type.3
  13.0 0.1 slice_bitcast_fusion.2
  13.1 0.8 convert_reduce_fusion
  13.9 0.1 concatenate.3
  14.1 0.6 copy.67
  14.7 1.2 shard_map.140
  15.9 10.3 %all_to_all.45.got = f32[8,4,8,128]{3,2,1,0:T(8,128)S(1)} all-to-all(f32[8,4,8,128]{3,2,1,0:T(8,128)S(1)} %get-tuple-element.63), channel_id=1, replica_groups=mesh['gz'=8,'xy'=32] {'gz'}, dimensions={0} | all-to-all | bytes 262144 | tf_op jit(solution)/shard_map/all_to_all | solution.py:143
  26.3 0.6 shard_map.141
  26.9 7.9 %all-to-all-start.1 = ((f32[32,2,128]{2,1,0:T(2,128)}), f32[32,2,128]{2,1,0:T(2,128)S(1)}, u32[]{:S(2)}, u32[]{:S(2)}) async-start(f32[32,2,128]{2,1,0:T(2,128)} %bitcast.31), calls=%async_computation.1 | async-start | bytes 65536 | tf_op jit(solution)/shard_map/all_to_all | solution.py:143
  34.8 1.7 %slice_bitcast_fusion.refs_6_ = bf16[6,12,2,8,128]{4,3,2,1,0:T(8,128)(2,1)} fusion(bf16[6,12,12,2,8,128]{5,4,3,2,1,0:T(8,128)(2,1)} %bitcast.97), kind=kLoop, calls=%fused_computation | loop fusion | bytes 589824 | tf_op jit(solution)/shard_map/squeeze | solution.py:549
  36.5 7.0 %all-to-all-done.1 = f32[32,2,128]{2,1,0:T(2,128)S(1)} async-done(((f32[32,2,128]{2,1,0:T(2,128)}), f32[32,2,128]{2,1,0:T(2,128)S(1)}, u32[]{:S(2)}, u32[]{:S(2)}) %all-to-all-start.1) | async-done | bytes 32800 | tf_op jit(solution)/shard_map/all_to_all | solution.py:143
  43.5 1.8 %shard_map.142 = (f32[2,8,128]{2,1,0:T(8,128)S(1)}, f32[8,2,8,128]{3,2,1,0:T(8,128)}, f32[8,128]{1,0:T(8,128)S(1)}, f32[8,128]{1,0:T(8,128)S(1)}, f32[8,128]{1,0:T(8,128)}) custom-call(f32[64,128]{1,0:T(8,128)S(1)} %bitcast.89, f32[16,128]{1,0:T(8,128)S(1)} %get-tuple-element.66.refs_1_, f32[4,8,128]{2,1,0:T(8,128)S(1)} %get-tuple-element.67.refs_2_.refs_7_, ...), custom_call_target="tpu_custom_call" | custom-call | tf_op jit(solution)/shard_map/pallas_call | solution.py:119
  45.3 5.5 %all-to-all-start.2 = ((f32[8,2,8,128]{3,2,1,0:T(8,128)}), f32[8,2,8,128]{3,2,1,0:T(8,128)S(1)}, u32[]{:S(2)}, u32[]{:S(2)}) async-start(f32[8,2,8,128]{3,2,1,0:T(8,128)} %get-tuple-element.70), calls=%async_computation.2 | async-start | bytes 131072 | tf_op jit(solution)/shard_map/all_to_all | solution.py:143
  50.9 0.3 collective-permute-start.4
  51.2 4.5 %collective-permute-start.5 = (f32[8,128]{1,0:T(8,128)S(1)}, f32[8,128]{1,0:T(8,128)S(1)}, u32[]{:S(2)}, u32[]{:S(2)}) collective-permute-start(f32[8,128]{1,0:T(8,128)S(1)} %get-tuple-element.72), channel_id=1, source_target_pairs={{0,31},{1,0},{2,1},{3,2},{4,3},{5,4},{6,5},{7,6},{8,7},{9,8},{10,9... | collective-permute-start | bytes 12296 | tf_op jit(solution)/shard_map/ppermute | solution.py:138
  55.6 1.4 slice_bitcast_fusion.1.refs_5_
  57.1 1.4 shard_map.143
  58.5 0.1 collective-permute-start.8
  58.6 4.8 %collective-permute-start.9 = (f32[13,8,128]{2,1,0:T(8,128)S(1)}, f32[13,8,128]{2,1,0:T(8,128)S(1)}, u32[]{:S(2)}, u32[]{:S(2)}) collective-permute-start(f32[13,8,128]{2,1,0:T(8,128)S(1)} %get-tuple-element.79), channel_id=1, source_target_pairs={{0,31},{1,0},{2,1},{3,2},{4,3},{5,4},{6,5},{7,6},{8,7},{9,8},{10,9... | collective-permute-start | bytes 159752 | tf_op jit(solution)/shard_map/ppermute | solution.py:138
  63.4 3.0 %collective-permute-start.6 = (f32[12,8,128]{2,1,0:T(8,128)S(1)}, f32[12,8,128]{2,1,0:T(8,128)S(1)}, u32[]{:S(2)}, u32[]{:S(2)}) collective-permute-start(f32[12,8,128]{2,1,0:T(8,128)S(1)} %get-tuple-element.76), channel_id=1, source_target_pairs={{0,32},{32,64},{64,96},{96,128},{128,160},{160,192},{192,224},{224... | collective-permute-start | bytes 147464 | tf_op jit(solution)/shard_map/ppermute | solution.py:138
  66.4 1.2 collective-permute-done.6.refs_1_
  67.6 2.3 %collective-permute-done.7.refs_2_ = f32[12,8,128]{2,1,0:T(8,128)S(1)} collective-permute-done((f32[12,8,128]{2,1,0:T(8,128)S(1)}, f32[12,8,128]{2,1,0:T(8,128)S(1)}, u32[]{:S(2)}, u32[]{:S(2)}) %collective-permute-start.7) | collective-permute-done | bytes 49184 | tf_op jit(solution)/shard_map/ppermute | solution.py:138
  69.9 3.9 %shard_map.144 = (f32[12,2,8,128]{3,2,1,0:T(8,128)S(1)}, f32[8,4,8,128]{3,2,1,0:T(8,128)}, f32[2,8,128]{2,1,0:T(8,128)S(1)}, f32[2,8,128]{2,1,0:T(8,128)S(1)}, f...) custom-call(f32[12,2,8,128]{3,2,1,0:T(8,128)S(1)} %get-tuple-element.75.refs_0_.refs_12_.d0, ...), custom_call_target="tpu_custom_call" | custom-call | tf_op jit(solution)/shard_map/pallas_call | solution.py:119
  73.8 4.1 %all-to-all-start.3 = ((f32[8,4,8,128]{3,2,1,0:T(8,128)}), f32[8,4,8,128]{3,2,1,0:T(8,128)S(1)}, u32[]{:S(2)}, u32[]{:S(2)}) async-start(f32[8,4,8,128]{3,2,1,0:T(8,128)} %get-tuple-element.84), calls=%async_computation.3 | async-start | bytes 262144 | tf_op jit(solution)/shard_map/all_to_all | solution.py:143
  77.8 4.8 %collective-permute-start.11 = (f32[8,128]{1,0:T(8,128)S(1)}, f32[8,128]{1,0:T(8,128)S(1)}, u32[]{:S(2)}, u32[]{:S(2)}) collective-permute-start(f32[8,128]{1,0:T(8,128)S(1)} %get-tuple-element.86), channel_id=1, source_target_pairs={{0,31},{1,0},{2,1},{3,2},{4,3},{5,4},{6,5},{7,6},{8,7},{9,8},{10,9... | collective-permute-start | bytes 12296 | tf_op jit(solution)/shard_map/ppermute | solution.py:138
  82.6 1.0 collective-permute-done.10.refs_8_
  83.6 1.6 shard_map.145
  85.2 10.4 %all_to_all.46 = f32[8,2,128]{2,1,0:T(2,128)S(1)} all-to-all(f32[8,2,128]{2,1,0:T(2,128)S(1)} %bitcast.95), channel_id=1, replica_groups=mesh['gz'=8,'xy'=32] {'gz'}, dimensions={0} | all-to-all | bytes 16384 | tf_op jit(solution)/shard_map/all_to_all | solution.py:143
  95.6 15.2 %all_to_all.47 = f32[32,2,128]{2,1,0:T(2,128)S(1)} all-to-all(f32[32,2,128]{2,1,0:T(2,128)S(1)} %bitcast.91), channel_id=1, replica_groups=mesh['gz'=8,'xy'=32] {'xy'}, dimensions={0} | all-to-all | bytes 65536 | tf_op jit(solution)/shard_map/all_to_all | solution.py:143
  110.8 1.8 %shard_map.147 = (f32[2,8,128]{2,1,0:T(8,128)S(1)}, f32[8,2,8,128]{3,2,1,0:T(8,128)}, f32[8,128]{1,0:T(8,128)S(1)}, f32[8,128]{1,0:T(8,128)S(1)}, f32[8,128]{1,0:T(8,128)S(1)}) custom-call(f32[64,128]{1,0:T(8,128)S(1)} %bitcast.90, f32[16,128]{1,0:T(8,128)S(1)} %bitcast.93, f32[4,8,128]{2,1,0:T(8,128)S(1)} %get-tuple-element.67.refs_2_.refs_7_, ...), custom_call_target="tpu_custom_call" | custom-call | tf_op jit(solution)/shard_map/pallas_call | solution.py:119
  112.6 5.4 %all-to-all-start.6 = ((f32[8,2,8,128]{3,2,1,0:T(8,128)}), f32[8,2,8,128]{3,2,1,0:T(8,128)S(1)}, u32[]{:S(2)}, u32[]{:S(2)}) async-start(f32[8,2,8,128]{3,2,1,0:T(8,128)} %get-tuple-element.93), calls=%async_computation.6 | async-start | bytes 131072 | tf_op jit(solution)/shard_map/all_to_all | solution.py:143
  118.0 0.3 collective-permute-start.12
  118.3 4.5 %collective-permute-start.13 = (f32[8,128]{1,0:T(8,128)S(1)}, f32[8,128]{1,0:T(8,128)S(1)}, u32[]{:S(2)}, u32[]{:S(2)}) collective-permute-start(f32[8,128]{1,0:T(8,128)S(1)} %get-tuple-element.95), channel_id=1, source_target_pairs={{0,31},{1,0},{2,1},{3,2},{4,3},{5,4},{6,5},{7,6},{8,7},{9,8},{10,9... | collective-permute-start | bytes 12296 | tf_op jit(solution)/shard_map/ppermute | solution.py:138
  122.8 1.0 collective-permute-done.12.refs_3_
  123.8 1.5 shard_map.148
  125.3 2.8 %collective-permute-start.14 = (f32[12,8,128]{2,1,0:T(8,128)S(1)}, f32[12,8,128]{2,1,0:T(8,128)S(1)}, u32[]{:S(2)}, u32[]{:S(2)}) collective-permute-start(f32[12,8,128]{2,1,0:T(8,128)S(1)} %get-tuple-element.99), channel_id=1, source_target_pairs={{0,32},{32,64},{64,96},{96,128},{128,160},{160,192},{192,224},{224... | collective-permute-start | bytes 147464 | tf_op jit(solution)/shard_map/ppermute | solution.py:138
  128.1 5.1 %collective-permute-start.17 = (f32[12,8,128]{2,1,0:T(8,128)S(1)}, f32[12,8,128]{2,1,0:T(8,128)S(1)}, u32[]{:S(2)}, u32[]{:S(2)}) collective-permute-start(f32[12,8,128]{2,1,0:T(8,128)S(1)} %get-tuple-element.102), channel_id=1, source_target_pairs={{0,31},{1,0},{2,1},{3,2},{4,3},{5,4},{6,5},{7,6},{8,7},{9,8},{10,9... | collective-permute-start | bytes 147464 | tf_op jit(solution)/shard_map/ppermute | solution.py:138
  133.2 1.5 collective-permute-done.16.refs_3_
  134.7 3.7 %shard_map.149 = (f32[12,2,8,128]{3,2,1,0:T(8,128)S(1)}, f32[8,6,8,128]{3,2,1,0:T(8,128)S(1)}) custom-call(f32[12,2,8,128]{3,2,1,0:T(8,128)S(1)} %get-tuple-element.98.refs_0_.d1, f32[12,8,128]{2,1,0:T(8,128)S(1)} %collective-permute-done.14.refs_1_, f32[12,8,128]{2,1,0:T(8,128)S(1)} %collective-permute-done.15.refs_2_, ...), custom_call_target="tpu_custom_call" | custom-call | tf_op jit(solution)/shard_map/pallas_call | solution.py:119
  138.4 11.4 %all_to_all.48.got = f32[8,6,8,128]{3,2,1,0:T(8,128)S(1)} all-to-all(f32[8,6,8,128]{3,2,1,0:T(8,128)S(1)} %get-tuple-element.104), channel_id=1, replica_groups=mesh['gz'=8,'xy'=32] {'gz'}, dimensions={0} | all-to-all | bytes 393216 | tf_op jit(solution)/shard_map/all_to_all | solution.py:143
  149.8 0.1 shard_map.150
  150.0 15.1 %all_to_all.49 = f32[32,1,128]{2,1,0:T(1,128)S(1)} all-to-all(f32[32,1,128]{2,1,0:T(1,128)S(1)} %bitcast.96), channel_id=1, replica_groups=mesh['gz'=8,'xy'=32] {'xy'}, dimensions={0} | all-to-all | bytes 32768 | tf_op jit(solution)/shard_map/all_to_all | solution.py:143
  165.1 2.1 %shard_map.151 = (f32[12,2,8,128]{3,2,1,0:T(8,128)}, f32[12,2,8,128]{3,2,1,0:T(8,128)}, f32[2,3]{1,0:T(2,128)}) custom-call(f32[32,128]{1,0:T(8,128)S(1)} %bitcast.94, f32[8,128]{1,0:T(8,128)S(1)} %get-tuple-element.96.refs_11_.tops, f32[12,2,8,128]{3,2,1,0:T(8,128)} %bitcast.105, f32[12,2,8,128]{3,2,1,0:T(8,128)S(1)} %get-tuple-element.75.refs_0_.refs_12_.d0, ...), custom_call_target="tpu_custom_call" | custom-call | tf_op jit(solution)/shard_map/pallas_call | solution.py:119
  (21 shorter events, 0.1 us)
Async XLA Ops:
  1.8 12.9 %collective-permute-start = (f32[6,8,128]{2,1,0:T(8,128)S(1)}, f32[6,8,128]{2,1,0:T(8,128)S(1)}, u32[]{:S(2)}, u32[]{:S(2)}) collective-permute-start(f32[6,8,128]{2,1,0:T(8,128)S(1)} %get-tuple-element.59), channel_id=1, source_target_pairs={{0,32},{32,64},{64,96},{96,128},{128,160},{160,192},{192,224},{224... | collective-permute-start | bytes 73736 | tf_op jit(solution)/shard_map/ppermute | solution.py:138
  4.5 10.2 %collective-permute-start.1 = (f32[6,8,128]{2,1,0:T(8,128)S(1)}, f32[6,8,128]{2,1,0:T(8,128)S(1)}, u32[]{:S(2)}, u32[]{:S(2)}) collective-permute-start(f32[6,8,128]{2,1,0:T(8,128)S(1)} %get-tuple-element.60), channel_id=1, source_target_pairs={{0,224},{32,0},{64,32},{96,64},{128,96},{160,128},{192,160},{224,1... | collective-permute-start | bytes 73736 | tf_op jit(solution)/shard_map/ppermute | solution.py:138
  5.1 9.6 %collective-permute-start.2 = (f32[6,8,128]{2,1,0:T(8,128)S(1)}, f32[6,8,128]{2,1,0:T(8,128)S(1)}, u32[]{:S(2)}, u32[]{:S(2)}) collective-permute-start(f32[6,8,128]{2,1,0:T(8,128)S(1)} %get-tuple-element.61), channel_id=1, source_target_pairs={{0,1},{1,2},{2,3},{3,4},{4,5},{5,6},{6,7},{7,8},{8,9},{9,10},{10,1... | collective-permute-start | bytes 73736 | tf_op jit(solution)/shard_map/ppermute | solution.py:138
  5.7 9.0 %collective-permute-start.3 = (f32[6,8,128]{2,1,0:T(8,128)S(1)}, f32[6,8,128]{2,1,0:T(8,128)S(1)}, u32[]{:S(2)}, u32[]{:S(2)}) collective-permute-start(f32[6,8,128]{2,1,0:T(8,128)S(1)} %get-tuple-element.62), channel_id=1, source_target_pairs={{0,31},{1,0},{2,1},{3,2},{4,3},{5,4},{6,5},{7,6},{8,7},{9,8},{10,9... | collective-permute-start | bytes 73736 | tf_op jit(solution)/shard_map/ppermute | solution.py:138
  26.9 16.6 %all-to-all-start.1 = ((f32[32,2,128]{2,1,0:T(2,128)}), f32[32,2,128]{2,1,0:T(2,128)S(1)}, u32[]{:S(2)}, u32[]{:S(2)}) async-start(f32[32,2,128]{2,1,0:T(2,128)} %bitcast.31), calls=%async_computation.1 | async-start | bytes 65536 | tf_op jit(solution)/shard_map/all_to_all | solution.py:143
  45.3 11.8 %all-to-all-start.2 = ((f32[8,2,8,128]{3,2,1,0:T(8,128)}), f32[8,2,8,128]{3,2,1,0:T(8,128)S(1)}, u32[]{:S(2)}, u32[]{:S(2)}) async-start(f32[8,2,8,128]{3,2,1,0:T(8,128)} %get-tuple-element.70), calls=%async_computation.2 | async-start | bytes 131072 | tf_op jit(solution)/shard_map/all_to_all | solution.py:143
  50.9 6.2 %collective-permute-start.4 = (f32[8,128]{1,0:T(8,128)S(1)}, f32[8,128]{1,0:T(8,128)S(1)}, u32[]{:S(2)}, u32[]{:S(2)}) collective-permute-start(f32[8,128]{1,0:T(8,128)S(1)} %get-tuple-element.71), channel_id=1, source_target_pairs={{0,1},{1,2},{2,3},{3,4},{4,5},{5,6},{6,7},{7,8},{8,9},{9,10},{10,1... | collective-permute-start | bytes 12296 | tf_op jit(solution)/shard_map/ppermute | solution.py:138
  51.2 5.9 %collective-permute-start.5 = (f32[8,128]{1,0:T(8,128)S(1)}, f32[8,128]{1,0:T(8,128)S(1)}, u32[]{:S(2)}, u32[]{:S(2)}) collective-permute-start(f32[8,128]{1,0:T(8,128)S(1)} %get-tuple-element.72), channel_id=1, source_target_pairs={{0,31},{1,0},{2,1},{3,2},{4,3},{5,4},{6,5},{7,6},{8,7},{9,8},{10,9... | collective-permute-start | bytes 12296 | tf_op jit(solution)/shard_map/ppermute | solution.py:138
  58.5 11.4 %collective-permute-start.8 = (f32[13,8,128]{2,1,0:T(8,128)S(1)}, f32[13,8,128]{2,1,0:T(8,128)S(1)}, u32[]{:S(2)}, u32[]{:S(2)}) collective-permute-start(f32[13,8,128]{2,1,0:T(8,128)S(1)} %get-tuple-element.78), channel_id=1, source_target_pairs={{0,1},{1,2},{2,3},{3,4},{4,5},{5,6},{6,7},{7,8},{8,9},{9,10},{10,1... | collective-permute-start | bytes 159752 | tf_op jit(solution)/shard_map/ppermute | solution.py:138
  58.6 11.3 %collective-permute-start.9 = (f32[13,8,128]{2,1,0:T(8,128)S(1)}, f32[13,8,128]{2,1,0:T(8,128)S(1)}, u32[]{:S(2)}, u32[]{:S(2)}) collective-permute-start(f32[13,8,128]{2,1,0:T(8,128)S(1)} %get-tuple-element.79), channel_id=1, source_target_pairs={{0,31},{1,0},{2,1},{3,2},{4,3},{5,4},{6,5},{7,6},{8,7},{9,8},{10,9... | collective-permute-start | bytes 159752 | tf_op jit(solution)/shard_map/ppermute | solution.py:138
  63.4 4.2 %collective-permute-start.6 = (f32[12,8,128]{2,1,0:T(8,128)S(1)}, f32[12,8,128]{2,1,0:T(8,128)S(1)}, u32[]{:S(2)}, u32[]{:S(2)}) collective-permute-start(f32[12,8,128]{2,1,0:T(8,128)S(1)} %get-tuple-element.76), channel_id=1, source_target_pairs={{0,32},{32,64},{64,96},{96,128},{128,160},{160,192},{192,224},{224... | collective-permute-start | bytes 147464 | tf_op jit(solution)/shard_map/ppermute | solution.py:138
  66.4 3.5 %collective-permute-start.7 = (f32[12,8,128]{2,1,0:T(8,128)S(1)}, f32[12,8,128]{2,1,0:T(8,128)S(1)}, u32[]{:S(2)}, u32[]{:S(2)}) collective-permute-start(f32[12,8,128]{2,1,0:T(8,128)S(1)} %get-tuple-element.77), channel_id=1, source_target_pairs={{0,224},{32,0},{64,32},{96,64},{128,96},{160,128},{192,160},{224,1... | collective-permute-start | bytes 147464 | tf_op jit(solution)/shard_map/ppermute | solution.py:138
  73.8 9.9 %all-to-all-start.3 = ((f32[8,4,8,128]{3,2,1,0:T(8,128)}), f32[8,4,8,128]{3,2,1,0:T(8,128)S(1)}, u32[]{:S(2)}, u32[]{:S(2)}) async-start(f32[8,4,8,128]{3,2,1,0:T(8,128)} %get-tuple-element.84), calls=%async_computation.3 | async-start | bytes 262144 | tf_op jit(solution)/shard_map/all_to_all | solution.py:143
  77.8 5.8 %collective-permute-start.10 = (f32[8,128]{1,0:T(8,128)S(1)}, f32[8,128]{1,0:T(8,128)S(1)}, u32[]{:S(2)}, u32[]{:S(2)}) collective-permute-start(f32[8,128]{1,0:T(8,128)S(1)} %get-tuple-element.85), channel_id=1, source_target_pairs={{0,1},{1,2},{2,3},{3,4},{4,5},{5,6},{6,7},{7,8},{8,9},{9,10},{10,1... | collective-permute-start | bytes 12296 | tf_op jit(solution)/shard_map/ppermute | solution.py:138
  77.8 5.8 %collective-permute-start.11 = (f32[8,128]{1,0:T(8,128)S(1)}, f32[8,128]{1,0:T(8,128)S(1)}, u32[]{:S(2)}, u32[]{:S(2)}) collective-permute-start(f32[8,128]{1,0:T(8,128)S(1)} %get-tuple-element.86), channel_id=1, source_target_pairs={{0,31},{1,0},{2,1},{3,2},{4,3},{5,4},{6,5},{7,6},{8,7},{9,8},{10,9... | collective-permute-start | bytes 12296 | tf_op jit(solution)/shard_map/ppermute | solution.py:138
  112.6 11.2 %all-to-all-start.6 = ((f32[8,2,8,128]{3,2,1,0:T(8,128)}), f32[8,2,8,128]{3,2,1,0:T(8,128)S(1)}, u32[]{:S(2)}, u32[]{:S(2)}) async-start(f32[8,2,8,128]{3,2,1,0:T(8,128)} %get-tuple-element.93), calls=%async_computation.6 | async-start | bytes 131072 | tf_op jit(solution)/shard_map/all_to_all | solution.py:143
  118.0 5.8 %collective-permute-start.12 = (f32[8,128]{1,0:T(8,128)S(1)}, f32[8,128]{1,0:T(8,128)S(1)}, u32[]{:S(2)}, u32[]{:S(2)}) collective-permute-start(f32[8,128]{1,0:T(8,128)S(1)} %get-tuple-element.94), channel_id=1, source_target_pairs={{0,1},{1,2},{2,3},{3,4},{4,5},{5,6},{6,7},{7,8},{8,9},{9,10},{10,1... | collective-permute-start | bytes 12296 | tf_op jit(solution)/shard_map/ppermute | solution.py:138
  118.3 5.5 %collective-permute-start.13 = (f32[8,128]{1,0:T(8,128)S(1)}, f32[8,128]{1,0:T(8,128)S(1)}, u32[]{:S(2)}, u32[]{:S(2)}) collective-permute-start(f32[8,128]{1,0:T(8,128)S(1)} %get-tuple-element.95), channel_id=1, source_target_pairs={{0,31},{1,0},{2,1},{3,2},{4,3},{5,4},{6,5},{7,6},{8,7},{9,8},{10,9... | collective-permute-start | bytes 12296 | tf_op jit(solution)/shard_map/ppermute | solution.py:138
  125.3 7.9 %collective-permute-start.14 = (f32[12,8,128]{2,1,0:T(8,128)S(1)}, f32[12,8,128]{2,1,0:T(8,128)S(1)}, u32[]{:S(2)}, u32[]{:S(2)}) collective-permute-start(f32[12,8,128]{2,1,0:T(8,128)S(1)} %get-tuple-element.99), channel_id=1, source_target_pairs={{0,32},{32,64},{64,96},{96,128},{128,160},{160,192},{192,224},{224... | collective-permute-start | bytes 147464 | tf_op jit(solution)/shard_map/ppermute | solution.py:138
  128.1 5.1 %collective-permute-start.15 = (f32[12,8,128]{2,1,0:T(8,128)S(1)}, f32[12,8,128]{2,1,0:T(8,128)S(1)}, u32[]{:S(2)}, u32[]{:S(2)}) collective-permute-start(f32[12,8,128]{2,1,0:T(8,128)S(1)} %get-tuple-element.100), channel_id=1, source_target_pairs={{0,224},{32,0},{64,32},{96,64},{128,96},{160,128},{192,160},{224,1... | collective-permute-start | bytes 147464 | tf_op jit(solution)/shard_map/ppermute | solution.py:138
  128.1 6.5 %collective-permute-start.16 = (f32[12,8,128]{2,1,0:T(8,128)S(1)}, f32[12,8,128]{2,1,0:T(8,128)S(1)}, u32[]{:S(2)}, u32[]{:S(2)}) collective-permute-start(f32[12,8,128]{2,1,0:T(8,128)S(1)} %get-tuple-element.101), channel_id=1, source_target_pairs={{0,1},{1,2},{2,3},{3,4},{4,5},{5,6},{6,7},{7,8},{8,9},{9,10},{10,1... | collective-permute-start | bytes 147464 | tf_op jit(solution)/shard_map/ppermute | solution.py:138
  128.1 6.5 %collective-permute-start.17 = (f32[12,8,128]{2,1,0:T(8,128)S(1)}, f32[12,8,128]{2,1,0:T(8,128)S(1)}, u32[]{:S(2)}, u32[]{:S(2)}) collective-permute-start(f32[12,8,128]{2,1,0:T(8,128)S(1)} %get-tuple-element.102), channel_id=1, source_target_pairs={{0,31},{1,0},{2,1},{3,2},{4,3},{5,4},{6,5},{7,6},{8,7},{9,8},{10,9... | collective-permute-start | bytes 147464 | tf_op jit(solution)/shard_map/ppermute | solution.py:138

commit v3 on v2

--- a/solution.py
+++ b/solution.py
@@ -12,6 +12,7 @@
 ROWS, LANES = 8, 128
 VMEM = pl.BlockSpec(memory_space=pltpu.VMEM)
 SMEM = pl.BlockSpec(memory_space=pltpu.SMEM)
+HBM = pl.BlockSpec(memory_space=pltpu.HBM)
 
 
 def dense(a):
@@ -131,12 +132,38 @@
 
 def rings(msgs):
     out = []
-    for m, (axis, step) in zip(msgs, (("gz", 1), ("gz", -1), ("xy", 1), ("xy", -1))):
+    for m, (axis, step) in zip(msgs, (("gz", 1), ("gz", -1), ("xy", 0), ("xy", 1))):
         if m is None:
             continue
         n = lax.axis_size(axis)
-        out.append(near_by(lax.ppermute(m, axis, [(i, (i + step) % n) for i in range(n)])))
+        if axis == "gz":
+            pairs = [(i, (i + step) % n) for i in range(n)]
+        else:
+            pairs = [(i, (((i + step) ^ 1) - step) % n) for i in range(n)]
+        out.append(near_by(lax.ppermute(m, axis, pairs)))
     return out
+
+
+def is_even():
+    return (position()[1] & 1) == 0
+
+
+def to_sides(first, second, at, up, down):
+    even = is_even()
+    first[at] = jnp.where(even, up, down)
+    second[at] = jnp.where(even, down, up)
+
+
+def from_sides(first, second):
+    even = is_even()
+
+    def low(at=...):
+        return jnp.where(even, second[at], first[at])
+
+    def high(at=...):
+        return jnp.where(even, first[at], second[at])
+
+    return low, high
 
 
 def spread(buf, axis, shape=None):
@@ -189,8 +216,35 @@
 GUESS, INVERSE, AGGREGATE, SHARE, WEIGHT = 0, 1, 3, 4, 5
 
 
+def stash_kernel(jo, jd, *refs):
+    *refs, sems = refs
+    n = len(refs) // 2 - 1
+    sources = [jo.at[:, :, 0], jd.at[:, 0], *refs[:n]]
+    copies = [pltpu.make_async_copy(a, b, sems.at[m]) for m, (a, b) in enumerate(zip(sources, refs[n:]))]
+    for c in copies:
+        c.start()
+    for c in copies:
+        c.wait()
+
+
+def stash(jo, jd, *arrays):
+    kept = [
+        jax.ShapeDtypeStruct(jo.shape[:2] + jo.shape[3:], jo.dtype),
+        jax.ShapeDtypeStruct(jd.shape[:1] + jd.shape[2:], jd.dtype),
+        *arrays,
+    ]
+    return pl.pallas_call(
+        stash_kernel,
+        out_shape=[pltpu.VMEM(a.shape, a.dtype) for a in kept],
+        in_specs=[HBM] * len(kept),
+        out_specs=[VMEM] * len(kept),
+        scratch_shapes=[pltpu.SemaphoreType.DMA((len(kept),))],
+    )(jo, jd, *arrays)
+
+
 def first_kernel(
-    cols, r, pw, pd, wi, ag, inv, rhs_ref, fg_ref, up_z, down_z, up_x, down_x, wc_ref, inv_ref
+    cols, r, pw, pd, po, wi, ag, inv, rhs_ref, fg_ref, up_z, down_z, up_x, down_x, wc_ref, inv_ref,
+    pd_ref, po_ref, wi_ref, ag_ref,
 ):
     v = [[r[i, z] for z in range(2)] for i in range(NC)]
     fg = guess_of(v, pw, pd, rhs_ref, fg_ref)
@@ -206,19 +260,22 @@
         wc_ref[z] = wc[z]
     share = [pw[0, z].astype(F32) * wc[z] / pd[z].astype(F32) for z in range(2)]
     agg = [ag[z].astype(F32) for z in range(2)]
+    for z in range(2):
+        pd_ref[z] = pd[z].astype(F32)
+        wi_ref[z] = wi[z]
+        ag_ref[z] = agg[z]
+        for k in range(6):
+            po_ref[k, z] = po[k, z].astype(F32)
     weight = wi[0] + wi[1]
-    for ref, pick, pair in (
-        (up_z, lambda f: f[1], (2, 3)),
-        (down_z, lambda f: f[0], (0, 1)),
-        (up_x, pack_high, (1, 3)),
-        (down_x, pack_low, (0, 2)),
-    ):
-        ref[GUESS] = pick(fg)
-        for n in range(2):
-            ref[INVERSE + n] = inv_ref[pair[n]]
-        ref[AGGREGATE] = pick(agg)
-        ref[SHARE] = pick(share)
-        ref[WEIGHT] = weight
+    def planes(pick, pair):
+        return [pick(fg), inv_ref[pair[0]], inv_ref[pair[1]], pick(agg), pick(share), weight]
+
+    for m, t in enumerate(planes(lambda f: f[1], (2, 3))):
+        up_z[m] = t
+    for m, t in enumerate(planes(lambda f: f[0], (0, 1))):
+        down_z[m] = t
+    for m, (up, down) in enumerate(zip(planes(pack_high, (1, 3)), planes(pack_low, (0, 2)))):
+        to_sides(up_x, down_x, m, up, down)
 
 
 def coarse_body(fg, rhs, halos, pd, po, ag, lv, part_ref):
@@ -250,29 +307,32 @@
 
 
 def first_coarse_kernel(sizes, fg, rhs, wi, zlo, zhi, xlo, xhi, pd, po, ag, lv, part_ref, rows_ref, buf):
-    halos = edges(sizes, [h[GUESS] for h in (zlo, zhi, xlo, xhi)])
+    xlo, xhi = from_sides(xlo, xhi)
+    halos = edges(sizes, [zlo[GUESS], zhi[GUESS], xlo(GUESS), xhi(GUESS)])
     tile, values = coarse_body([fg[0], fg[1]], rhs, halos, pd, po, ag, lv, part_ref)
     two_rows(rows_ref, tile, values)
     weight = wi[0] + wi[1]
     for m in range(buf.shape[0]):
         buf[m, 0] = rows_ref[0:ROWS]
         buf[m, 1] = weight
-        buf[m, 2] = xlo[WEIGHT]
-        buf[m, 3] = xhi[WEIGHT]
+        buf[m, 2] = xlo(WEIGHT)
+        buf[m, 3] = xhi(WEIGHT)
 
 
 def second_coarse_kernel(
     sizes, fg, rhs, r, w, wc, pw, wsums, got, xlo, xhi, szlo, szhi, sxlo, sxhi, dots, pd, po, ag, lv,
     part_ref, rhs_ref, halo_ref, level_ref, rows_ref,
 ):
+    xlo, xhi = from_sides(xlo, xhi)
+    sxlo, sxhi = from_sides(sxlo, sxhi)
     level = summed(got, 1) / wsums[0]
     level_ref[...] = level
     sides = packed([summed(got, 2) / wsums[1], summed(got, 3) / wsums[2]])
     halos = [
         beside_z(sizes, got, 0, True) - szlo[SHARE] * level,
         beside_z(sizes, got, 0, False) - szhi[SHARE] * level,
-        xlo[...] - sxlo[SHARE] * sides[0],
-        xhi[...] - sxhi[SHARE] * sides[1],
+        xlo() - sxlo(SHARE) * sides[0],
+        xhi() - sxhi(SHARE) * sides[1],
     ]
     halos = edges(sizes, halos)
     for n in range(4):
@@ -336,11 +396,12 @@
     above = in_rows(got_z[pl.ds(2 * jnp.minimum(g + 1, sizes[0] - 1) + 1, 1), :])
     low_even, high_odd = turn(low, -1, 0), turn(high, 1, 0)
     halos = []
-    for n, ref in enumerate((zlo, zhi, xlo, xhi)):
-        c = [total(ref[INVERSE + m] * t) for m in range(2)]
-        h = halo[n] if later else ref[GUESS]
+    sides = (lambda at: zlo[at], lambda at: zhi[at], *from_sides(xlo, xhi))
+    for n, side in enumerate(sides):
+        c = [total(side(INVERSE + m) * t) for m in range(2)]
+        h = halo[n] if later else side(GUESS)
         h = h + jnp.where(even, c[0], c[1])
-        agg = ref[AGGREGATE]
+        agg = side(AGGREGATE)
         for a in range(AGG):
             one, two = slice(a, a + 1), slice(AGG + a, AGG + a + 1)
             value = (
@@ -358,8 +419,7 @@
     for z in range(2):
         p.append(f[z] + (rhs[z] - applied[z]) / pd[z].astype(F32))
         p_ref[z] = p[z]
-    up_x[...] = pack_high(p)
-    down_x[...] = pack_low(p)
+    to_sides(up_x, down_x, ..., pack_high(p), pack_low(p))
     column = wi[0] * p[0] + wi[1] * p[1]
     for m in range(buf.shape[0]):
         buf[m, 0] = jnp.where(g < m, p[1], p[0])
@@ -381,7 +441,7 @@
         scale = 1.0 / (beta * h10)
     d_ref, up_z, down_z, up_x, down_x, column_ref = more
     f = [p[0], p[1]]
-    halos = [beside_z(sizes, got, 0, True), beside_z(sizes, got, 0, False), hxlo[...], hxhi[...]]
+    halos = [beside_z(sizes, got, 0, True), beside_z(sizes, got, 0, False), *[h() for h in from_sides(hxlo, hxhi)]]
     nb = near(f, *edges(sizes, halos))
     level = summed(got, 1) / wsums[0]
     rem = []
@@ -413,8 +473,7 @@
             pair.append(t)
         up_z[i] = pair[1]
         down_z[i] = pair[0]
-        up_x[i] = pack_high(pair)
-        down_x[i] = pack_low(pair)
+        to_sides(up_x, down_x, i, pack_high(pair), pack_low(pair))
         if i == 0:
             column = wi[0] * pair[0] + wi[1] * pair[1]
             column_ref[...] = column
@@ -423,20 +482,34 @@
                 down_x[NC] = column
 
 
-def image_kernel(sizes, later, d, zlo, zhi, xlo, xhi, column, jd, jo, wc, r, *more):
+def image_kernel(sizes, later, jo_far, jd_far, d, zlo, zhi, xlo, xhi, column, wc, r, *more):
+    *more, nb, jo, jd, sems = more
+    xlo, xhi = from_sides(xlo, xhi)
     if later:
-        w0, tops, old, w_ref, buf, nb = more
+        w0, tops, old, w_ref, buf = more
     else:
-        pw, pd, w_ref, buf, rhs_ref, fg_ref, up_x, down_x, dots_ref, nb = more
+        pw, pd, w_ref, buf, rhs_ref, fg_ref, up_x, down_x, dots_ref = more
+
+    def rows_of(i):
+        return (
+            pltpu.make_async_copy(jo_far.at[:, i], jo.at[:, i], sems.at[0, i]),
+            pltpu.make_async_copy(jd_far.at[i], jd.at[i], sems.at[1, i]),
+        )
+
+    for i in range(NC):
+        for copy in rows_of(i):
+            copy.start()
     for j in range(NC):
         f = [d[j, 0], d[j, 1]]
-        n = near(f, *edges(sizes, [h[j] for h in (zlo, zhi, xlo, xhi)]))
+        n = near(f, *edges(sizes, [zlo[j], zhi[j], xlo(j), xhi(j)]))
         for z in range(2):
             nb[0, j, z] = f[z]
             for k in range(6):
                 nb[k + 1, j, z] = n[k][z]
 
     def row(i, carry):
+        for copy in rows_of(i):
+            copy.wait()
         for z in range(2):
             ts = [None] * 4
             for k in range(7):
@@ -484,9 +557,8 @@
         dots_ref[...] = t
         v = [[w_ref[i, z] for z in range(2)] for i in range(NC)]
         fg = guess_of(v, pw, pd, rhs_ref, fg_ref)
-        up_x[...] = pack_high(fg)
-        down_x[...] = pack_low(fg)
-        below, above = edges(sizes, [zero, zero, xlo[NC], xhi[NC]])[2:]
+        to_sides(up_x, down_x, ..., pack_high(fg), pack_low(fg))
+        below, above = edges(sizes, [zero, zero, xlo(NC), xhi(NC)])[2:]
         g, _ = position()
         for m in range(buf.shape[0]):
             buf[m, 0] = jnp.where(g < m, fg[1], fg[0])
@@ -546,7 +618,6 @@
     op = level1_op.astype(F32)
     lv = jnp.concatenate([jnp.stack([op[a, a] for a in range(AGG)]), jnp.sum(op, axis=0)])
     lv = lv.transpose(1, 3, 2, 0).reshape(2, ROWS, 2 * AGG)
-    jd0, jo0 = jd[:, 0], jo[:, :, 0]
     vec, field, plane = (NC, 2, ROWS, LANES), (2, ROWS, LANES), (ROWS, LANES)
     gz, xy = sizes
 
@@ -556,25 +627,30 @@
 
         return kernel
 
-    given = (r, jd, jo, bi, pw, pd, po, wi, ag, lv, jd0, jo0)
+    far = (jo, jd)
+
 
     def run(body, outs, *args, **kw):
-        args = [a if any(a is b for b in given) else near_by(a) for a in args]
-        return call(body, outs, [VMEM] * len(args), args, **kw)
+        away = [any(a is b for b in far) for a in args]
+        specs = [HBM if b else VMEM for b in away]
+        args = [a if b or a is lv else near_by(a) for a, b in zip(args, away)]
+        return call(body, outs, specs, args, **kw)
 
     def many(size, parts):
         return (size, parts, ROWS, LANES)
 
-    rhs, fg, *msgs, wc, inv = call(
-        first_kernel, [field, field] + [(6, ROWS, LANES)] * 4 + [field, (4, ROWS, LANES)],
-        [SMEM] + [VMEM] * 6, (well_columns, r, pw, pd, wi, ag, coarsest_inv.reshape(64, 64)),
+    rhs, fg, *msgs, wc, inv, pd, po, wi, ag = call(
+        first_kernel,
+        [field, field] + [(6, ROWS, LANES)] * 4
+        + [field, (4, ROWS, LANES), field, (6, 2, ROWS, LANES), field, field],
+        [SMEM] + [VMEM] * 7, (well_columns, r, pw, pd, po, wi, ag, coarsest_inv.reshape(64, 64)),
     )
     fixed = rings(msgs)
+    jo0, jd0, bi, r, pw = stash(jo, jd, bi, r, pw)
     part, rows, buf = run(
         bind(first_coarse_kernel, sizes), [field, (2 * gz, LANES), many(gz, 4)],
         fg, rhs, wi, *fixed, pd, po, ag, lv,
     )
-    shapes = [(7, NC, 2, ROWS, LANES)]
     for step in range(2):
         later = step == 1
         if later:
@@ -600,19 +676,24 @@
             w0 if later else r, p, got, xlo, xhi, jd0, jo0, bi, wc, wsums, wi, *more,
         )
         sides = rings(msgs)
-        scratch = [pltpu.VMEM(s, F32) for s in shapes]
+        scratch = [
+            pltpu.VMEM((7, NC, 2, ROWS, LANES), F32),
+            pltpu.VMEM(jo.shape, jo.dtype),
+            pltpu.VMEM(jd.shape, jd.dtype),
+            pltpu.SemaphoreType.DMA((2, NC)),
+        ]
         if later:
             d1 = d
             w1, buf = run(
                 bind(image_kernel, sizes, later), [vec, many(gz, 6)],
-                d, *sides, column, jd, jo, wc, r, w0, tops, level0, scratch_shapes=scratch,
+                jo, jd, d, *sides, column, wc, r, w0, tops, level0, scratch_shapes=scratch,
             )
         else:
             d0 = d
             w0, buf, rhs, fg, *msgs, dots = run(
                 bind(image_kernel, sizes, later),
                 [vec, many(gz, 4), field, field, plane, plane, plane],
-                d, *sides, column, jd, jo, wc, r, pw, pd, scratch_shapes=scratch,
+                jo, jd, d, *sides, column, wc, r, pw, pd, scratch_shapes=scratch,
             )
             xlo, xhi = rings([None, None, *msgs])
             got = spread(buf, "gz")

time: 168 us -> 152 us (0.905)
  starting transfers between devices: 63.5 us -> 40.3 us
  blocking collectives: 62.5 us -> 71.2 us
  waiting for transfers between devices: 14 us -> 21.6 us
  Pallas kernels: 21 us -> 14.9 us
  local copies, waits for them, and re-layouts: 3.96 us -> 0.82 us
    ppermute x18, starting transfers between devices: 40.5 us -> 23.7 us  [rings(): out.append(near_by(lax.ppermute(m, axis, pairs)))]
    ppermute x18, waiting for transfers between devices: 7 us -> 21.5 us  [rings(): out.append(near_by(lax.ppermute(m, axis, pairs)))]
    all_to_all x5 -> x6, blocking collectives: 62.5 us -> 71.2 us  [spread(): got = lax.all_to_all(buf, axis, 0, 0, tiled=True)]
    pallas_call x13, Pallas kernels: 21 us -> 13.6 us  [call(): pl.pallas_call(body, out_shape=[pltpu.VMEM(o, F32) if fast else jax.Shape...]
    all_to_all x4 -> x3, waiting for transfers between devices: 6.99 us -> 0.01 us  [spread(): got = lax.all_to_all(buf, axis, 0, 0, tiled=True)]
    all_to_all x4 -> x3, starting transfers between devices: 22.9 us -> 16.6 us  [spread(): got = lax.all_to_all(buf, axis, 0, 0, tiled=True)]
    squeeze x2 -> x0, local copies, waits for them, and re-layouts: 3.14 us -> none  [on_device(): jd0, jo0 = (jd[:, 0], jo[:, :, 0])]
  transfers between devices with their start and end apart: 22 -> 21, of which waited for: 6 -> 11; matrix products, arithmetic and copies ran while one was open for 3% -> 2% of each run, Pallas kernels for 0% -> 1%
where the time goes in v3:
time: 152 us; the launch traced here: 151 us
  blocking collectives  71.2 us (47%)
  starting transfers between devices  40.3 us (27%)
  waiting for transfers between devices  21.6 us (14%)
  Pallas kernels  14.9 us (10%)
  other arithmetic  1.56 us (1%)
    all_to_all x6, blocking collectives, spread(): got = lax.all_to_all(buf, axis, 0, 0, tiled=True)  71.2 us
    ppermute x18, starting transfers between devices, rings(): out.append(near_by(lax.ppermute(m, axis, pairs)))  23.7 us
    ppermute x18, waiting for transfers between devices, rings(): out.append(near_by(lax.ppermute(m, axis, pairs)))  21.5 us
    all_to_all x3, starting transfers between devices, spread(): got = lax.all_to_all(buf, axis, 0, 0, tiled=True)  16.6 us
    pallas_call x13, Pallas kernels, call(): pl.pallas_call(body, out_shape=[pltpu.VMEM(o, F32) if fast else jax.Shape...  13.6 us
  transfers between devices with their start and end apart: 21, of which 11 were waited for; matrix products, arithmetic and copies ran while one was open for 2% of the time, Pallas kernels for 1%

profile of v3, /device:TPU:1, one launch (start us, length us, event | category | flops | bytes accessed | tf_op | source)
XLA Modules:
  0.0 151.1 jit_solution(14252227555966038178)
XLA Ops:
  0.6 1.2 shard_map.140
  1.8 2.7 %collective-permute-start = (f32[6,8,128]{2,1,0:T(8,128)S(1)}, f32[6,8,128]{2,1,0:T(8,128)S(1)}, u32[]{:S(2)}, u32[]{:S(2)}) collective-permute-start(f32[6,8,128]{2,1,0:T(8,128)S(1)} %get-tuple-element.70), channel_id=1, source_target_pairs={{0,32},{32,64},{64,96},{96,128},{128,160},{160,192},{192,224},{224... | collective-permute-start | bytes 73736 | tf_op jit(solution)/shard_map/ppermute | solution.py:143
  4.5 0.6 collective-permute-start.1
  5.1 0.7 collective-permute-start.2
  5.7 7.1 %collective-permute-start.3 = (f32[6,8,128]{2,1,0:T(8,128)S(1)}, f32[6,8,128]{2,1,0:T(8,128)S(1)}, u32[]{:S(2)}, u32[]{:S(2)}) collective-permute-start(f32[6,8,128]{2,1,0:T(8,128)S(1)} %get-tuple-element.73), channel_id=1, source_target_pairs={{0,31},{1,2},{2,1},{3,4},{4,3},{5,6},{6,5},{7,8},{8,7},{9,10},{10,... | collective-permute-start | bytes 73736 | tf_op jit(solution)/shard_map/ppermute | solution.py:143
  12.8 0.8 convert_element_type.3
  13.7 0.8 convert_reduce_fusion
  14.5 0.1 concatenate.3
  14.6 0.6 copy.70
  15.2 1.1 shard_map.141
  16.4 10.6 %all_to_all.45.got = f32[8,4,8,128]{3,2,1,0:T(8,128)S(1)} all-to-all(f32[8,4,8,128]{3,2,1,0:T(8,128)S(1)} %get-tuple-element.77), channel_id=1, replica_groups=mesh['gz'=8,'xy'=32] {'gz'}, dimensions={0} | all-to-all | bytes 262144 | tf_op jit(solution)/shard_map/all_to_all | solution.py:170
  27.0 14.7 %all_to_all.46 = f32[32,2,128]{2,1,0:T(2,128)S(1)} all-to-all(f32[32,2,128]{2,1,0:T(2,128)S(1)} %bitcast.91), channel_id=1, replica_groups=mesh['gz'=8,'xy'=32] {'xy'}, dimensions={0} | all-to-all | bytes 65536 | tf_op jit(solution)/shard_map/all_to_all | solution.py:170
  41.7 1.1 shard_map.143
  42.8 5.5 %all-to-all-start.2 = ((f32[8,2,8,128]{3,2,1,0:T(8,128)}), f32[8,2,8,128]{3,2,1,0:T(8,128)S(1)}, u32[]{:S(2)}, u32[]{:S(2)}) async-start(f32[8,2,8,128]{3,2,1,0:T(8,128)} %get-tuple-element.84), calls=%async_computation.2 | async-start | bytes 131072 | tf_op jit(solution)/shard_map/all_to_all | solution.py:170
  48.4 0.3 collective-permute-start.4
  48.7 0.9 collective-permute-start.5
  49.5 1.2 shard_map.139
  50.8 3.6 %collective-permute-done.5.refs_4_ = f32[8,128]{1,0:T(8,128)S(1)} collective-permute-done((f32[8,128]{1,0:T(8,128)S(1)}, f32[8,128]{1,0:T(8,128)S(1)}, u32[]{:S(2)}, u32[]{:S(2)}) %collective-permute-start.5) | collective-permute-done | bytes 4128 | tf_op jit(solution)/shard_map/ppermute | solution.py:143
  54.4 0.2 shard_map.144
  54.8 0.9 collective-permute-start.9
  55.7 3.3 %collective-permute-start.6 = (f32[12,8,128]{2,1,0:T(8,128)S(1)}, f32[12,8,128]{2,1,0:T(8,128)S(1)}, u32[]{:S(2)}, u32[]{:S(2)}) collective-permute-start(f32[12,8,128]{2,1,0:T(8,128)S(1)} %get-tuple-element.93), channel_id=1, source_target_pairs={{0,32},{32,64},{64,96},{96,128},{128,160},{160,192},{192,224},{224... | collective-permute-start | bytes 147464 | tf_op jit(solution)/shard_map/ppermute | solution.py:143
  59.1 1.2 collective-permute-done.6.refs_3_
  60.3 2.6 %collective-permute-done.7.refs_4_ = f32[12,8,128]{2,1,0:T(8,128)S(1)} collective-permute-done((f32[12,8,128]{2,1,0:T(8,128)S(1)}, f32[12,8,128]{2,1,0:T(8,128)S(1)}, u32[]{:S(2)}, u32[]{:S(2)}) %collective-permute-start.7) | collective-permute-done | bytes 49184 | tf_op jit(solution)/shard_map/ppermute | solution.py:143
  62.9 3.1 %shard_map.145 = (f32[12,2,8,128]{3,2,1,0:T(8,128)S(1)}, f32[8,4,8,128]{3,2,1,0:T(8,128)}, f32[2,8,128]{2,1,0:T(8,128)S(1)}, f32[2,8,128]{2,1,0:T(8,128)S(1)}, f...) custom-call(bf16[6,12,12,2,8,128]{5,4,3,2,1,0:T(8,128)(2,1)} %bitcast.95, ...), custom_call_target="tpu_custom_call" | custom-call | tf_op jit(solution)/shard_map/pallas_call | solution.py:120
  66.0 5.7 %all-to-all-start.3 = ((f32[8,4,8,128]{3,2,1,0:T(8,128)}), f32[8,4,8,128]{3,2,1,0:T(8,128)S(1)}, u32[]{:S(2)}, u32[]{:S(2)}) async-start(f32[8,4,8,128]{3,2,1,0:T(8,128)} %get-tuple-element.102), calls=%async_computation.3 | async-start | bytes 262144 | tf_op jit(solution)/shard_map/all_to_all | solution.py:170
  71.7 2.0 %collective-permute-start.11 = (f32[8,128]{1,0:T(8,128)S(1)}, f32[8,128]{1,0:T(8,128)S(1)}, u32[]{:S(2)}, u32[]{:S(2)}) collective-permute-start(f32[8,128]{1,0:T(8,128)S(1)} %get-tuple-element.104), channel_id=1, source_target_pairs={{0,31},{1,2},{2,1},{3,4},{4,3},{5,6},{6,5},{7,8},{8,7},{9,10},{10,... | collective-permute-start | bytes 12296 | tf_op jit(solution)/shard_map/ppermute | solution.py:143
  73.8 0.4 collective-permute-done.10.refs_8_
  74.2 3.3 %collective-permute-done.11.refs_9_ = f32[8,128]{1,0:T(8,128)S(1)} collective-permute-done((f32[8,128]{1,0:T(8,128)S(1)}, f32[8,128]{1,0:T(8,128)S(1)}, u32[]{:S(2)}, u32[]{:S(2)}) %collective-permute-start.11) | collective-permute-done | bytes 4128 | tf_op jit(solution)/shard_map/ppermute | solution.py:143
  77.5 1.3 shard_map.146
  78.8 10.4 %all_to_all.47 = f32[8,2,128]{2,1,0:T(2,128)S(1)} all-to-all(f32[8,2,128]{2,1,0:T(2,128)S(1)} %bitcast.92), channel_id=1, replica_groups=mesh['gz'=8,'xy'=32] {'gz'}, dimensions={0} | all-to-all | bytes 16384 | tf_op jit(solution)/shard_map/all_to_all | solution.py:170
  89.2 12.2 %all_to_all.48 = f32[32,2,128]{2,1,0:T(2,128)S(1)} all-to-all(f32[32,2,128]{2,1,0:T(2,128)S(1)} %bitcast.85), channel_id=1, replica_groups=mesh['gz'=8,'xy'=32] {'xy'}, dimensions={0} | all-to-all | bytes 65536 | tf_op jit(solution)/shard_map/all_to_all | solution.py:170
  101.4 1.1 shard_map.148
  102.5 5.4 %all-to-all-start.6 = ((f32[8,2,8,128]{3,2,1,0:T(8,128)}), f32[8,2,8,128]{3,2,1,0:T(8,128)S(1)}, u32[]{:S(2)}, u32[]{:S(2)}) async-start(f32[8,2,8,128]{3,2,1,0:T(8,128)} %get-tuple-element.111), calls=%async_computation.6 | async-start | bytes 131072 | tf_op jit(solution)/shard_map/all_to_all | solution.py:170
  107.9 0.3 collective-permute-start.12
  108.2 0.9 collective-permute-start.13
  109.0 1.3 collective-permute-done.12.refs_3_
  110.3 3.6 %collective-permute-done.13.refs_4_ = f32[8,128]{1,0:T(8,128)S(1)} collective-permute-done((f32[8,128]{1,0:T(8,128)S(1)}, f32[8,128]{1,0:T(8,128)S(1)}, u32[]{:S(2)}, u32[]{:S(2)}) %collective-permute-start.13) | collective-permute-done | bytes 4128 | tf_op jit(solution)/shard_map/ppermute | solution.py:143
  113.9 0.4 shard_map.149
  114.3 3.1 %collective-permute-start.14 = (f32[12,8,128]{2,1,0:T(8,128)S(1)}, f32[12,8,128]{2,1,0:T(8,128)S(1)}, u32[]{:S(2)}, u32[]{:S(2)}) collective-permute-start(f32[12,8,128]{2,1,0:T(8,128)S(1)} %get-tuple-element.117), channel_id=1, source_target_pairs={{0,32},{32,64},{64,96},{96,128},{128,160},{160,192},{192,224},{224... | collective-permute-start | bytes 147464 | tf_op jit(solution)/shard_map/ppermute | solution.py:143
  117.4 0.9 collective-permute-start.17
  118.3 0.3 collective-permute-done.14.refs_3_
  118.6 2.3 %collective-permute-done.15.refs_4_ = f32[12,8,128]{2,1,0:T(8,128)S(1)} collective-permute-done((f32[12,8,128]{2,1,0:T(8,128)S(1)}, f32[12,8,128]{2,1,0:T(8,128)S(1)}, u32[]{:S(2)}, u32[]{:S(2)}) %collective-permute-start.15) | collective-permute-done | bytes 49184 | tf_op jit(solution)/shard_map/ppermute | solution.py:143
  120.9 2.7 %collective-permute-done.17.refs_6_ = f32[12,8,128]{2,1,0:T(8,128)S(1)} collective-permute-done((f32[12,8,128]{2,1,0:T(8,128)S(1)}, f32[12,8,128]{2,1,0:T(8,128)S(1)}, u32[]{:S(2)}, u32[]{:S(2)}) %collective-permute-start.17) | collective-permute-done | bytes 49184 | tf_op jit(solution)/shard_map/ppermute | solution.py:143
  123.7 2.8 %shard_map.150 = (f32[12,2,8,128]{3,2,1,0:T(8,128)S(1)}, f32[8,6,8,128]{3,2,1,0:T(8,128)S(1)}) custom-call(bf16[6,12,12,2,8,128]{5,4,3,2,1,0:T(8,128)(2,1)} %bitcast.96, bf16[12,12,2,8,128]{4,3,2,1,0:T(8,128)(2,1)} %bitcast.99, f32[12,2,8,128]{3,2,1,0:T(8,128)S(1)} %get-tuple-element.116.refs_2_.d1, f32[12,8,128]{2,1,0:T(8,128)S(1)} %collective-permute-done.14.refs_3_, ...), custom_call_target="tpu_custom_call" | custom-call | tf_op jit(solution)/shard_map/pallas_call | solution.py:120
  126.5 11.7 %all_to_all.49.got = f32[8,6,8,128]{3,2,1,0:T(8,128)S(1)} all-to-all(f32[8,6,8,128]{3,2,1,0:T(8,128)S(1)} %get-tuple-element.122), channel_id=1, replica_groups=mesh['gz'=8,'xy'=32] {'gz'}, dimensions={0} | all-to-all | bytes 393216 | tf_op jit(solution)/shard_map/all_to_all | solution.py:170
  138.2 0.1 shard_map.151
  138.3 11.6 %all_to_all.50 = f32[32,1,128]{2,1,0:T(1,128)S(1)} all-to-all(f32[32,1,128]{2,1,0:T(1,128)S(1)} %bitcast.93), channel_id=1, replica_groups=mesh['gz'=8,'xy'=32] {'xy'}, dimensions={0} | all-to-all | bytes 32768 | tf_op jit(solution)/shard_map/all_to_all | solution.py:170
  149.9 1.2 shard_map.152
  (19 shorter events, 0.3 us)
Async XLA Ops:
  1.8 13.4 %collective-permute-start = (f32[6,8,128]{2,1,0:T(8,128)S(1)}, f32[6,8,128]{2,1,0:T(8,128)S(1)}, u32[]{:S(2)}, u32[]{:S(2)}) collective-permute-start(f32[6,8,128]{2,1,0:T(8,128)S(1)} %get-tuple-element.70), channel_id=1, source_target_pairs={{0,32},{32,64},{64,96},{96,128},{128,160},{160,192},{192,224},{224... | collective-permute-start | bytes 73736 | tf_op jit(solution)/shard_map/ppermute | solution.py:143
  4.5 10.7 %collective-permute-start.1 = (f32[6,8,128]{2,1,0:T(8,128)S(1)}, f32[6,8,128]{2,1,0:T(8,128)S(1)}, u32[]{:S(2)}, u32[]{:S(2)}) collective-permute-start(f32[6,8,128]{2,1,0:T(8,128)S(1)} %get-tuple-element.71), channel_id=1, source_target_pairs={{0,224},{32,0},{64,32},{96,64},{128,96},{160,128},{192,160},{224,1... | collective-permute-start | bytes 73736 | tf_op jit(solution)/shard_map/ppermute | solution.py:143
  5.1 10.2 %collective-permute-start.2 = (f32[6,8,128]{2,1,0:T(8,128)S(1)}, f32[6,8,128]{2,1,0:T(8,128)S(1)}, u32[]{:S(2)}, u32[]{:S(2)}) collective-permute-start(f32[6,8,128]{2,1,0:T(8,128)S(1)} %get-tuple-element.72), channel_id=1, source_target_pairs={{0,1},{1,0},{2,3},{3,2},{4,5},{5,4},{6,7},{7,6},{8,9},{9,8},{10,11... | collective-permute-start | bytes 73736 | tf_op jit(solution)/shard_map/ppermute | solution.py:143
  5.7 9.5 %collective-permute-start.3 = (f32[6,8,128]{2,1,0:T(8,128)S(1)}, f32[6,8,128]{2,1,0:T(8,128)S(1)}, u32[]{:S(2)}, u32[]{:S(2)}) collective-permute-start(f32[6,8,128]{2,1,0:T(8,128)S(1)} %get-tuple-element.73), channel_id=1, source_target_pairs={{0,31},{1,2},{2,1},{3,4},{4,3},{5,6},{6,5},{7,8},{8,7},{9,10},{10,... | collective-permute-start | bytes 73736 | tf_op jit(solution)/shard_map/ppermute | solution.py:143
  42.8 11.6 %all-to-all-start.2 = ((f32[8,2,8,128]{3,2,1,0:T(8,128)}), f32[8,2,8,128]{3,2,1,0:T(8,128)S(1)}, u32[]{:S(2)}, u32[]{:S(2)}) async-start(f32[8,2,8,128]{3,2,1,0:T(8,128)} %get-tuple-element.84), calls=%async_computation.2 | async-start | bytes 131072 | tf_op jit(solution)/shard_map/all_to_all | solution.py:170
  48.4 2.5 %collective-permute-start.4 = (f32[8,128]{1,0:T(8,128)S(1)}, f32[8,128]{1,0:T(8,128)S(1)}, u32[]{:S(2)}, u32[]{:S(2)}) collective-permute-start(f32[8,128]{1,0:T(8,128)S(1)} %get-tuple-element.85), channel_id=1, source_target_pairs={{0,1},{1,0},{2,3},{3,2},{4,5},{5,4},{6,7},{7,6},{8,9},{9,8},{10,11... | collective-permute-start | bytes 12296 | tf_op jit(solution)/shard_map/ppermute | solution.py:143
  48.7 5.8 %collective-permute-start.5 = (f32[8,128]{1,0:T(8,128)S(1)}, f32[8,128]{1,0:T(8,128)S(1)}, u32[]{:S(2)}, u32[]{:S(2)}) collective-permute-start(f32[8,128]{1,0:T(8,128)S(1)} %get-tuple-element.86), channel_id=1, source_target_pairs={{0,31},{1,2},{2,1},{3,4},{4,3},{5,6},{6,5},{7,8},{8,7},{9,10},{10,... | collective-permute-start | bytes 12296 | tf_op jit(solution)/shard_map/ppermute | solution.py:143
  54.7 8.2 %collective-permute-start.8 = (f32[13,8,128]{2,1,0:T(8,128)S(1)}, f32[13,8,128]{2,1,0:T(8,128)S(1)}, u32[]{:S(2)}, u32[]{:S(2)}) collective-permute-start(f32[13,8,128]{2,1,0:T(8,128)S(1)} %get-tuple-element.95), channel_id=1, source_target_pairs={{0,1},{1,0},{2,3},{3,2},{4,5},{5,4},{6,7},{7,6},{8,9},{9,8},{10,11... | collective-permute-start | bytes 159752 | tf_op jit(solution)/shard_map/ppermute | solution.py:143
  54.8 8.1 %collective-permute-start.9 = (f32[13,8,128]{2,1,0:T(8,128)S(1)}, f32[13,8,128]{2,1,0:T(8,128)S(1)}, u32[]{:S(2)}, u32[]{:S(2)}) collective-permute-start(f32[13,8,128]{2,1,0:T(8,128)S(1)} %get-tuple-element.96), channel_id=1, source_target_pairs={{0,31},{1,2},{2,1},{3,4},{4,3},{5,6},{6,5},{7,8},{8,7},{9,10},{10,... | collective-permute-start | bytes 159752 | tf_op jit(solution)/shard_map/ppermute | solution.py:143
  55.7 4.5 %collective-permute-start.6 = (f32[12,8,128]{2,1,0:T(8,128)S(1)}, f32[12,8,128]{2,1,0:T(8,128)S(1)}, u32[]{:S(2)}, u32[]{:S(2)}) collective-permute-start(f32[12,8,128]{2,1,0:T(8,128)S(1)} %get-tuple-element.93), channel_id=1, source_target_pairs={{0,32},{32,64},{64,96},{96,128},{128,160},{160,192},{192,224},{224... | collective-permute-start | bytes 147464 | tf_op jit(solution)/shard_map/ppermute | solution.py:143
  59.1 3.8 %collective-permute-start.7 = (f32[12,8,128]{2,1,0:T(8,128)S(1)}, f32[12,8,128]{2,1,0:T(8,128)S(1)}, u32[]{:S(2)}, u32[]{:S(2)}) collective-permute-start(f32[12,8,128]{2,1,0:T(8,128)S(1)} %get-tuple-element.94), channel_id=1, source_target_pairs={{0,224},{32,0},{64,32},{96,64},{128,96},{160,128},{192,160},{224,1... | collective-permute-start | bytes 147464 | tf_op jit(solution)/shard_map/ppermute | solution.py:143
  66.0 11.5 %all-to-all-start.3 = ((f32[8,4,8,128]{3,2,1,0:T(8,128)}), f32[8,4,8,128]{3,2,1,0:T(8,128)S(1)}, u32[]{:S(2)}, u32[]{:S(2)}) async-start(f32[8,4,8,128]{3,2,1,0:T(8,128)} %get-tuple-element.102), calls=%async_computation.3 | async-start | bytes 262144 | tf_op jit(solution)/shard_map/all_to_all | solution.py:170
  71.7 2.5 %collective-permute-start.10 = (f32[8,128]{1,0:T(8,128)S(1)}, f32[8,128]{1,0:T(8,128)S(1)}, u32[]{:S(2)}, u32[]{:S(2)}) collective-permute-start(f32[8,128]{1,0:T(8,128)S(1)} %get-tuple-element.103), channel_id=1, source_target_pairs={{0,1},{1,0},{2,3},{3,2},{4,5},{5,4},{6,7},{7,6},{8,9},{9,8},{10,11... | collective-permute-start | bytes 12296 | tf_op jit(solution)/shard_map/ppermute | solution.py:143
  71.7 5.8 %collective-permute-start.11 = (f32[8,128]{1,0:T(8,128)S(1)}, f32[8,128]{1,0:T(8,128)S(1)}, u32[]{:S(2)}, u32[]{:S(2)}) collective-permute-start(f32[8,128]{1,0:T(8,128)S(1)} %get-tuple-element.104), channel_id=1, source_target_pairs={{0,31},{1,2},{2,1},{3,4},{4,3},{5,6},{6,5},{7,8},{8,7},{9,10},{10,... | collective-permute-start | bytes 12296 | tf_op jit(solution)/shard_map/ppermute | solution.py:143
  102.5 11.5 %all-to-all-start.6 = ((f32[8,2,8,128]{3,2,1,0:T(8,128)}), f32[8,2,8,128]{3,2,1,0:T(8,128)S(1)}, u32[]{:S(2)}, u32[]{:S(2)}) async-start(f32[8,2,8,128]{3,2,1,0:T(8,128)} %get-tuple-element.111), calls=%async_computation.6 | async-start | bytes 131072 | tf_op jit(solution)/shard_map/all_to_all | solution.py:170
  107.9 2.5 %collective-permute-start.12 = (f32[8,128]{1,0:T(8,128)S(1)}, f32[8,128]{1,0:T(8,128)S(1)}, u32[]{:S(2)}, u32[]{:S(2)}) collective-permute-start(f32[8,128]{1,0:T(8,128)S(1)} %get-tuple-element.112), channel_id=1, source_target_pairs={{0,1},{1,0},{2,3},{3,2},{4,5},{5,4},{6,7},{7,6},{8,9},{9,8},{10,11... | collective-permute-start | bytes 12296 | tf_op jit(solution)/shard_map/ppermute | solution.py:143
  108.2 5.8 %collective-permute-start.13 = (f32[8,128]{1,0:T(8,128)S(1)}, f32[8,128]{1,0:T(8,128)S(1)}, u32[]{:S(2)}, u32[]{:S(2)}) collective-permute-start(f32[8,128]{1,0:T(8,128)S(1)} %get-tuple-element.113), channel_id=1, source_target_pairs={{0,31},{1,2},{2,1},{3,4},{4,3},{5,6},{6,5},{7,8},{8,7},{9,10},{10,... | collective-permute-start | bytes 12296 | tf_op jit(solution)/shard_map/ppermute | solution.py:143
  114.3 4.3 %collective-permute-start.14 = (f32[12,8,128]{2,1,0:T(8,128)S(1)}, f32[12,8,128]{2,1,0:T(8,128)S(1)}, u32[]{:S(2)}, u32[]{:S(2)}) collective-permute-start(f32[12,8,128]{2,1,0:T(8,128)S(1)} %get-tuple-element.117), channel_id=1, source_target_pairs={{0,32},{32,64},{64,96},{96,128},{128,160},{160,192},{192,224},{224... | collective-permute-start | bytes 147464 | tf_op jit(solution)/shard_map/ppermute | solution.py:143
  117.4 3.5 %collective-permute-start.15 = (f32[12,8,128]{2,1,0:T(8,128)S(1)}, f32[12,8,128]{2,1,0:T(8,128)S(1)}, u32[]{:S(2)}, u32[]{:S(2)}) collective-permute-start(f32[12,8,128]{2,1,0:T(8,128)S(1)} %get-tuple-element.118), channel_id=1, source_target_pairs={{0,224},{32,0},{64,32},{96,64},{128,96},{160,128},{192,160},{224,1... | collective-permute-start | bytes 147464 | tf_op jit(solution)/shard_map/ppermute | solution.py:143
  117.4 3.5 %collective-permute-start.16 = (f32[12,8,128]{2,1,0:T(8,128)S(1)}, f32[12,8,128]{2,1,0:T(8,128)S(1)}, u32[]{:S(2)}, u32[]{:S(2)}) collective-permute-start(f32[12,8,128]{2,1,0:T(8,128)S(1)} %get-tuple-element.119), channel_id=1, source_target_pairs={{0,1},{1,0},{2,3},{3,2},{4,5},{5,4},{6,7},{7,6},{8,9},{9,8},{10,11... | collective-permute-start | bytes 147464 | tf_op jit(solution)/shard_map/ppermute | solution.py:143
  117.4 6.3 %collective-permute-start.17 = (f32[12,8,128]{2,1,0:T(8,128)S(1)}, f32[12,8,128]{2,1,0:T(8,128)S(1)}, u32[]{:S(2)}, u32[]{:S(2)}) collective-permute-start(f32[12,8,128]{2,1,0:T(8,128)S(1)} %get-tuple-element.120), channel_id=1, source_target_pairs={{0,31},{1,2},{2,1},{3,4},{4,3},{5,6},{6,5},{7,8},{8,7},{9,10},{10,... | collective-permute-start | bytes 147464 | tf_op jit(solution)/shard_map/ppermute | solution.py:143
